TPU v7x, 32 devices: a whole 2x2x4 slice. The times are simulated.
32 devices in a mesh: cuts: 4 (over y, core), rows: 8 (over z, x).
Axes of the slice: x: 2, y: 2, z: 4, core: 2. Of those that a mesh axis runs over, the one named last changes fastest.
Arguments:
- upstream_loss_derivative: float32 [4, 2, 1, 256, 256], P('cuts', None, None, 'rows'), may hold values from -6 to 6
- estimated_slice_image: float32 [4, 2, 1, 256, 256], P('cuts', None, None, 'rows'), may hold values from -6 to 6
- receiver_profile_maps: float32 [4, 8, 2, 256, 256], P('cuts', None, None, 'rows'), may hold values from -1.5 to 1.5
- measured_fourier_data: float32 [4, 8, 2, 1, 256, 256], P('cuts', None, None, None, 'rows'), may hold values from -6 to 6
- acquisition_choice_odds: float32 [1, 256, 256], P(None, 'rows'), may hold values from -6 to 6
- sigmoid_steepness: float32 [1], replicated, may hold values from 0.5 to 2
Outputs:
- adjoint_field: float32 [4, 2, 1, 256, 256], P('cuts', None, None, 'rows')
- logit_gradient_output: float32 [1, 256, 256], P(None, 'rows')
All inputs are finite; a program needn't handle non-finite values.
Results may differ from a plain program's by a relative error of at most 0.0001.
Values sent between devices are 32-bit elements; how exact they have to be, the bound alone decides.
No kernel may reach another device: no remote copies, remote signals or barrier semaphores. Data moves between devices by JAX's collectives and lax.ppermute only.
A program may use at most 64 MiB of HBM per device.

v0:
```python
import functools
import math

import jax
import jax.numpy as jnp
import ml_dtypes
import numpy as np
from jax import lax
from jax.experimental import pallas as pl
from jax.experimental.pallas import tpu as pltpu
from jax.sharding import PartitionSpec as P


DAMPING = 0.1
F32 = jnp.float32
BF16 = jnp.bfloat16
BOTH = ("cuts", "rows")


def host_split(table):
    high = table.astype(np.float32).astype(ml_dtypes.bfloat16)
    low = (table - high.astype(np.float64)).astype(ml_dtypes.bfloat16)
    return high, low


def dft_tables(extent):
    position = np.arange(extent)
    angle = (np.outer(position, position) % extent) * (2.0 * math.pi / extent)
    cos = np.cos(angle) / math.sqrt(extent)
    sin = np.sin(angle) / math.sqrt(extent)
    out = [*host_split(cos)]
    for imag in (-sin, sin):
        out += [*host_split(imag - cos), *host_split(cos + imag)]
    return out


def split(values):
    high = values.astype(BF16)
    low = (values - high.astype(F32)).astype(BF16)
    return high, low


def dot(first, second):
    return lax.dot_general(
        first, second, (((1,), (0,)), ((), ())), preferred_element_type=F32
    )


def by_right(values, high, low):
    vh, vl = split(values)
    return dot(vh, high) + dot(vl, high) + dot(vh, low)


def by_left(values, high, low):
    vh, vl = split(values)
    return dot(high, vh) + dot(high, vl) + dot(low, vh)


def complex_product(multiply, real, imag, t):
    shared = multiply(real + imag, t[0][...], t[1][...])
    cross_real = multiply(real, t[2][...], t[3][...])
    cross_imag = multiply(imag, t[4][...], t[5][...])
    return shared - cross_imag, shared + cross_real


def pick(tables, inverse):
    return [*tables[:2], *(tables[6:10] if inverse else tables[2:6])]


def to_lanes(values, count):
    rows = values.shape[0] // count
    return jnp.concatenate([values[c * rows : (c + 1) * rows] for c in range(count)], axis=1)


def to_rows(values, count):
    cols = values.shape[1] // count
    return jnp.concatenate([values[:, c * cols : (c + 1) * cols] for c in range(count)], axis=0)


def forward(real, imag, maps, count, tables):
    t = pick(tables, False)
    prod_real = jnp.concatenate(
        [maps[2 * c] * real - maps[2 * c + 1] * imag for c in range(count)], axis=0
    )
    prod_imag = jnp.concatenate(
        [maps[2 * c] * imag + maps[2 * c + 1] * real for c in range(count)], axis=0
    )
    re, im = complex_product(by_right, prod_real, prod_imag, t)
    return complex_product(by_left, to_lanes(re, count), to_lanes(im, count), t)


def adjoint(re, im, maps, count, tables):
    t = pick(tables, True)
    re, im = complex_product(by_left, re, im, t)
    re, im = complex_product(by_right, to_rows(re, count), to_rows(im, count), t)
    rows = re.shape[0] // count
    out_real = out_imag = 0.0
    for c in range(count):
        a, b = re[c * rows : (c + 1) * rows], im[c * rows : (c + 1) * rows]
        sr, si = maps[2 * c], maps[2 * c + 1]
        out_real = out_real + (sr * a + si * b)
        out_imag = out_imag + (sr * b - si * a)
    return out_real, out_imag


def total(values):
    return jnp.sum(jnp.sum(values, axis=0, keepdims=True), axis=1, keepdims=True)


def inner(first, second):
    return total(first[0] * second[0] + first[1] * second[1])


def normal(real, imag, maps, count, tables, wt, spec_ref, part_ref):
    re, im = forward(real, imag, maps, count, tables)
    spec_ref[0], spec_ref[1] = re, im
    wide = jnp.concatenate([wt] * count, axis=1)
    part_ref[0], part_ref[1] = adjoint(re * wide, im * wide, maps, count, tables)


def block_row(turn, flip, extent):
    return pl.multiple_of(lax.bitwise_xor(jnp.int32(turn), flip) * extent, extent)


def at_home(kernel):
    def guarded(*refs):
        @pl.when(refs[0][1] == 1)
        def _():
            kernel(*refs)

    return guarded


def first_kernel(blocks, planes, info, steep_ref, *refs):
    messages, refs = refs[:blocks], refs[blocks:]
    tables, refs = refs[:10], refs[10:]
    maps, image, wt_ref, spec_ref, part_ref, odds, sems = refs
    extent = messages[0].shape[1]
    copies = []
    for k, msg in enumerate(messages):
        rows = pl.ds(block_row(k, info[0], extent), extent)
        copies += [
            pltpu.make_async_copy(msg.at[:planes], maps.at[:, rows], sems.at[0, k]),
            pltpu.make_async_copy(msg.at[pl.ds(planes, 2)], image.at[:, rows], sems.at[1, k]),
            pltpu.make_async_copy(msg.at[planes + 2], odds.at[rows], sems.at[2, k]),
        ]
    for copy in copies:
        copy.start()
    for copy in copies:
        copy.wait()
    wt = jax.nn.sigmoid(steep_ref[0] * odds[...]).T
    wt_ref[...] = wt
    normal(image[0], image[1], maps, planes // 2, tables, wt, spec_ref, part_ref)


def second_kernel(info, image, part, other, maps, wt_ref, *refs):
    tables, refs = refs[:10], refs[10:]
    residual_ref, dir_ref, sc_ref, spec_ref, part_ref = refs
    u = (image[0], image[1])
    q = tuple(part[i] + other[i] + DAMPING * u[i] for i in range(2))
    norm = inner(u, u)
    alpha = norm / inner(u, q)
    r = tuple(u[i] - alpha * q[i] for i in range(2))
    norm_next = inner(r, r)
    p = tuple(r[i] + (norm_next / norm) * u[i] for i in range(2))
    for i in range(2):
        residual_ref[i] = r[i]
        dir_ref[i] = p[i]
    sc_ref[0] = jnp.broadcast_to(alpha, sc_ref.shape[1:])
    sc_ref[1] = jnp.broadcast_to(norm_next, sc_ref.shape[1:])
    normal(p[0], p[1], maps, maps.shape[0] // 2, tables, wt_ref[...], spec_ref, part_ref)


def third_kernel(blocks, planes, info, image, res_ref, dir_ref, sc_in, part, other, maps,
                 wt_ref, spec0_ref, spec1_ref, *refs):
    messages, refs = refs[:blocks], refs[blocks:]
    tables, refs = refs[:10], refs[10:]
    sol_ref, p_ref, sc_ref, out_ref, data, recon, spec0, spec1, sems = refs
    extent = messages[0].shape[1]
    copies = []
    for k, msg in enumerate(messages):
        rows = pl.ds(block_row(k, info[0], extent), extent)
        copies += [
            pltpu.make_async_copy(msg.at[pl.ds(planes, 2)], recon.at[:, rows], sems.at[1, k]),
            pltpu.make_async_copy(msg.at[:planes], data.at[:, rows], sems.at[0, k]),
        ]
    copies += [
        pltpu.make_async_copy(spec0_ref, spec0, sems.at[2, 0]),
        pltpu.make_async_copy(spec1_ref, spec1, sems.at[2, 1]),
    ]
    for copy in copies:
        copy.start()
    count = planes // 2
    n = image.shape[1]
    alpha0, norm = sc_in[0, :1, :1], sc_in[1, :1, :1]
    p = (dir_ref[0], dir_ref[1])
    q = tuple(part[i] + other[i] + DAMPING * p[i] for i in range(2))
    alpha1 = norm / inner(p, q)
    r = tuple(res_ref[i] - alpha1 * q[i] for i in range(2))
    norm_next = inner(r, r)
    for i in range(2):
        sol_ref[i] = alpha0 * image[i] + alpha1 * p[i]
    p = tuple(r[i] + (norm_next / norm) * p[i] for i in range(2))
    p_ref[0], p_ref[1] = p
    re, im = forward(p[0], p[1], maps, count, tables)
    wide = jnp.concatenate([wt_ref[...]] * count, axis=1)
    energy = total(wide * (re * re + im * im))
    sc_ref[0] = jnp.broadcast_to(norm_next, sc_ref.shape[1:])
    sc_ref[1] = jnp.broadcast_to(inner(p, p), sc_ref.shape[1:])
    for copy in copies:
        copy.wait()
    est_re, est_im = forward(recon[0], recon[1], maps, count, tables)
    known = last = 0.0
    for c in range(count):
        s = slice(c * n, (c + 1) * n)
        diff_re = data[2 * c].T - est_re[:, s]
        diff_im = data[2 * c + 1].T - est_im[:, s]
        sol_re = alpha0 * spec0[0, :, s] + alpha1 * spec1[0, :, s]
        sol_im = alpha0 * spec0[1, :, s] + alpha1 * spec1[1, :, s]
        known = known + (sol_re * diff_re + sol_im * diff_im)
        last = last + (re[:, s] * diff_re + im[:, s] * diff_im)
    out_ref[:n] = known
    out_ref[n : 2 * n] = last
    out_ref[2 * n :] = jnp.broadcast_to(energy, (out_ref.shape[0] - 2 * n, n))


def fourth_kernel(info, mine, other, sol, p_ref, sc, *refs):
    outs, terms = refs[:-1], refs[-1]
    half = info[2]
    n = sol.shape[1]
    extent = outs[0].shape[1]
    energy = mine[2 * n :, :][:1, :1] + other[2 * n :, :][:1, :1] + DAMPING * sc[1, :1, :1]
    alpha = sc[0, :1, :1] / energy
    terms[...] = (
        (mine[:n] + other[:n]) + alpha * (mine[n : 2 * n] + other[n : 2 * n])
    ).T
    for k, out in enumerate(outs):
        rows = pl.ds(pl.multiple_of((half * len(outs) + k) * extent, extent), extent)
        out[0] = sol[0, rows] + alpha * p_ref[0, rows]
        out[1] = sol[1, rows] + alpha * p_ref[1, rows]
        out[2] = terms[rows]


def call(*args, **kwargs):
    def run(*operands):
        return pl.pallas_call(*args, compiler_params=PARAMS, **kwargs)(*operands)

    return run


VMEM = pl.BlockSpec(memory_space=pltpu.VMEM)
SMEM = pl.BlockSpec(memory_space=pltpu.SMEM)
ANY = pl.BlockSpec(memory_space=pl.ANY)
PARAMS = pltpu.CompilerParams(vmem_limit_bytes=48 << 20)


def shape(*dims):
    return jax.ShapeDtypeStruct(dims, F32)


def home_row(piece, blocks):
    first = blocks // 4
    return first if piece % 2 == 0 else blocks - 1 - first


def gather_pairs(turn, pieces, blocks):
    pairs = []
    for piece in range(pieces):
        for half in range(2):
            block = turn ^ half ^ (blocks // 2 if piece % 2 else 0)
            target = (piece - piece % 2 + half) * blocks + home_row(piece, blocks)
            pairs.append((piece * blocks + block, target))
    return pairs


def scatter_pairs(turn, pieces, blocks):
    pairs = []
    for piece in range(pieces):
        for half in range(2):
            source = (piece - piece % 2 + half) * blocks + home_row(piece, blocks)
            target = piece * blocks + turn + half * (blocks // 2)
            pairs.append((source, target))
    return pairs


def steps(
    upstream_loss_derivative,
    estimated_slice_image,
    receiver_profile_maps,
    measured_fourier_data,
    acquisition_choice_odds,
    sigmoid_steepness,
):
    blocks = lax.axis_size("rows")
    pieces = lax.axis_size("cuts")
    row = lax.axis_index("rows")
    half = lax.rem(lax.axis_index("cuts"), 2)
    upper = row >= blocks // 2
    home = (row == home_row(0, blocks)) | (row == home_row(1, blocks))
    flip = jnp.bitwise_xor(half, jnp.where(upper, blocks // 2, 0))
    info = jnp.stack([flip, home.astype(jnp.int32), half]).astype(jnp.int32)
    odd = lax.rem(row, 2)
    extent = upstream_loss_derivative.shape[3]
    n = upstream_loss_derivative.shape[4]
    coils = receiver_profile_maps.shape[1]
    planes = coils
    count = coils // 2
    tables = [jnp.asarray(t) for t in dft_tables(n)]
    swap = [(i, i ^ 1) for i in range(pieces)]

    maps = receiver_profile_maps.reshape(2, planes, extent, n)
    data = measured_fourier_data.reshape(2, planes, extent, n)
    upstream = upstream_loss_derivative.reshape(2, extent, n)
    recon = estimated_slice_image.reshape(2, extent, n)
    take = lambda values, i: lax.dynamic_index_in_dim(values, i, 0, keepdims=False)

    def build(values, *more):
        return [
            jnp.concatenate([take(values, i), *more], axis=0) for i in (odd, 1 - odd)
        ]

    def gather(sends, turns):
        return [lax.ppermute(sends[k % 2], BOTH, gather_pairs(k, pieces, blocks)) for k in turns]

    near, far = range(blocks // 2), range(blocks // 2, blocks)
    sends = build(maps, upstream, acquisition_choice_odds)
    first = gather(sends, near) + gather(sends, far)
    sends = build(data, recon)
    sends = lax.optimization_barrier((*sends, *first[: blocks // 2]))[:2]
    second = gather(sends, near)

    image, spectrum = shape(2, n, n), shape(2, n, count * n)
    scalars = shape(2, 8, 128)
    stacked = shape(planes, n, n)
    maps_full, u, wt, spec0, part0 = call(
        at_home(functools.partial(first_kernel, blocks, planes)),
        in_specs=[SMEM, SMEM] + [ANY] * blocks + [VMEM] * 10,
        out_specs=[VMEM] * 5,
        out_shape=[stacked, image, shape(n, n), spectrum, image],
        scratch_shapes=[pltpu.VMEM((n, n), F32), pltpu.SemaphoreType.DMA((3, blocks))],
    )(info, sigmoid_steepness, *first, *tables)
    other0 = lax.ppermute(part0, "cuts", swap)
    sends = lax.optimization_barrier((*sends, part0))[:2]
    second += gather(sends, far)
    res1, dir1, sc1, spec1, part1 = call(
        at_home(second_kernel),
        in_specs=[SMEM] + [VMEM] * 15,
        out_specs=[VMEM] * 5,
        out_shape=[image, image, scalars, spectrum, image],
    )(info, u, part0, other0, maps_full, wt, *tables)
    other1 = lax.ppermute(part1, "cuts", swap)
    sol2, dir2, sc2, mine = call(
        at_home(functools.partial(third_kernel, blocks, planes)),
        in_specs=[SMEM] + [VMEM] * 8 + [ANY] * 2 + [ANY] * blocks + [VMEM] * 10,
        out_specs=[VMEM] * 4,
        out_shape=[image, image, scalars, shape(2 * n + 8, n)],
        scratch_shapes=[
            pltpu.VMEM((planes, n, n), F32),
            pltpu.VMEM((2, n, n), F32),
            pltpu.VMEM((2, n, count * n), F32),
            pltpu.VMEM((2, n, count * n), F32),
            pltpu.SemaphoreType.DMA((3, blocks)),
        ],
    )(info, u, res1, dir1, sc1, part1, other1, maps_full, wt, spec0, spec1, *second, *tables)
    other = lax.ppermute(mine, "cuts", swap)
    turns = blocks // 2
    outs = call(
        at_home(fourth_kernel),
        in_specs=[SMEM] + [VMEM] * 5,
        out_specs=[VMEM] * turns,
        out_shape=[shape(3, extent, n)] * turns,
        scratch_shapes=[pltpu.VMEM((n, n), F32)],
    )(info, mine, other, sol2, dir2, sc2)
    parts = [
        lax.ppermute(outs[k], BOTH, scatter_pairs(k, pieces, blocks)) for k in range(turns)
    ]
    whole = parts[0]
    for part in parts[1:]:
        whole = whole + part
    term = whole[2]
    step = 1
    while step < pieces:
        term = term + lax.ppermute(term, "cuts", [(i, i ^ step) for i in range(pieces)])
        step *= 2
    steep = sigmoid_steepness[0]
    weights = jax.nn.sigmoid(steep * acquisition_choice_odds)
    slices = upstream_loss_derivative.shape[0] * pieces
    gradient = steep * weights * (1.0 - weights) * term[None] / slices
    return whole[:2].reshape(upstream_loss_derivative.shape), gradient


def solution(mesh):
    return jax.shard_map(
        steps,
        mesh=mesh,
        in_specs=(
            P("cuts", None, None, "rows", None),
            P("cuts", None, None, "rows", None),
            P("cuts", None, None, "rows", None),
            P("cuts", None, None, None, "rows", None),
            P(None, "rows", None),
            P(),
        ),
        out_specs=(P("cuts", None, None, "rows", None), P(None, "rows", None)),
        check_vma=False,
    )
```

profile of v0, /device:TPU:10, one launch (start us, length us, event | category | flops | bytes accessed | tf_op | source)
XLA Modules:
  0.0 131.1 jit_solution(11488286393404850095)
XLA Ops:
  0.8 2.3 %dynamic-slice_bitcast_fusion = (f32[8,32,256]{2,1,0:T(8,128)}, f32[8,32,256]{2,1,0:T(8,128)}, f32[8,32,256]{2,1,0:T(8,128)S(1)}, f32[8,32,256]{2,1,0:T(8,128)S(1)}) fusion(f32[2,8,32,256]{3,2,1,0:T(8,128)} %bitcast.29, s32[]{:T(128)S(6)} %select_n.15, s32[]{:T(128)S(6)} %select_n.14, f32[2,8,32,256]{3,2,1,0:T(8,128)} %bitcast.30), kind=kLoop, calls=%fused_computation.6 | loop fusion | bytes 2097160 | tf_op jit(solution)/shard_map/jit(dynamic_index_in_dim)/squeeze | solution.py:315
  3.1 1.0 pad_maximum_fusion
  4.7 0.7 collective-permute-start.5
  5.4 3.7 %collective-permute-start.3 = (f32[11,32,256]{2,1,0:T(8,128)}, f32[11,32,256]{2,1,0:T(8,128)S(1)}, u32[]{:S(2)}, u32[]{:S(2)}) collective-permute-start(f32[11,32,256]{2,1,0:T(8,128)} %get-tuple-element.52), channel_id=1, source_target_pairs={{3,2},{2,10},{15,5},{14,13},{19,18},{18,26},{31,21},{30,29}} | collective-permute-start | bytes 1081352 | tf_op jit(solution)/shard_map/ppermute | solution.py:323
  9.1 0.7 collective-permute-start.1
  9.8 0.7 collective-permute-start.6
  10.5 0.7 collective-permute-start.4
  11.2 12.8 %collective-permute-start.2 = (f32[11,32,256]{2,1,0:T(8,128)}, f32[11,32,256]{2,1,0:T(8,128)}, u32[]{:S(2)}, u32[]{:S(2)}) collective-permute-start(f32[11,32,256]{2,1,0:T(8,128)} %get-tuple-element.53), channel_id=1, source_target_pairs={{2,2},{3,10},{14,5},{15,13},{18,18},{19,26},{30,21},{31,29}} | collective-permute-start | bytes 1081352 | tf_op jit(solution)/shard_map/ppermute | solution.py:323
  24.0 12.7 %collective-permute-done.3.refs_5_ = f32[11,32,256]{2,1,0:T(8,128)S(1)} collective-permute-done((f32[11,32,256]{2,1,0:T(8,128)}, f32[11,32,256]{2,1,0:T(8,128)S(1)}, u32[]{:S(2)}, u32[]{:S(2)}) %collective-permute-start.3) | collective-permute-done | bytes 360480 | tf_op jit(solution)/shard_map/ppermute | solution.py:323
  36.7 1.4 %collective-permute-start = (f32[11,32,256]{2,1,0:T(8,128)}, f32[11,32,256]{2,1,0:T(8,128)}, u32[]{:S(2)}, u32[]{:S(2)}) collective-permute-start(f32[11,32,256]{2,1,0:T(8,128)} %get-tuple-element.53), channel_id=1, source_target_pairs={{0,2},{1,10},{12,5},{13,13},{16,18},{17,26},{28,21},{29,29}} | collective-permute-start | bytes 1081352 | tf_op jit(solution)/shard_map/ppermute | solution.py:323
  38.9 1.7 %collective-permute-done.2.refs_4_ = f32[11,32,256]{2,1,0:T(8,128)} collective-permute-done((f32[11,32,256]{2,1,0:T(8,128)}, f32[11,32,256]{2,1,0:T(8,128)}, u32[]{:S(2)}, u32[]{:S(2)}) %collective-permute-start.2) | collective-permute-done | bytes 360480 | tf_op jit(solution)/shard_map/ppermute | solution.py:323
  40.7 2.8 %shard_map.167 = (f32[8,256,256]{2,1,0:T(8,128)}, f32[2,256,256]{2,1,0:T(8,128)S(1)}, f32[256,256]{1,0:T(8,128)S(1)}, f32[2,256,1024]{2,1,0:T(8,128)}, f32[2,256,256]{2,1,0:T(8,128)S(1)}) custom-call(s32[3]{0:T(128)S(1)} %pad_add_fusion.refs_0_, f32[1]{0:T(128)} %copy.19.refs_1_, f32[11,32,256]{2,1,0:T(8,128)} %collective-permute-done.refs_2_, ...), custom_call_target="tpu_custom_call" | custom-call | tf_op jit(solution)/shard_map/pallas_call | solution.py:246
  43.6 17.7 %collective-permute-start.12 = (f32[10,32,256]{2,1,0:T(8,128)S(1)}, f32[10,32,256]{2,1,0:T(8,128)S(1)}, u32[]{:S(2)}, u32[]{:S(2)}) collective-permute-start(f32[10,32,256]{2,1,0:T(8,128)S(1)} %get-tuple-element.36), channel_id=1, source_target_pairs={{2,2},{3,10},{14,5},{15,13},{18,18},{19,26},{30,21},{31,29}} | collective-permute-start | bytes 983048 | tf_op jit(solution)/shard_map/ppermute | solution.py:323
  61.3 0.7 collective-permute-start.10
  62.0 1.3 collective-permute-start.13
  63.3 0.7 collective-permute-start.11
  64.0 3.2 %shard_map.168 = (f32[2,256,256]{2,1,0:T(8,128)S(1)}, f32[2,256,256]{2,1,0:T(8,128)S(1)}, f32[2,8,128]{2,1,0:T(8,128)S(1)}, f32[2,256,1024]{2,1,0:T(8,128)}, f32[2,256,256]{2,1,0:T(8,128)S(1)}) custom-call(s32[3]{0:T(128)S(1)} %pad_add_fusion.refs_0_, f32[2,256,256]{2,1,0:T(8,128)S(1)} %get-tuple-element.24.refs_1_, ...), custom_call_target="tpu_custom_call" | custom-call | tf_op jit(solution)/shard_map/pallas_call | solution.py:246
  67.2 0.8 copy-done.11
  68.0 0.8 copy-done.12
  68.9 4.1 %collective-permute-done.12.refs_13_ = f32[10,32,256]{2,1,0:T(8,128)S(1)} collective-permute-done((f32[10,32,256]{2,1,0:T(8,128)S(1)}, f32[10,32,256]{2,1,0:T(8,128)S(1)}, u32[]{:S(2)}, u32[]{:S(2)}) %collective-permute-start.12) | collective-permute-done | bytes 327712 | tf_op jit(solution)/shard_map/ppermute | solution.py:323
  74.3 2.1 %collective-permute-done.13.refs_14_ = f32[10,32,256]{2,1,0:T(8,128)S(1)} collective-permute-done((f32[10,32,256]{2,1,0:T(8,128)S(1)}, f32[10,32,256]{2,1,0:T(8,128)S(1)}, u32[]{:S(2)}, u32[]{:S(2)}) %collective-permute-start.13) | collective-permute-done | bytes 327712 | tf_op jit(solution)/shard_map/ppermute | solution.py:323
  77.9 0.8 copy-done.16
  78.7 3.5 %shard_map.169 = (f32[2,256,256]{2,1,0:T(8,128)S(1)}, f32[2,256,256]{2,1,0:T(8,128)S(1)}, f32[2,8,128]{2,1,0:T(8,128)S(1)}, f32[520,256]{1,0:T(8,128)}) custom-call(s32[3]{0:T(128)S(1)} %pad_add_fusion.refs_0_, f32[2,256,256]{2,1,0:T(8,128)S(1)} %get-tuple-element.24.refs_1_, f32[2,256,256]{2,1,0:T(8,128)} %copy-done.11, f32[2,256,256]{2,1,0:T(8,128)} %copy-done.12, ...), custom_call_target="tpu_custom_call" | custom-call | tf_op jit(solution)/shard_map/pallas_call | solution.py:246
  82.2 14.7 %collective-permute-start.18 = (f32[520,256]{1,0:T(8,128)}, f32[520,256]{1,0:T(8,128)S(1)}, u32[]{:S(2)}, u32[]{:S(2)}) collective-permute-start(f32[520,256]{1,0:T(8,128)} %get-tuple-element.38.refs_1_), channel_id=1, source_target_pairs={{0,8},{8,0},{16,24},{24,16},{1,9},{9,1},{17,25},{25,17},{2,10},{10... | collective-permute-start | bytes 1597448 | tf_op jit(solution)/shard_map/ppermute | solution.py:365
  96.9 1.8 %collective-permute-done.18.refs_2_ = f32[520,256]{1,0:T(8,128)S(1)} collective-permute-done((f32[520,256]{1,0:T(8,128)}, f32[520,256]{1,0:T(8,128)S(1)}, u32[]{:S(2)}, u32[]{:S(2)}) %collective-permute-start.18) | collective-permute-done | bytes 532512 | tf_op jit(solution)/shard_map/ppermute | solution.py:365
  98.6 1.0 copy-done.10
  102.2 1.3 collective-permute-start.22
  103.6 19.6 %collective-permute-done.22 = f32[3,32,256]{2,1,0:T(8,128)S(1)} collective-permute-done((f32[3,32,256]{2,1,0:T(8,128)S(1)}, f32[3,32,256]{2,1,0:T(8,128)S(1)}, u32[]{:S(2)}, u32[]{:S(2)}) %collective-permute-start.22) | collective-permute-done | bytes 98336 | tf_op jit(solution)/shard_map/ppermute | solution.py:375
  123.2 2.5 %collective-permute-start.23 = (f32[32,256]{1,0:T(8,128)S(1)}, f32[32,256]{1,0:T(8,128)S(1)}, u32[]{:S(2)}, u32[]{:S(2)}) collective-permute-start(f32[32,256]{1,0:T(8,128)S(1)} %slice_bitcast_fusion.1), channel_id=1, source_target_pairs={{0,8},{8,0},{16,24},{24,16},{1,9},{9,1},{17,25},{25,17},{2,10},{10... | collective-permute-start | bytes 98312 | tf_op jit(solution)/shard_map/ppermute | solution.py:383
  125.7 0.9 collective-permute-done.23
  126.5 1.5 %collective-permute-start.24 = (f32[32,256]{1,0:T(8,128)S(1)}, f32[32,256]{1,0:T(8,128)S(1)}, u32[]{:S(2)}, u32[]{:S(2)}) collective-permute-start(f32[32,256]{1,0:T(8,128)S(1)} %fusion.1), channel_id=1, source_target_pairs={{0,16},{8,24},{16,0},{24,8},{1,17},{9,25},{17,1},{25,9},{2,18},{10... | collective-permute-start | bytes 98312 | tf_op jit(solution)/shard_map/ppermute | solution.py:383
  128.7 1.8 %collective-permute-done.24 = f32[32,256]{1,0:T(8,128)S(1)} collective-permute-done((f32[32,256]{1,0:T(8,128)S(1)}, f32[32,256]{1,0:T(8,128)S(1)}, u32[]{:S(2)}, u32[]{:S(2)}) %collective-permute-start.24) | collective-permute-done | bytes 32800 | tf_op jit(solution)/shard_map/ppermute | solution.py:383
  (71 shorter events, 7.6 us)
Async XLA Ops:
  0.6 39.9 %copy-start = (bf16[256,256]{1,0:T(8,128)(2,1)S(1)}, bf16[256,256]{1,0:T(8,128)(2,1)}, u32[]{:S(2)}) copy-start(bf16[256,256]{1,0:T(8,128)(2,1)} %constant.68.clone.refs_19_.refs_15_.refs_28_) | copy-start | bytes 393220
  0.6 39.9 %copy-start.1 = (bf16[256,256]{1,0:T(8,128)(2,1)S(1)}, bf16[256,256]{1,0:T(8,128)(2,1)}, u32[]{:S(2)}) copy-start(bf16[256,256]{1,0:T(8,128)(2,1)} %constant.67.clone.refs_18_.refs_14_.refs_27_) | copy-start | bytes 393220
  0.7 39.9 %copy-start.2 = (bf16[256,256]{1,0:T(8,128)(2,1)S(1)}, bf16[256,256]{1,0:T(8,128)(2,1)}, u32[]{:S(2)}) copy-start(bf16[256,256]{1,0:T(8,128)(2,1)} %constant.66.clone.refs_17_.refs_13_.refs_26_) | copy-start | bytes 393220
  0.7 39.9 %copy-start.3 = (bf16[256,256]{1,0:T(8,128)(2,1)S(1)}, bf16[256,256]{1,0:T(8,128)(2,1)}, u32[]{:S(2)}) copy-start(bf16[256,256]{1,0:T(8,128)(2,1)} %constant.65.clone.refs_16_.refs_12_.refs_25_) | copy-start | bytes 393220
  0.7 39.9 %copy-start.4 = (bf16[256,256]{1,0:T(8,128)(2,1)S(1)}, bf16[256,256]{1,0:T(8,128)(2,1)}, u32[]{:S(2)}) copy-start(bf16[256,256]{1,0:T(8,128)(2,1)} %constant.64.clone.refs_15_.refs_11_.refs_24_) | copy-start | bytes 393220
  0.7 39.9 %copy-start.5 = (bf16[256,256]{1,0:T(8,128)(2,1)S(1)}, bf16[256,256]{1,0:T(8,128)(2,1)}, u32[]{:S(2)}) copy-start(bf16[256,256]{1,0:T(8,128)(2,1)} %constant.63.clone.refs_14_.refs_10_.refs_23_) | copy-start | bytes 393220
  0.7 39.9 %copy-start.6 = (bf16[256,256]{1,0:T(8,128)(2,1)S(1)}, bf16[256,256]{1,0:T(8,128)(2,1)}, u32[]{:S(2)}) copy-start(bf16[256,256]{1,0:T(8,128)(2,1)} %constant.62.clone.refs_13_.refs_9_.refs_22_) | copy-start | bytes 393220
  4.1 6.4 %collective-permute-start.7 = (f32[11,32,256]{2,1,0:T(8,128)}, f32[11,32,256]{2,1,0:T(8,128)S(1)}, u32[]{:S(2)}, u32[]{:S(2)}) collective-permute-start(f32[11,32,256]{2,1,0:T(8,128)} %get-tuple-element.52), channel_id=1, source_target_pairs={{7,2},{6,10},{11,5},{10,13},{23,18},{22,26},{27,21},{26,29}} | collective-permute-start | bytes 1081352 | tf_op jit(solution)/shard_map/ppermute | solution.py:323
  4.7 6.5 %collective-permute-start.5 = (f32[11,32,256]{2,1,0:T(8,128)}, f32[11,32,256]{2,1,0:T(8,128)S(1)}, u32[]{:S(2)}, u32[]{:S(2)}) collective-permute-start(f32[11,32,256]{2,1,0:T(8,128)} %get-tuple-element.52), channel_id=1, source_target_pairs={{5,2},{4,10},{9,5},{8,13},{21,18},{20,26},{25,21},{24,29}} | collective-permute-start | bytes 1081352 | tf_op jit(solution)/shard_map/ppermute | solution.py:323
  5.4 31.3 %collective-permute-start.3 = (f32[11,32,256]{2,1,0:T(8,128)}, f32[11,32,256]{2,1,0:T(8,128)S(1)}, u32[]{:S(2)}, u32[]{:S(2)}) collective-permute-start(f32[11,32,256]{2,1,0:T(8,128)} %get-tuple-element.52), channel_id=1, source_target_pairs={{3,2},{2,10},{15,5},{14,13},{19,18},{18,26},{31,21},{30,29}} | collective-permute-start | bytes 1081352 | tf_op jit(solution)/shard_map/ppermute | solution.py:323
  9.1 29.7 %collective-permute-start.1 = (f32[11,32,256]{2,1,0:T(8,128)}, f32[11,32,256]{2,1,0:T(8,128)S(1)}, u32[]{:S(2)}, u32[]{:S(2)}) collective-permute-start(f32[11,32,256]{2,1,0:T(8,128)} %get-tuple-element.52), channel_id=1, source_target_pairs={{1,2},{0,10},{13,5},{12,13},{17,18},{16,26},{29,21},{28,29}} | collective-permute-start | bytes 1081352 | tf_op jit(solution)/shard_map/ppermute | solution.py:323
  9.8 29.0 %collective-permute-start.6 = (f32[11,32,256]{2,1,0:T(8,128)}, f32[11,32,256]{2,1,0:T(8,128)S(1)}, u32[]{:S(2)}, u32[]{:S(2)}) collective-permute-start(f32[11,32,256]{2,1,0:T(8,128)} %get-tuple-element.53), channel_id=1, source_target_pairs={{6,2},{7,10},{10,5},{11,13},{22,18},{23,26},{26,21},{27,29}} | collective-permute-start | bytes 1081352 | tf_op jit(solution)/shard_map/ppermute | solution.py:323
  10.5 28.3 %collective-permute-start.4 = (f32[11,32,256]{2,1,0:T(8,128)}, f32[11,32,256]{2,1,0:T(8,128)S(1)}, u32[]{:S(2)}, u32[]{:S(2)}) collective-permute-start(f32[11,32,256]{2,1,0:T(8,128)} %get-tuple-element.53), channel_id=1, source_target_pairs={{4,2},{5,10},{8,5},{9,13},{20,18},{21,26},{24,21},{25,29}} | collective-permute-start | bytes 1081352 | tf_op jit(solution)/shard_map/ppermute | solution.py:323
  11.2 29.4 %collective-permute-start.2 = (f32[11,32,256]{2,1,0:T(8,128)}, f32[11,32,256]{2,1,0:T(8,128)}, u32[]{:S(2)}, u32[]{:S(2)}) collective-permute-start(f32[11,32,256]{2,1,0:T(8,128)} %get-tuple-element.53), channel_id=1, source_target_pairs={{2,2},{3,10},{14,5},{15,13},{18,18},{19,26},{30,21},{31,29}} | collective-permute-start | bytes 1081352 | tf_op jit(solution)/shard_map/ppermute | solution.py:323
  36.7 3.9 %collective-permute-start = (f32[11,32,256]{2,1,0:T(8,128)}, f32[11,32,256]{2,1,0:T(8,128)}, u32[]{:S(2)}, u32[]{:S(2)}) collective-permute-start(f32[11,32,256]{2,1,0:T(8,128)} %get-tuple-element.53), channel_id=1, source_target_pairs={{0,2},{1,10},{12,5},{13,13},{16,18},{17,26},{28,21},{29,29}} | collective-permute-start | bytes 1081352 | tf_op jit(solution)/shard_map/ppermute | solution.py:323
  43.4 20.6 %collective-permute-start.8 = (f32[2,256,256]{2,1,0:T(8,128)S(1)}, f32[2,256,256]{2,1,0:T(8,128)S(1)}, u32[]{:S(2)}, u32[]{:S(2)}) collective-permute-start(f32[2,256,256]{2,1,0:T(8,128)S(1)} %get-tuple-element.25.refs_2_), channel_id=1, source_target_pairs={{0,8},{8,0},{16,24},{24,16},{1,9},{9,1},{17,25},{25,17},{2,10},{10... | collective-permute-start | bytes 1572872 | tf_op jit(solution)/shard_map/ppermute | solution.py:342
  43.6 29.3 %collective-permute-start.12 = (f32[10,32,256]{2,1,0:T(8,128)S(1)}, f32[10,32,256]{2,1,0:T(8,128)S(1)}, u32[]{:S(2)}, u32[]{:S(2)}) collective-permute-start(f32[10,32,256]{2,1,0:T(8,128)S(1)} %get-tuple-element.36), channel_id=1, source_target_pairs={{2,2},{3,10},{14,5},{15,13},{18,18},{19,26},{30,21},{31,29}} | collective-permute-start | bytes 983048 | tf_op jit(solution)/shard_map/ppermute | solution.py:323
  61.3 12.3 %collective-permute-start.10 = (f32[10,32,256]{2,1,0:T(8,128)S(1)}, f32[10,32,256]{2,1,0:T(8,128)S(1)}, u32[]{:S(2)}, u32[]{:S(2)}) collective-permute-start(f32[10,32,256]{2,1,0:T(8,128)S(1)} %get-tuple-element.36), channel_id=1, source_target_pairs={{0,2},{1,10},{12,5},{13,13},{16,18},{17,26},{28,21},{29,29}} | collective-permute-start | bytes 983048 | tf_op jit(solution)/shard_map/ppermute | solution.py:323
  62.0 14.4 %collective-permute-start.13 = (f32[10,32,256]{2,1,0:T(8,128)S(1)}, f32[10,32,256]{2,1,0:T(8,128)S(1)}, u32[]{:S(2)}, u32[]{:S(2)}) collective-permute-start(f32[10,32,256]{2,1,0:T(8,128)S(1)} %get-tuple-element.37), channel_id=1, source_target_pairs={{3,2},{2,10},{15,5},{14,13},{19,18},{18,26},{31,21},{30,29}} | collective-permute-start | bytes 983048 | tf_op jit(solution)/shard_map/ppermute | solution.py:323
  63.3 13.8 %collective-permute-start.11 = (f32[10,32,256]{2,1,0:T(8,128)S(1)}, f32[10,32,256]{2,1,0:T(8,128)S(1)}, u32[]{:S(2)}, u32[]{:S(2)}) collective-permute-start(f32[10,32,256]{2,1,0:T(8,128)S(1)} %get-tuple-element.37), channel_id=1, source_target_pairs={{1,2},{0,10},{13,5},{12,13},{17,18},{16,26},{29,21},{28,29}} | collective-permute-start | bytes 983048 | tf_op jit(solution)/shard_map/ppermute | solution.py:323
  68.9 9.0 %collective-permute-start.9 = (f32[2,256,256]{2,1,0:T(8,128)S(1)}, f32[2,256,256]{2,1,0:T(8,128)S(1)}, u32[]{:S(2)}, u32[]{:S(2)}) collective-permute-start(f32[2,256,256]{2,1,0:T(8,128)S(1)} %get-tuple-element.31.refs_5_), channel_id=1, source_target_pairs={{0,8},{8,0},{16,24},{24,16},{1,9},{9,1},{17,25},{25,17},{2,10},{10... | collective-permute-start | bytes 1572872 | tf_op jit(solution)/shard_map/ppermute | solution.py:351
  72.9 4.9 %collective-permute-start.16 = (f32[10,32,256]{2,1,0:T(8,128)S(1)}, f32[10,32,256]{2,1,0:T(8,128)S(1)}, u32[]{:S(2)}, u32[]{:S(2)}) collective-permute-start(f32[10,32,256]{2,1,0:T(8,128)S(1)} %get-tuple-element.36), channel_id=1, source_target_pairs={{6,2},{7,10},{10,5},{11,13},{22,18},{23,26},{26,21},{27,29}} | collective-permute-start | bytes 983048 | tf_op jit(solution)/shard_map/ppermute | solution.py:323
  73.6 4.2 %collective-permute-start.14 = (f32[10,32,256]{2,1,0:T(8,128)S(1)}, f32[10,32,256]{2,1,0:T(8,128)S(1)}, u32[]{:S(2)}, u32[]{:S(2)}) collective-permute-start(f32[10,32,256]{2,1,0:T(8,128)S(1)} %get-tuple-element.36), channel_id=1, source_target_pairs={{4,2},{5,10},{8,5},{9,13},{20,18},{21,26},{24,21},{25,29}} | collective-permute-start | bytes 983048 | tf_op jit(solution)/shard_map/ppermute | solution.py:323
  76.4 1.4 %collective-permute-start.17 = (f32[10,32,256]{2,1,0:T(8,128)S(1)}, f32[10,32,256]{2,1,0:T(8,128)S(1)}, u32[]{:S(2)}, u32[]{:S(2)}) collective-permute-start(f32[10,32,256]{2,1,0:T(8,128)S(1)} %get-tuple-element.37), channel_id=1, source_target_pairs={{7,2},{6,10},{11,5},{10,13},{23,18},{22,26},{27,21},{26,29}} | collective-permute-start | bytes 983048 | tf_op jit(solution)/shard_map/ppermute | solution.py:323
  77.1 0.7 collective-permute-start.15
  82.2 16.4 %collective-permute-start.18 = (f32[520,256]{1,0:T(8,128)}, f32[520,256]{1,0:T(8,128)S(1)}, u32[]{:S(2)}, u32[]{:S(2)}) collective-permute-start(f32[520,256]{1,0:T(8,128)} %get-tuple-element.38.refs_1_), channel_id=1, source_target_pairs={{0,8},{8,0},{16,24},{24,16},{1,9},{9,1},{17,25},{25,17},{2,10},{10... | collective-permute-start | bytes 1597448 | tf_op jit(solution)/shard_map/ppermute | solution.py:365
  100.2 3.3 %collective-permute-start.19 = (f32[3,32,256]{2,1,0:T(8,128)S(1)}, f32[3,32,256]{2,1,0:T(8,128)S(1)}, u32[]{:S(2)}, u32[]{:S(2)}) collective-permute-start(f32[3,32,256]{2,1,0:T(8,128)S(1)} %get-tuple-element.42), channel_id=1, source_target_pairs={{2,0},{10,4},{5,8},{13,12},{18,16},{26,20},{21,24},{29,28}} | collective-permute-start | bytes 294920 | tf_op jit(solution)/shard_map/ppermute | solution.py:375
  100.9 2.7 %collective-permute-start.20 = (f32[3,32,256]{2,1,0:T(8,128)S(1)}, f32[3,32,256]{2,1,0:T(8,128)S(1)}, u32[]{:S(2)}, u32[]{:S(2)}) collective-permute-start(f32[3,32,256]{2,1,0:T(8,128)S(1)} %get-tuple-element.43), channel_id=1, source_target_pairs={{2,1},{10,5},{5,9},{13,13},{18,17},{26,21},{21,25},{29,29}} | collective-permute-start | bytes 294920 | tf_op jit(solution)/shard_map/ppermute | solution.py:375
  101.6 2.0 %collective-permute-start.21 = (f32[3,32,256]{2,1,0:T(8,128)S(1)}, f32[3,32,256]{2,1,0:T(8,128)S(1)}, u32[]{:S(2)}, u32[]{:S(2)}) collective-permute-start(f32[3,32,256]{2,1,0:T(8,128)S(1)} %get-tuple-element.44), channel_id=1, source_target_pairs={{2,2},{10,6},{5,10},{13,14},{18,18},{26,22},{21,26},{29,30}} | collective-permute-start | bytes 294920 | tf_op jit(solution)/shard_map/ppermute | solution.py:375
  102.2 20.9 %collective-permute-start.22 = (f32[3,32,256]{2,1,0:T(8,128)S(1)}, f32[3,32,256]{2,1,0:T(8,128)S(1)}, u32[]{:S(2)}, u32[]{:S(2)}) collective-permute-start(f32[3,32,256]{2,1,0:T(8,128)S(1)} %get-tuple-element.45), channel_id=1, source_target_pairs={{2,3},{10,7},{5,11},{13,15},{18,19},{26,23},{21,27},{29,31}} | collective-permute-start | bytes 294920 | tf_op jit(solution)/shard_map/ppermute | solution.py:375
  123.2 3.3 %collective-permute-start.23 = (f32[32,256]{1,0:T(8,128)S(1)}, f32[32,256]{1,0:T(8,128)S(1)}, u32[]{:S(2)}, u32[]{:S(2)}) collective-permute-start(f32[32,256]{1,0:T(8,128)S(1)} %slice_bitcast_fusion.1), channel_id=1, source_target_pairs={{0,8},{8,0},{16,24},{24,16},{1,9},{9,1},{17,25},{25,17},{2,10},{10... | collective-permute-start | bytes 98312 | tf_op jit(solution)/shard_map/ppermute | solution.py:383
  126.5 3.9 %collective-permute-start.24 = (f32[32,256]{1,0:T(8,128)S(1)}, f32[32,256]{1,0:T(8,128)S(1)}, u32[]{:S(2)}, u32[]{:S(2)}) collective-permute-start(f32[32,256]{1,0:T(8,128)S(1)} %fusion.1), channel_id=1, source_target_pairs={{0,16},{8,24},{16,0},{24,8},{1,17},{9,25},{17,1},{25,9},{2,18},{10... | collective-permute-start | bytes 98312 | tf_op jit(solution)/shard_map/ppermute | solution.py:383
  (13 other events, 151.0 us)
where the time goes:
time: 132 us; the launch traced here: 131 us
  starting transfers between devices  66.4 us (50%)
  waiting for transfers between devices  44.6 us (34%)
  Pallas kernels  9.96 us (8%)
  local copies, waits for them, and re-layouts  6.52 us (5%)
  between operations  1.82 us (1%)
  other arithmetic  1.77 us (1%)
    ppermute x16, starting transfers between devices, gather(): lax.ppermute(sends[k % 2], BOTH, gather_pairs(k, pieces, blocks))  44.4 us
    ppermute x16, waiting for transfers between devices, gather(): lax.ppermute(sends[k % 2], BOTH, gather_pairs(k, pieces, blocks))  20.6 us
    ppermute x4, waiting for transfers between devices, steps(): lax.ppermute(outs[k], BOTH, scatter_pairs(k, pieces, blocks))  19.6 us
    ppermute x1, starting transfers between devices, steps(): other = lax.ppermute(mine, 'cuts', swap)  14.7 us
    pallas_call x4, Pallas kernels, run(): return pl.pallas_call(*args, compiler_params=PARAMS, **kwargs)(*operands)  9.96 us
    unnamed x41, local copies, waits for them, and re-layouts  4.21 us
    ppermute x2, starting transfers between devices, steps(): lax.ppermute(term, 'cuts', [(i, i ^ step) for i in range(pieces)])  3.99 us
    ppermute x4, starting transfers between devices, steps(): lax.ppermute(outs[k], BOTH, scatter_pairs(k, pieces, blocks))  3.29 us
  transfers between devices with their start and end apart: 25, of which 8 were waited for; matrix products, arithmetic and copies ran while one was open for 1% of the time, Pallas kernels for 2%

commit v1 on v0

--- a/solution.py
+++ b/solution.py
@@ -118,8 +118,14 @@
     part_ref[0], part_ref[1] = adjoint(re * wide, im * wide, maps, count, tables)
 
 
-def block_row(turn, flip, extent):
-    return pl.multiple_of(lax.bitwise_xor(jnp.int32(turn), flip) * extent, extent)
+def block_of(turn, half, column, blocks):
+    return ((turn % (blocks // 2)) ^ half) * 2 + (column ^ (2 * turn // blocks))
+
+
+def block_row(turn, info, blocks, extent):
+    across = lax.bitwise_xor(jnp.int32(turn % (blocks // 2)), info[2])
+    block = across * 2 + lax.bitwise_xor(info[0], jnp.int32(2 * turn // blocks))
+    return pl.multiple_of(block * extent, extent)
 
 
 def at_home(kernel):
@@ -138,7 +144,7 @@
     extent = messages[0].shape[1]
     copies = []
     for k, msg in enumerate(messages):
-        rows = pl.ds(block_row(k, info[0], extent), extent)
+        rows = pl.ds(block_row(k, info, blocks, extent), extent)
         copies += [
             pltpu.make_async_copy(msg.at[:planes], maps.at[:, rows], sems.at[0, k]),
             pltpu.make_async_copy(msg.at[pl.ds(planes, 2)], image.at[:, rows], sems.at[1, k]),
@@ -179,7 +185,7 @@
     extent = messages[0].shape[1]
     copies = []
     for k, msg in enumerate(messages):
-        rows = pl.ds(block_row(k, info[0], extent), extent)
+        rows = pl.ds(block_row(k, info, blocks, extent), extent)
         copies += [
             pltpu.make_async_copy(msg.at[pl.ds(planes, 2)], recon.at[:, rows], sems.at[1, k]),
             pltpu.make_async_copy(msg.at[:planes], data.at[:, rows], sems.at[0, k]),
@@ -251,7 +257,7 @@
 VMEM = pl.BlockSpec(memory_space=pltpu.VMEM)
 SMEM = pl.BlockSpec(memory_space=pltpu.SMEM)
 ANY = pl.BlockSpec(memory_space=pl.ANY)
-PARAMS = pltpu.CompilerParams(vmem_limit_bytes=48 << 20)
+PARAMS = pltpu.CompilerParams(vmem_limit_bytes=24 << 20)
 
 
 def shape(*dims):
@@ -267,7 +273,7 @@
     pairs = []
     for piece in range(pieces):
         for half in range(2):
-            block = turn ^ half ^ (blocks // 2 if piece % 2 else 0)
+            block = block_of(turn, half, piece % 2, blocks)
             target = (piece - piece % 2 + half) * blocks + home_row(piece, blocks)
             pairs.append((piece * blocks + block, target))
     return pairs
@@ -295,11 +301,10 @@
     pieces = lax.axis_size("cuts")
     row = lax.axis_index("rows")
     half = lax.rem(lax.axis_index("cuts"), 2)
-    upper = row >= blocks // 2
-    home = (row == home_row(0, blocks)) | (row == home_row(1, blocks))
-    flip = jnp.bitwise_xor(half, jnp.where(upper, blocks // 2, 0))
-    info = jnp.stack([flip, home.astype(jnp.int32), half]).astype(jnp.int32)
-    odd = lax.rem(row, 2)
+    column = (row == home_row(1, blocks)).astype(jnp.int32)
+    home = column + (row == home_row(0, blocks)).astype(jnp.int32)
+    info = jnp.stack([column, home, half]).astype(jnp.int32)
+    odd = lax.rem(row // 2, 2)
     extent = upstream_loss_derivative.shape[3]
     n = upstream_loss_derivative.shape[4]
     coils = receiver_profile_maps.shape[1]
@@ -326,8 +331,7 @@
     sends = build(maps, upstream, acquisition_choice_odds)
     first = gather(sends, near) + gather(sends, far)
     sends = build(data, recon)
-    sends = lax.optimization_barrier((*sends, *first[: blocks // 2]))[:2]
-    second = gather(sends, near)
+    second = gather(sends, near) + gather(sends, far)
 
     image, spectrum = shape(2, n, n), shape(2, n, count * n)
     scalars = shape(2, 8, 128)
@@ -340,8 +344,6 @@
         scratch_shapes=[pltpu.VMEM((n, n), F32), pltpu.SemaphoreType.DMA((3, blocks))],
     )(info, sigmoid_steepness, *first, *tables)
     other0 = lax.ppermute(part0, "cuts", swap)
-    sends = lax.optimization_barrier((*sends, part0))[:2]
-    second += gather(sends, far)
     res1, dir1, sc1, spec1, part1 = call(
         at_home(second_kernel),
         in_specs=[SMEM] + [VMEM] * 15,

time: 132 us -> 124 us (0.939)
  Pallas kernels: 9.96 us -> 3.11 us
  waiting for transfers between devices: 44.6 us -> 49.5 us
  local copies, waits for them, and re-layouts: 6.52 us -> 3.03 us
  starting transfers between devices: 66.4 us -> 63.9 us
    ppermute x1, starting transfers between devices: 14.7 us -> 0.07 us  [steps(): other = lax.ppermute(mine, 'cuts', swap)]
    ppermute x16, waiting for transfers between devices: 20.6 us -> 29.9 us  [gather(): lax.ppermute(sends[k % 2], BOTH, gather_pairs(k, pieces, blocks))]
    ppermute x16, starting transfers between devices: 44.4 us -> 52.2 us  [gather(): lax.ppermute(sends[k % 2], BOTH, gather_pairs(k, pieces, blocks))]
    pallas_call x4, Pallas kernels: 9.96 us -> 3.11 us  [run(): return pl.pallas_call(*args, compiler_params=PARAMS, **kwargs)(*operands)]
    ppermute x4, waiting for transfers between devices: 19.6 us -> 15.1 us  [steps(): lax.ppermute(outs[k], BOTH, scatter_pairs(k, pieces, blocks))]
    ppermute x1, starting transfers between devices: 0.01 us -> 3.56 us  [steps(): other1 = lax.ppermute(part1, 'cuts', swap)]
    unnamed x41 -> x31, local copies, waits for them, and re-layouts: 4.21 us -> 0.72 us
  transfers between devices with their start and end apart: 25 -> 25, of which waited for: 8 -> 8; matrix products, arithmetic and copies ran while one was open for 1% -> 1% of each run, Pallas kernels for 2% -> 1%
where the time goes in v1:
time: 124 us; the launch traced here: 123 us
  starting transfers between devices  63.9 us (52%)
  waiting for transfers between devices  49.5 us (40%)
  Pallas kernels  3.11 us (3%)
  local copies, waits for them, and re-layouts  3.03 us (2%)
  between operations  1.78 us (1%)
  other arithmetic  1.76 us (1%)
    ppermute x16, starting transfers between devices, gather(): lax.ppermute(sends[k % 2], BOTH, gather_pairs(k, pieces, blocks))  52.2 us
    ppermute x16, waiting for transfers between devices, gather(): lax.ppermute(sends[k % 2], BOTH, gather_pairs(k, pieces, blocks))  29.9 us
    ppermute x4, waiting for transfers between devices, steps(): lax.ppermute(outs[k], BOTH, scatter_pairs(k, pieces, blocks))  15.1 us
    ppermute x2, starting transfers between devices, steps(): lax.ppermute(term, 'cuts', [(i, i ^ step) for i in range(pieces)])  4.1 us
    ppermute x1, starting transfers between devices, steps(): other1 = lax.ppermute(part1, 'cuts', swap)  3.56 us
    ppermute x4, starting transfers between devices, steps(): lax.ppermute(outs[k], BOTH, scatter_pairs(k, pieces, blocks))  3.29 us
    pallas_call x4, Pallas kernels, run(): return pl.pallas_call(*args, compiler_params=PARAMS, **kwargs)(*operands)  3.11 us
    ppermute x2, waiting for transfers between devices, steps(): lax.ppermute(term, 'cuts', [(i, i ^ step) for i in range(pieces)])  2.62 us
  transfers between devices with their start and end apart: 25, of which 8 were waited for; matrix products, arithmetic and copies ran while one was open for 1% of the time, Pallas kernels for 1%

profile of v1, /device:TPU:10, one launch (start us, length us, event | category | flops | bytes accessed | tf_op | source)
XLA Modules:
  0.0 123.1 jit_solution(139175256398642471)
XLA Ops:
  0.8 2.3 %dynamic-slice_bitcast_fusion = (f32[8,32,256]{2,1,0:T(8,128)}, f32[8,32,256]{2,1,0:T(8,128)}, f32[8,32,256]{2,1,0:T(8,128)S(1)}, f32[8,32,256]{2,1,0:T(8,128)S(1)}) fusion(f32[2,8,32,256]{3,2,1,0:T(8,128)} %bitcast.29, s32[]{:T(128)S(6)} %select_n.16, s32[]{:T(128)S(6)} %select_n.15, f32[2,8,32,256]{3,2,1,0:T(8,128)} %bitcast.30), kind=kLoop, calls=%fused_computation.6 | loop fusion | bytes 2097160 | tf_op jit(solution)/shard_map/jit(dynamic_index_in_dim)/squeeze | solution.py:320
  3.1 1.0 pad_maximum_fusion
  4.1 0.7 collective-permute-start.7
  4.8 3.1 %collective-permute-start.5 = (f32[11,32,256]{2,1,0:T(8,128)}, f32[11,32,256]{2,1,0:T(8,128)S(1)}, u32[]{:S(2)}, u32[]{:S(2)}) collective-permute-start(f32[11,32,256]{2,1,0:T(8,128)} %get-tuple-element.44), channel_id=1, source_target_pairs={{3,2},{1,10},{10,5},{8,13},{19,18},{17,26},{26,21},{24,29}} | collective-permute-start | bytes 1081352 | tf_op jit(solution)/shard_map/ppermute | solution.py:328
  7.8 0.7 collective-permute-start.3
  8.5 0.7 collective-permute-start.1
  9.2 0.7 collective-permute-start.6
  9.9 18.0 %collective-permute-start.4 = (f32[11,32,256]{2,1,0:T(8,128)}, f32[11,32,256]{2,1,0:T(8,128)S(1)}, u32[]{:S(2)}, u32[]{:S(2)}) collective-permute-start(f32[11,32,256]{2,1,0:T(8,128)} %get-tuple-element.45), channel_id=1, source_target_pairs={{1,2},{3,10},{8,5},{10,13},{17,18},{19,26},{24,21},{26,29}} | collective-permute-start | bytes 1081352 | tf_op jit(solution)/shard_map/ppermute | solution.py:328
  27.9 7.5 %collective-permute-done.5.refs_7_ = f32[11,32,256]{2,1,0:T(8,128)S(1)} collective-permute-done((f32[11,32,256]{2,1,0:T(8,128)}, f32[11,32,256]{2,1,0:T(8,128)S(1)}, u32[]{:S(2)}, u32[]{:S(2)}) %collective-permute-start.5) | collective-permute-done | bytes 360480 | tf_op jit(solution)/shard_map/ppermute | solution.py:328
  35.4 1.4 %collective-permute-start.2 = (f32[11,32,256]{2,1,0:T(8,128)}, f32[11,32,256]{2,1,0:T(8,128)}, u32[]{:S(2)}, u32[]{:S(2)}) collective-permute-start(f32[11,32,256]{2,1,0:T(8,128)} %get-tuple-element.45), channel_id=1, source_target_pairs={{4,2},{6,10},{13,5},{15,13},{20,18},{22,26},{29,21},{31,29}} | collective-permute-start | bytes 1081352 | tf_op jit(solution)/shard_map/ppermute | solution.py:328
  36.8 1.4 %collective-permute-start = (f32[11,32,256]{2,1,0:T(8,128)}, f32[11,32,256]{2,1,0:T(8,128)}, u32[]{:S(2)}, u32[]{:S(2)}) collective-permute-start(f32[11,32,256]{2,1,0:T(8,128)} %get-tuple-element.45), channel_id=1, source_target_pairs={{0,2},{2,10},{9,5},{11,13},{16,18},{18,26},{25,21},{27,29}} | collective-permute-start | bytes 1081352 | tf_op jit(solution)/shard_map/ppermute | solution.py:328
  39.4 0.8 shard_map.167
  40.2 0.7 collective-permute-start.8
  40.9 0.7 collective-permute-start.17
  41.6 19.1 %collective-permute-start.15 = (f32[10,32,256]{2,1,0:T(8,128)S(1)}, f32[10,32,256]{2,1,0:T(8,128)S(1)}, u32[]{:S(2)}, u32[]{:S(2)}) collective-permute-start(f32[10,32,256]{2,1,0:T(8,128)S(1)} %get-tuple-element.46), channel_id=1, source_target_pairs={{3,2},{1,10},{10,5},{8,13},{19,18},{17,26},{26,21},{24,29}} | collective-permute-start | bytes 983048 | tf_op jit(solution)/shard_map/ppermute | solution.py:328
  60.8 0.7 collective-permute-start.13
  61.4 0.7 collective-permute-start.11
  62.1 0.7 shard_map.168
  62.9 3.6 %collective-permute-start.9 = (f32[2,256,256]{2,1,0:T(8,128)S(1)}, f32[2,256,256]{2,1,0:T(8,128)S(1)}, u32[]{:S(2)}, u32[]{:S(2)}) collective-permute-start(f32[2,256,256]{2,1,0:T(8,128)S(1)} %get-tuple-element.27.refs_5_), channel_id=1, source_target_pairs={{0,8},{8,0},{16,24},{24,16},{1,9},{9,1},{17,25},{25,17},{2,10},{10... | collective-permute-start | bytes 1572872 | tf_op jit(solution)/shard_map/ppermute | solution.py:353
  67.1 8.4 %collective-permute-done.15.refs_16_ = f32[10,32,256]{2,1,0:T(8,128)S(1)} collective-permute-done((f32[10,32,256]{2,1,0:T(8,128)S(1)}, f32[10,32,256]{2,1,0:T(8,128)S(1)}, u32[]{:S(2)}, u32[]{:S(2)}) %collective-permute-start.15) | collective-permute-done | bytes 327712 | tf_op jit(solution)/shard_map/ppermute | solution.py:328
  75.5 2.4 %collective-permute-start.14 = (f32[10,32,256]{2,1,0:T(8,128)S(1)}, f32[10,32,256]{2,1,0:T(8,128)S(1)}, u32[]{:S(2)}, u32[]{:S(2)}) collective-permute-start(f32[10,32,256]{2,1,0:T(8,128)S(1)} %get-tuple-element.47), channel_id=1, source_target_pairs={{1,2},{3,10},{8,5},{10,13},{17,18},{19,26},{24,21},{26,29}} | collective-permute-start | bytes 983048 | tf_op jit(solution)/shard_map/ppermute | solution.py:328
  78.0 0.7 collective-permute-start.12
  78.7 0.7 collective-permute-start.10
  79.4 13.6 %collective-permute-done.14.refs_15_ = f32[10,32,256]{2,1,0:T(8,128)S(1)} collective-permute-done((f32[10,32,256]{2,1,0:T(8,128)S(1)}, f32[10,32,256]{2,1,0:T(8,128)S(1)}, u32[]{:S(2)}, u32[]{:S(2)}) %collective-permute-start.14) | collective-permute-done | bytes 327712 | tf_op jit(solution)/shard_map/ppermute | solution.py:328
  93.0 1.0 shard_map.169
  94.1 1.9 %collective-permute-done.18.refs_2_ = f32[520,256]{1,0:T(8,128)S(1)} collective-permute-done((f32[520,256]{1,0:T(8,128)S(1)}, f32[520,256]{1,0:T(8,128)S(1)}, u32[]{:S(2)}, u32[]{:S(2)}) %collective-permute-start.18) | collective-permute-done | bytes 532512 | tf_op jit(solution)/shard_map/ppermute | solution.py:367
  98.6 1.3 %collective-permute-start.22 = (f32[3,32,256]{2,1,0:T(8,128)S(1)}, f32[3,32,256]{2,1,0:T(8,128)S(1)}, u32[]{:S(2)}, u32[]{:S(2)}) collective-permute-start(f32[3,32,256]{2,1,0:T(8,128)S(1)} %get-tuple-element.37), channel_id=1, source_target_pairs={{2,3},{10,7},{5,11},{13,15},{18,19},{26,23},{21,27},{29,31}} | collective-permute-start | bytes 294920 | tf_op jit(solution)/shard_map/ppermute | solution.py:377
  100.0 15.1 %collective-permute-done.22 = f32[3,32,256]{2,1,0:T(8,128)S(1)} collective-permute-done((f32[3,32,256]{2,1,0:T(8,128)S(1)}, f32[3,32,256]{2,1,0:T(8,128)S(1)}, u32[]{:S(2)}, u32[]{:S(2)}) %collective-permute-start.22) | collective-permute-done | bytes 98336 | tf_op jit(solution)/shard_map/ppermute | solution.py:377
  115.1 2.6 %collective-permute-start.23 = (f32[32,256]{1,0:T(8,128)S(1)}, f32[32,256]{1,0:T(8,128)S(1)}, u32[]{:S(2)}, u32[]{:S(2)}) collective-permute-start(f32[32,256]{1,0:T(8,128)S(1)} %slice_bitcast_fusion.1), channel_id=1, source_target_pairs={{0,8},{8,0},{16,24},{24,16},{1,9},{9,1},{17,25},{25,17},{2,10},{10... | collective-permute-start | bytes 98312 | tf_op jit(solution)/shard_map/ppermute | solution.py:385
  117.7 0.9 collective-permute-done.23
  118.6 1.5 %collective-permute-start.24 = (f32[32,256]{1,0:T(8,128)S(1)}, f32[32,256]{1,0:T(8,128)S(1)}, u32[]{:S(2)}, u32[]{:S(2)}) collective-permute-start(f32[32,256]{1,0:T(8,128)S(1)} %fusion.1), channel_id=1, source_target_pairs={{0,16},{8,24},{16,0},{24,8},{1,17},{9,25},{17,1},{25,9},{2,18},{10... | collective-permute-start | bytes 98312 | tf_op jit(solution)/shard_map/ppermute | solution.py:385
  120.7 1.8 %collective-permute-done.24 = f32[32,256]{1,0:T(8,128)S(1)} collective-permute-done((f32[32,256]{1,0:T(8,128)S(1)}, f32[32,256]{1,0:T(8,128)S(1)}, u32[]{:S(2)}, u32[]{:S(2)}) %collective-permute-start.24) | collective-permute-done | bytes 32800 | tf_op jit(solution)/shard_map/ppermute | solution.py:385
  (61 shorter events, 5.2 us)
Async XLA Ops:
  0.6 38.7 %copy-start = (bf16[256,256]{1,0:T(8,128)(2,1)S(1)}, bf16[256,256]{1,0:T(8,128)(2,1)}, u32[]{:S(2)}) copy-start(bf16[256,256]{1,0:T(8,128)(2,1)} %constant.76.clone.refs_19_.refs_15_.refs_28_) | copy-start | bytes 393220
  0.6 38.6 %copy-start.1 = (bf16[256,256]{1,0:T(8,128)(2,1)S(1)}, bf16[256,256]{1,0:T(8,128)(2,1)}, u32[]{:S(2)}) copy-start(bf16[256,256]{1,0:T(8,128)(2,1)} %constant.75.clone.refs_18_.refs_14_.refs_27_) | copy-start | bytes 393220
  0.7 38.6 %copy-start.2 = (bf16[256,256]{1,0:T(8,128)(2,1)S(1)}, bf16[256,256]{1,0:T(8,128)(2,1)}, u32[]{:S(2)}) copy-start(bf16[256,256]{1,0:T(8,128)(2,1)} %constant.74.clone.refs_17_.refs_13_.refs_26_) | copy-start | bytes 393220
  0.7 38.6 %copy-start.3 = (bf16[256,256]{1,0:T(8,128)(2,1)S(1)}, bf16[256,256]{1,0:T(8,128)(2,1)}, u32[]{:S(2)}) copy-start(bf16[256,256]{1,0:T(8,128)(2,1)} %constant.73.clone.refs_16_.refs_12_.refs_25_) | copy-start | bytes 393220
  0.7 38.6 %copy-start.4 = (bf16[256,256]{1,0:T(8,128)(2,1)S(1)}, bf16[256,256]{1,0:T(8,128)(2,1)}, u32[]{:S(2)}) copy-start(bf16[256,256]{1,0:T(8,128)(2,1)} %constant.72.clone.refs_15_.refs_11_.refs_24_) | copy-start | bytes 393220
  0.7 38.6 %copy-start.5 = (bf16[256,256]{1,0:T(8,128)(2,1)S(1)}, bf16[256,256]{1,0:T(8,128)(2,1)}, u32[]{:S(2)}) copy-start(bf16[256,256]{1,0:T(8,128)(2,1)} %constant.71.clone.refs_14_.refs_10_.refs_23_) | copy-start | bytes 393220
  0.7 38.6 %copy-start.6 = (bf16[256,256]{1,0:T(8,128)(2,1)S(1)}, bf16[256,256]{1,0:T(8,128)(2,1)}, u32[]{:S(2)}) copy-start(bf16[256,256]{1,0:T(8,128)(2,1)} %constant.70.clone.refs_13_.refs_9_.refs_22_) | copy-start | bytes 393220
  4.1 5.8 %collective-permute-start.7 = (f32[11,32,256]{2,1,0:T(8,128)}, f32[11,32,256]{2,1,0:T(8,128)S(1)}, u32[]{:S(2)}, u32[]{:S(2)}) collective-permute-start(f32[11,32,256]{2,1,0:T(8,128)} %get-tuple-element.44), channel_id=1, source_target_pairs={{7,2},{5,10},{14,5},{12,13},{23,18},{21,26},{30,21},{28,29}} | collective-permute-start | bytes 1081352 | tf_op jit(solution)/shard_map/ppermute | solution.py:328
  4.8 30.7 %collective-permute-start.5 = (f32[11,32,256]{2,1,0:T(8,128)}, f32[11,32,256]{2,1,0:T(8,128)S(1)}, u32[]{:S(2)}, u32[]{:S(2)}) collective-permute-start(f32[11,32,256]{2,1,0:T(8,128)} %get-tuple-element.44), channel_id=1, source_target_pairs={{3,2},{1,10},{10,5},{8,13},{19,18},{17,26},{26,21},{24,29}} | collective-permute-start | bytes 1081352 | tf_op jit(solution)/shard_map/ppermute | solution.py:328
  7.8 29.0 %collective-permute-start.3 = (f32[11,32,256]{2,1,0:T(8,128)}, f32[11,32,256]{2,1,0:T(8,128)S(1)}, u32[]{:S(2)}, u32[]{:S(2)}) collective-permute-start(f32[11,32,256]{2,1,0:T(8,128)} %get-tuple-element.44), channel_id=1, source_target_pairs={{6,2},{4,10},{15,5},{13,13},{22,18},{20,26},{31,21},{29,29}} | collective-permute-start | bytes 1081352 | tf_op jit(solution)/shard_map/ppermute | solution.py:328
  8.5 30.4 %collective-permute-start.1 = (f32[11,32,256]{2,1,0:T(8,128)}, f32[11,32,256]{2,1,0:T(8,128)S(1)}, u32[]{:S(2)}, u32[]{:S(2)}) collective-permute-start(f32[11,32,256]{2,1,0:T(8,128)} %get-tuple-element.44), channel_id=1, source_target_pairs={{2,2},{0,10},{11,5},{9,13},{18,18},{16,26},{27,21},{25,29}} | collective-permute-start | bytes 1081352 | tf_op jit(solution)/shard_map/ppermute | solution.py:328
  9.2 29.8 %collective-permute-start.6 = (f32[11,32,256]{2,1,0:T(8,128)}, f32[11,32,256]{2,1,0:T(8,128)S(1)}, u32[]{:S(2)}, u32[]{:S(2)}) collective-permute-start(f32[11,32,256]{2,1,0:T(8,128)} %get-tuple-element.45), channel_id=1, source_target_pairs={{5,2},{7,10},{12,5},{14,13},{21,18},{23,26},{28,21},{30,29}} | collective-permute-start | bytes 1081352 | tf_op jit(solution)/shard_map/ppermute | solution.py:328
  9.9 29.4 %collective-permute-start.4 = (f32[11,32,256]{2,1,0:T(8,128)}, f32[11,32,256]{2,1,0:T(8,128)S(1)}, u32[]{:S(2)}, u32[]{:S(2)}) collective-permute-start(f32[11,32,256]{2,1,0:T(8,128)} %get-tuple-element.45), channel_id=1, source_target_pairs={{1,2},{3,10},{8,5},{10,13},{17,18},{19,26},{24,21},{26,29}} | collective-permute-start | bytes 1081352 | tf_op jit(solution)/shard_map/ppermute | solution.py:328
  35.4 3.9 %collective-permute-start.2 = (f32[11,32,256]{2,1,0:T(8,128)}, f32[11,32,256]{2,1,0:T(8,128)}, u32[]{:S(2)}, u32[]{:S(2)}) collective-permute-start(f32[11,32,256]{2,1,0:T(8,128)} %get-tuple-element.45), channel_id=1, source_target_pairs={{4,2},{6,10},{13,5},{15,13},{20,18},{22,26},{29,21},{31,29}} | collective-permute-start | bytes 1081352 | tf_op jit(solution)/shard_map/ppermute | solution.py:328
  36.8 2.5 %collective-permute-start = (f32[11,32,256]{2,1,0:T(8,128)}, f32[11,32,256]{2,1,0:T(8,128)}, u32[]{:S(2)}, u32[]{:S(2)}) collective-permute-start(f32[11,32,256]{2,1,0:T(8,128)} %get-tuple-element.45), channel_id=1, source_target_pairs={{0,2},{2,10},{9,5},{11,13},{16,18},{18,26},{25,21},{27,29}} | collective-permute-start | bytes 1081352 | tf_op jit(solution)/shard_map/ppermute | solution.py:328
  40.2 22.0 %collective-permute-start.8 = (f32[2,256,256]{2,1,0:T(8,128)S(1)}, f32[2,256,256]{2,1,0:T(8,128)S(1)}, u32[]{:S(2)}, u32[]{:S(2)}) collective-permute-start(f32[2,256,256]{2,1,0:T(8,128)S(1)} %get-tuple-element.21.refs_2_), channel_id=1, source_target_pairs={{0,8},{8,0},{16,24},{24,16},{1,9},{9,1},{17,25},{25,17},{2,10},{10... | collective-permute-start | bytes 1572872 | tf_op jit(solution)/shard_map/ppermute | solution.py:346
  40.9 25.5 %collective-permute-start.17 = (f32[10,32,256]{2,1,0:T(8,128)S(1)}, f32[10,32,256]{2,1,0:T(8,128)S(1)}, u32[]{:S(2)}, u32[]{:S(2)}) collective-permute-start(f32[10,32,256]{2,1,0:T(8,128)S(1)} %get-tuple-element.46), channel_id=1, source_target_pairs={{7,2},{5,10},{14,5},{12,13},{23,18},{21,26},{30,21},{28,29}} | collective-permute-start | bytes 983048 | tf_op jit(solution)/shard_map/ppermute | solution.py:328
  41.6 33.9 %collective-permute-start.15 = (f32[10,32,256]{2,1,0:T(8,128)S(1)}, f32[10,32,256]{2,1,0:T(8,128)S(1)}, u32[]{:S(2)}, u32[]{:S(2)}) collective-permute-start(f32[10,32,256]{2,1,0:T(8,128)S(1)} %get-tuple-element.46), channel_id=1, source_target_pairs={{3,2},{1,10},{10,5},{8,13},{19,18},{17,26},{26,21},{24,29}} | collective-permute-start | bytes 983048 | tf_op jit(solution)/shard_map/ppermute | solution.py:328
  60.8 17.2 %collective-permute-start.13 = (f32[10,32,256]{2,1,0:T(8,128)S(1)}, f32[10,32,256]{2,1,0:T(8,128)S(1)}, u32[]{:S(2)}, u32[]{:S(2)}) collective-permute-start(f32[10,32,256]{2,1,0:T(8,128)S(1)} %get-tuple-element.46), channel_id=1, source_target_pairs={{6,2},{4,10},{15,5},{13,13},{22,18},{20,26},{31,21},{29,29}} | collective-permute-start | bytes 983048 | tf_op jit(solution)/shard_map/ppermute | solution.py:328
  61.4 17.2 %collective-permute-start.11 = (f32[10,32,256]{2,1,0:T(8,128)S(1)}, f32[10,32,256]{2,1,0:T(8,128)S(1)}, u32[]{:S(2)}, u32[]{:S(2)}) collective-permute-start(f32[10,32,256]{2,1,0:T(8,128)S(1)} %get-tuple-element.46), channel_id=1, source_target_pairs={{2,2},{0,10},{11,5},{9,13},{18,18},{16,26},{27,21},{25,29}} | collective-permute-start | bytes 983048 | tf_op jit(solution)/shard_map/ppermute | solution.py:328
  62.9 30.1 %collective-permute-start.9 = (f32[2,256,256]{2,1,0:T(8,128)S(1)}, f32[2,256,256]{2,1,0:T(8,128)S(1)}, u32[]{:S(2)}, u32[]{:S(2)}) collective-permute-start(f32[2,256,256]{2,1,0:T(8,128)S(1)} %get-tuple-element.27.refs_5_), channel_id=1, source_target_pairs={{0,8},{8,0},{16,24},{24,16},{1,9},{9,1},{17,25},{25,17},{2,10},{10... | collective-permute-start | bytes 1572872 | tf_op jit(solution)/shard_map/ppermute | solution.py:353
  66.5 12.9 %collective-permute-start.16 = (f32[10,32,256]{2,1,0:T(8,128)S(1)}, f32[10,32,256]{2,1,0:T(8,128)S(1)}, u32[]{:S(2)}, u32[]{:S(2)}) collective-permute-start(f32[10,32,256]{2,1,0:T(8,128)S(1)} %get-tuple-element.47), channel_id=1, source_target_pairs={{5,2},{7,10},{12,5},{14,13},{21,18},{23,26},{28,21},{30,29}} | collective-permute-start | bytes 983048 | tf_op jit(solution)/shard_map/ppermute | solution.py:328
  75.5 17.5 %collective-permute-start.14 = (f32[10,32,256]{2,1,0:T(8,128)S(1)}, f32[10,32,256]{2,1,0:T(8,128)S(1)}, u32[]{:S(2)}, u32[]{:S(2)}) collective-permute-start(f32[10,32,256]{2,1,0:T(8,128)S(1)} %get-tuple-element.47), channel_id=1, source_target_pairs={{1,2},{3,10},{8,5},{10,13},{17,18},{19,26},{24,21},{26,29}} | collective-permute-start | bytes 983048 | tf_op jit(solution)/shard_map/ppermute | solution.py:328
  78.0 15.0 %collective-permute-start.12 = (f32[10,32,256]{2,1,0:T(8,128)S(1)}, f32[10,32,256]{2,1,0:T(8,128)S(1)}, u32[]{:S(2)}, u32[]{:S(2)}) collective-permute-start(f32[10,32,256]{2,1,0:T(8,128)S(1)} %get-tuple-element.47), channel_id=1, source_target_pairs={{4,2},{6,10},{13,5},{15,13},{20,18},{22,26},{29,21},{31,29}} | collective-permute-start | bytes 983048 | tf_op jit(solution)/shard_map/ppermute | solution.py:328
  78.7 14.3 %collective-permute-start.10 = (f32[10,32,256]{2,1,0:T(8,128)S(1)}, f32[10,32,256]{2,1,0:T(8,128)S(1)}, u32[]{:S(2)}, u32[]{:S(2)}) collective-permute-start(f32[10,32,256]{2,1,0:T(8,128)S(1)} %get-tuple-element.47), channel_id=1, source_target_pairs={{0,2},{2,10},{9,5},{11,13},{16,18},{18,26},{25,21},{27,29}} | collective-permute-start | bytes 983048 | tf_op jit(solution)/shard_map/ppermute | solution.py:328
  94.1 2.0 %collective-permute-start.18 = (f32[520,256]{1,0:T(8,128)S(1)}, f32[520,256]{1,0:T(8,128)S(1)}, u32[]{:S(2)}, u32[]{:S(2)}) collective-permute-start(f32[520,256]{1,0:T(8,128)S(1)} %get-tuple-element.30.refs_1_), channel_id=1, source_target_pairs={{0,8},{8,0},{16,24},{24,16},{1,9},{9,1},{17,25},{25,17},{2,10},{10... | collective-permute-start | bytes 1597448 | tf_op jit(solution)/shard_map/ppermute | solution.py:367
  96.6 3.3 %collective-permute-start.19 = (f32[3,32,256]{2,1,0:T(8,128)S(1)}, f32[3,32,256]{2,1,0:T(8,128)S(1)}, u32[]{:S(2)}, u32[]{:S(2)}) collective-permute-start(f32[3,32,256]{2,1,0:T(8,128)S(1)} %get-tuple-element.34), channel_id=1, source_target_pairs={{2,0},{10,4},{5,8},{13,12},{18,16},{26,20},{21,24},{29,28}} | collective-permute-start | bytes 294920 | tf_op jit(solution)/shard_map/ppermute | solution.py:377
  97.3 2.7 %collective-permute-start.20 = (f32[3,32,256]{2,1,0:T(8,128)S(1)}, f32[3,32,256]{2,1,0:T(8,128)S(1)}, u32[]{:S(2)}, u32[]{:S(2)}) collective-permute-start(f32[3,32,256]{2,1,0:T(8,128)S(1)} %get-tuple-element.35), channel_id=1, source_target_pairs={{2,1},{10,5},{5,9},{13,13},{18,17},{26,21},{21,25},{29,29}} | collective-permute-start | bytes 294920 | tf_op jit(solution)/shard_map/ppermute | solution.py:377
  98.0 2.0 %collective-permute-start.21 = (f32[3,32,256]{2,1,0:T(8,128)S(1)}, f32[3,32,256]{2,1,0:T(8,128)S(1)}, u32[]{:S(2)}, u32[]{:S(2)}) collective-permute-start(f32[3,32,256]{2,1,0:T(8,128)S(1)} %get-tuple-element.36), channel_id=1, source_target_pairs={{2,2},{10,6},{5,10},{13,14},{18,18},{26,22},{21,26},{29,30}} | collective-permute-start | bytes 294920 | tf_op jit(solution)/shard_map/ppermute | solution.py:377
  98.6 16.5 %collective-permute-start.22 = (f32[3,32,256]{2,1,0:T(8,128)S(1)}, f32[3,32,256]{2,1,0:T(8,128)S(1)}, u32[]{:S(2)}, u32[]{:S(2)}) collective-permute-start(f32[3,32,256]{2,1,0:T(8,128)S(1)} %get-tuple-element.37), channel_id=1, source_target_pairs={{2,3},{10,7},{5,11},{13,15},{18,19},{26,23},{21,27},{29,31}} | collective-permute-start | bytes 294920 | tf_op jit(solution)/shard_map/ppermute | solution.py:377
  115.1 3.4 %collective-permute-start.23 = (f32[32,256]{1,0:T(8,128)S(1)}, f32[32,256]{1,0:T(8,128)S(1)}, u32[]{:S(2)}, u32[]{:S(2)}) collective-permute-start(f32[32,256]{1,0:T(8,128)S(1)} %slice_bitcast_fusion.1), channel_id=1, source_target_pairs={{0,8},{8,0},{16,24},{24,16},{1,9},{9,1},{17,25},{25,17},{2,10},{10... | collective-permute-start | bytes 98312 | tf_op jit(solution)/shard_map/ppermute | solution.py:385
  118.6 3.9 %collective-permute-start.24 = (f32[32,256]{1,0:T(8,128)S(1)}, f32[32,256]{1,0:T(8,128)S(1)}, u32[]{:S(2)}, u32[]{:S(2)}) collective-permute-start(f32[32,256]{1,0:T(8,128)S(1)} %fusion.1), channel_id=1, source_target_pairs={{0,16},{8,24},{16,0},{24,8},{1,17},{9,25},{17,1},{25,9},{2,18},{10... | collective-permute-start | bytes 98312 | tf_op jit(solution)/shard_map/ppermute | solution.py:385
  (8 other events, 126.4 us)

commit v2 on v1

--- a/solution.py
+++ b/solution.py
@@ -119,13 +119,18 @@
 
 
 def block_of(turn, half, column, blocks):
-    return ((turn % (blocks // 2)) ^ half) * 2 + (column ^ (2 * turn // blocks))
+    if turn < blocks // 2:
+        return turn ^ half, column
+    return (turn - blocks // 2) ^ half ^ (2 - 2 * column), 1 - column
 
 
 def block_row(turn, info, blocks, extent):
-    across = lax.bitwise_xor(jnp.int32(turn % (blocks // 2)), info[2])
-    block = across * 2 + lax.bitwise_xor(info[0], jnp.int32(2 * turn // blocks))
-    return pl.multiple_of(block * extent, extent)
+    column, half = info[0], info[2]
+    pair = lax.bitwise_xor(jnp.int32(turn % (blocks // 2)), half)
+    if turn >= blocks // 2:
+        pair = lax.bitwise_xor(pair, 2 - 2 * column)
+        column = 1 - column
+    return pl.multiple_of((pair * 2 + column) * extent, extent)
 
 
 def at_home(kernel):
@@ -269,13 +274,31 @@
     return first if piece % 2 == 0 else blocks - 1 - first
 
 
-def gather_pairs(turn, pieces, blocks):
+def detour(piece, blocks):
+    return (blocks // 2 - 1) * (piece % 2)
+
+
+def gather_pairs(turn, pieces, blocks, moved):
     pairs = []
     for piece in range(pieces):
         for half in range(2):
-            block = block_of(turn, half, piece % 2, blocks)
+            pair, column = block_of(turn, half, piece % 2, blocks)
+            source = piece * blocks + pair * 2 + column
+            if column != piece % 2 and moved(piece, pair):
+                source = (piece ^ 1) * blocks + pair * 2 + 1 - column
             target = (piece - piece % 2 + half) * blocks + home_row(piece, blocks)
-            pairs.append((piece * blocks + block, target))
+            pairs.append((source, target))
+    return pairs
+
+
+def move_pairs(pieces, blocks, moved):
+    pairs = []
+    for piece in range(pieces):
+        for pair in range(blocks // 2):
+            if moved(piece, pair):
+                column = piece % 2
+                source = piece * blocks + pair * 2 + 1 - column
+                pairs.append((source, (piece ^ 1) * blocks + pair * 2 + column))
     return pairs
 
 
@@ -320,18 +343,44 @@
     take = lambda values, i: lax.dynamic_index_in_dim(values, i, 0, keepdims=False)
 
     def build(values, *more):
-        return [
-            jnp.concatenate([take(values, i), *more], axis=0) for i in (odd, 1 - odd)
-        ]
-
-    def gather(sends, turns):
-        return [lax.ppermute(sends[k % 2], BOTH, gather_pairs(k, pieces, blocks)) for k in turns]
-
-    near, far = range(blocks // 2), range(blocks // 2, blocks)
+        sends = [jnp.concatenate([take(values, i), *more], axis=0) for i in (odd, 1 - odd)]
+        return lax.optimization_barrier(sends)
+
+    away = lax.rem(row + half, 2) == 1
+    far_end = row // 2 == (blocks // 2 - 1) * (1 - half)
+
+    def ends(piece, pair):
+        return pair == detour(piece, blocks)
+
+    def every(piece, pair):
+        return True
+
+    def move(sends, moved):
+        both = jnp.concatenate(sends, axis=0)
+        return jnp.split(lax.ppermute(both, BOTH, move_pairs(pieces, blocks, moved)), 2)
+
+    def gather(sends, turns, moved):
+        return {
+            k: lax.ppermute(sends[k % 2], BOTH, gather_pairs(k, pieces, blocks, moved))
+            for k in turns
+        }
+
+    turns = blocks // 2
+    near, far = range(turns), range(turns, blocks)
+    late = sorted({turns + 2, turns + 3, blocks - 2, blocks - 1})
     sends = build(maps, upstream, acquisition_choice_odds)
-    first = gather(sends, near) + gather(sends, far)
+    carried = move(sends, ends)
+    first = gather(sends, near, ends)
+    first |= gather(sends, [k for k in far if k not in late], ends)
+    sends = [jnp.where(away & far_end, c, s) for c, s in zip(carried, sends)]
+    first |= gather(sends, late, ends)
+    first = [first[k] for k in range(blocks)]
     sends = build(data, recon)
-    second = gather(sends, near) + gather(sends, far)
+    carried = move(sends, every)
+    second = gather(sends, near, every)
+    sends = [jnp.where(away, c, s) for c, s in zip(carried, sends)]
+    second |= gather(sends, far, every)
+    second = [second[k] for k in range(blocks)]
 
     image, spectrum = shape(2, n, n), shape(2, n, count * n)
     scalars = shape(2, 8, 128)
@@ -365,7 +414,6 @@
         ],
     )(info, u, res1, dir1, sc1, part1, other1, maps_full, wt, spec0, spec1, *second, *tables)
     other = lax.ppermute(mine, "cuts", swap)
-    turns = blocks // 2
     outs = call(
         at_home(fourth_kernel),
         in_specs=[SMEM] + [VMEM] * 5,

time: 124 us -> 113 us (0.911)
  waiting for transfers between devices: 49.5 us -> 39.9 us
  starting transfers between devices: 63.9 us -> 56.2 us
  other arithmetic: 1.76 us -> 8.35 us
    ppermute x16 -> x18, starting transfers between devices: 52.2 us -> 38.4 us  [the longest x16 35 us: gather(): lax.ppermute(sends[k % 2], BOTH, gather_pairs(k, pieces, blocks, moved))]
    ppermute x16 -> x18, waiting for transfers between devices: 29.9 us -> 16.8 us  [the longest x16 13 us: gather(): lax.ppermute(sends[k % 2], BOTH, gather_pairs(k, pieces, blocks, moved))]
    ppermute x1, starting transfers between devices: 3.56 us -> 10.4 us  [steps(): other1 = lax.ppermute(part1, 'cuts', swap)]
    ppermute x4, waiting for transfers between devices: 15.1 us -> 18.6 us  [steps(): lax.ppermute(outs[k], BOTH, scatter_pairs(k, pieces, blocks))]
    select_n x0 -> x2, other arithmetic: none -> 2.42 us  [the longest x1 2.3 us: steps(): sends = [jnp.where(away & far_end, c, s) for c, s in zip(carried, sends)]]
    concatenate x0 -> x2, other arithmetic: none -> 2.26 us  [move(): both = jnp.concatenate(sends, axis=0)]
    concatenate x2, other arithmetic: 1.01 us -> 2.92 us  [build(): jnp.concatenate([take(values, i), *more], axis=0)]
  transfers between devices with their start and end apart: 25 -> 27, of which waited for: 8 -> 8; matrix products, arithmetic and copies ran while one was open for 1% -> 6% of each run, Pallas kernels for 1% -> 1%
where the time goes in v2:
time: 113 us; the launch traced here: 112 us
  starting transfers between devices  56.2 us (50%)
  waiting for transfers between devices  39.9 us (35%)
  other arithmetic  8.35 us (7%)
  Pallas kernels  3.06 us (3%)
  local copies, waits for them, and re-layouts  2.82 us (2%)
  between operations  1.86 us (2%)
    ppermute x16, starting transfers between devices, gather(): lax.ppermute(sends[k % 2], BOTH, gather_pairs(k, pieces, blocks, moved))  35 us
    ppermute x4, waiting for transfers between devices, steps(): lax.ppermute(outs[k], BOTH, scatter_pairs(k, pieces, blocks))  18.6 us
    ppermute x16, waiting for transfers between devices, gather(): lax.ppermute(sends[k % 2], BOTH, gather_pairs(k, pieces, blocks, moved))  13 us
    ppermute x1, starting transfers between devices, steps(): other1 = lax.ppermute(part1, 'cuts', swap)  10.4 us
    ppermute x2, starting transfers between devices, steps(): lax.ppermute(term, 'cuts', [(i, i ^ step) for i in range(pieces)])  3.85 us
    ppermute x2, waiting for transfers between devices, move(): lax.ppermute(both, BOTH, move_pairs(pieces, blocks, moved))  3.77 us
    ppermute x2, starting transfers between devices, move(): lax.ppermute(both, BOTH, move_pairs(pieces, blocks, moved))  3.47 us
    ppermute x4, starting transfers between devices, steps(): lax.ppermute(outs[k], BOTH, scatter_pairs(k, pieces, blocks))  3.29 us
  transfers between devices with their start and end apart: 27, of which 8 were waited for; matrix products, arithmetic and copies ran while one was open for 6% of the time, Pallas kernels for 1%

profile of v2, /device:TPU:10, one launch (start us, length us, event | category | flops | bytes accessed | tf_op | source)
XLA Modules:
  0.0 112.2 jit_solution(16487646342439598495)
XLA Ops:
  0.7 2.1 %dynamic-slice_bitcast_fusion = (f32[8,32,256]{2,1,0:T(8,128)}, f32[8,32,256]{2,1,0:T(8,128)}, f32[8,32,256]{2,1,0:T(8,128)S(1)}, f32[8,32,256]{2,1,0:T(8,128)S(1)}) fusion(f32[2,8,32,256]{3,2,1,0:T(8,128)} %bitcast.29, s32[]{:T(128)S(6)} %select_n.41, s32[]{:T(128)S(6)} %select_n.40, f32[2,8,32,256]{3,2,1,0:T(8,128)} %bitcast.30), kind=kLoop, calls=%fused_computation.12 | loop fusion | bytes 2097160 | tf_op jit(solution)/shard_map/jit(dynamic_index_in_dim)/squeeze | solution.py:343
  2.8 0.9 pad_maximum_fusion.2
  3.7 1.1 %pad_maximum_fusion = f32[22,32,256]{2,1,0:T(8,128)S(1)} fusion(f32[11,32,256]{2,1,0:T(8,128)} %get-tuple-element.25, f32[11,32,256]{2,1,0:T(8,128)} %get-tuple-element.24), kind=kLoop, calls=%fused_computation | loop fusion | flops 180224 | bytes 1441792 | tf_op jit(solution)/shard_map/concatenate | solution.py:359
  4.9 1.5 %collective-permute-start.6 = (f32[22,32,256]{2,1,0:T(8,128)S(1)}, f32[22,32,256]{2,1,0:T(8,128)}, u32[]{:S(2)}, u32[]{:S(2)}) collective-permute-start(f32[22,32,256]{2,1,0:T(8,128)S(1)} %pad_maximum_fusion), channel_id=1, source_target_pairs={{1,8},{14,7},{17,24},{30,23}} | collective-permute-start | bytes 2162696 | tf_op jit(solution)/shard_map/ppermute | solution.py:360
  7.1 0.7 collective-permute-start.2
  7.8 0.7 collective-permute-start
  8.5 0.7 collective-permute-start.5
  10.0 0.8 collective-permute-start.3
  10.8 2.3 %slice_select_fusion = (f32[11,32,256]{2,1,0:T(8,128)}, f32[11,32,256]{2,1,0:T(8,128)}) fusion(f32[11,32,256]{2,1,0:T(8,128)} %get-tuple-element.25, f32[22,32,256]{2,1,0:T(8,128)} %collective-permute-done.6, pred[]{:T(512)S(6)} %and.16, f32[11,32,256]{2,1,0:T(8,128)} %get-tuple-element.24), kind=kLoop, calls=%fused_computation.8 | loop fusion | flops 180224 | bytes 2162689 | tf_op jit(solution)/shard_map/jit(_where)/select_n | solution.py:375
  13.8 11.7 %collective-permute-start.8 = (f32[11,32,256]{2,1,0:T(8,128)}, f32[11,32,256]{2,1,0:T(8,128)}, u32[]{:S(2)}, u32[]{:S(2)}) collective-permute-start(f32[11,32,256]{2,1,0:T(8,128)} %get-tuple-element.48), channel_id=1, source_target_pairs={{3,2},{8,10},{7,5},{12,13},{19,18},{24,26},{23,21},{28,29}} | collective-permute-start | bytes 1081352 | tf_op jit(solution)/shard_map/ppermute | solution.py:364
  25.5 2.0 %collective-permute-start.7 = (f32[11,32,256]{2,1,0:T(8,128)}, f32[11,32,256]{2,1,0:T(8,128)}, u32[]{:S(2)}, u32[]{:S(2)}) collective-permute-start(f32[11,32,256]{2,1,0:T(8,128)} %get-tuple-element.49), channel_id=1, source_target_pairs={{8,2},{3,10},{12,5},{7,13},{24,18},{19,26},{28,21},{23,29}} | collective-permute-start | bytes 1081352 | tf_op jit(solution)/shard_map/ppermute | solution.py:364
  27.6 2.0 %pad_maximum_fusion.6 = (f32[10,32,256]{2,1,0:T(8,128)}, f32[10,32,256]{2,1,0:T(8,128)}) fusion(f32[2,32,256]{2,1,0:T(8,128)} %bitcast.31, f32[8,32,256]{2,1,0:T(8,128)} %get-tuple-element.52, f32[8,32,256]{2,1,0:T(8,128)} %get-tuple-element.53), kind=kLoop, calls=%fused_computation.6 | loop fusion | flops 163840 | bytes 1245184 | tf_op jit(solution)/shard_map/concatenate | solution.py:346
  29.5 1.1 pad_maximum_fusion.1
  30.7 1.9 %collective-permute-start.15 = (f32[20,32,256]{2,1,0:T(8,128)S(1)}, f32[20,32,256]{2,1,0:T(8,128)S(1)}, u32[]{:S(2)}, u32[]{:S(2)}) collective-permute-start(f32[20,32,256]{2,1,0:T(8,128)S(1)} %pad_maximum_fusion.1), channel_id=1, source_target_pairs={{1,8},{3,10},{5,12},{7,14},{8,1},{10,3},{12,5},{14,7},{17,24},{19,... | collective-permute-start | bytes 1966088 | tf_op jit(solution)/shard_map/ppermute | solution.py:360
  32.7 1.6 %collective-permute-done.7.refs_8_ = f32[11,32,256]{2,1,0:T(8,128)} collective-permute-done((f32[11,32,256]{2,1,0:T(8,128)}, f32[11,32,256]{2,1,0:T(8,128)}, u32[]{:S(2)}, u32[]{:S(2)}) %collective-permute-start.7) | collective-permute-done | bytes 360480 | tf_op jit(solution)/shard_map/ppermute | solution.py:364
  34.4 0.8 shard_map.167
  35.3 0.7 collective-permute-start.13
  38.0 0.7 shard_map.168
  38.8 3.8 %collective-permute-done.15 = f32[20,32,256]{2,1,0:T(8,128)S(1)} collective-permute-done((f32[20,32,256]{2,1,0:T(8,128)S(1)}, f32[20,32,256]{2,1,0:T(8,128)S(1)}, u32[]{:S(2)}, u32[]{:S(2)}) %collective-permute-start.15) | collective-permute-done | bytes 655392 | tf_op jit(solution)/shard_map/ppermute | solution.py:360
  42.6 10.4 %collective-permute-start.10 = (f32[2,256,256]{2,1,0:T(8,128)S(1)}, f32[2,256,256]{2,1,0:T(8,128)S(1)}, u32[]{:S(2)}, u32[]{:S(2)}) collective-permute-start(f32[2,256,256]{2,1,0:T(8,128)S(1)} %get-tuple-element.33.refs_5_), channel_id=1, source_target_pairs={{0,8},{8,0},{16,24},{24,16},{1,9},{9,1},{17,25},{25,17},{2,10},{10... | collective-permute-start | bytes 1572872 | tf_op jit(solution)/shard_map/ppermute | solution.py:402
  53.8 10.0 %collective-permute-start.17 = (f32[10,32,256]{2,1,0:T(8,128)S(1)}, f32[10,32,256]{2,1,0:T(8,128)S(1)}, u32[]{:S(2)}, u32[]{:S(2)}) collective-permute-start(f32[10,32,256]{2,1,0:T(8,128)S(1)} %get-tuple-element.50), channel_id=1, source_target_pairs={{14,2},{12,10},{3,5},{1,13},{30,18},{28,26},{19,21},{17,29}} | collective-permute-start | bytes 983048 | tf_op jit(solution)/shard_map/ppermute | solution.py:364
  64.5 3.0 %collective-permute-start.16 = (f32[10,32,256]{2,1,0:T(8,128)S(1)}, f32[10,32,256]{2,1,0:T(8,128)S(1)}, u32[]{:S(2)}, u32[]{:S(2)}) collective-permute-start(f32[10,32,256]{2,1,0:T(8,128)S(1)} %get-tuple-element.51), channel_id=1, source_target_pairs={{12,2},{14,10},{1,5},{3,13},{28,18},{30,26},{17,21},{19,29}} | collective-permute-start | bytes 983048 | tf_op jit(solution)/shard_map/ppermute | solution.py:364
  67.5 7.9 %collective-permute-done.17.refs_16_ = f32[10,32,256]{2,1,0:T(8,128)S(1)} collective-permute-done((f32[10,32,256]{2,1,0:T(8,128)S(1)}, f32[10,32,256]{2,1,0:T(8,128)S(1)}, u32[]{:S(2)}, u32[]{:S(2)}) %collective-permute-start.17) | collective-permute-done | bytes 327712 | tf_op jit(solution)/shard_map/ppermute | solution.py:364
  75.4 3.5 %collective-permute-done.16.refs_15_ = f32[10,32,256]{2,1,0:T(8,128)S(1)} collective-permute-done((f32[10,32,256]{2,1,0:T(8,128)S(1)}, f32[10,32,256]{2,1,0:T(8,128)S(1)}, u32[]{:S(2)}, u32[]{:S(2)}) %collective-permute-start.16) | collective-permute-done | bytes 327712 | tf_op jit(solution)/shard_map/ppermute | solution.py:364
  78.9 1.0 shard_map.169
  80.0 1.9 %collective-permute-done.20.refs_2_ = f32[520,256]{1,0:T(8,128)S(1)} collective-permute-done((f32[520,256]{1,0:T(8,128)S(1)}, f32[520,256]{1,0:T(8,128)S(1)}, u32[]{:S(2)}, u32[]{:S(2)}) %collective-permute-start.20) | collective-permute-done | bytes 532512 | tf_op jit(solution)/shard_map/ppermute | solution.py:416
  84.5 1.3 %collective-permute-start.24 = (f32[3,32,256]{2,1,0:T(8,128)S(1)}, f32[3,32,256]{2,1,0:T(8,128)S(1)}, u32[]{:S(2)}, u32[]{:S(2)}) collective-permute-start(f32[3,32,256]{2,1,0:T(8,128)S(1)} %get-tuple-element.45), channel_id=1, source_target_pairs={{2,3},{10,7},{5,11},{13,15},{18,19},{26,23},{21,27},{29,31}} | collective-permute-start | bytes 294920 | tf_op jit(solution)/shard_map/ppermute | solution.py:425
  85.8 18.6 %collective-permute-done.24 = f32[3,32,256]{2,1,0:T(8,128)S(1)} collective-permute-done((f32[3,32,256]{2,1,0:T(8,128)S(1)}, f32[3,32,256]{2,1,0:T(8,128)S(1)}, u32[]{:S(2)}, u32[]{:S(2)}) %collective-permute-start.24) | collective-permute-done | bytes 98336 | tf_op jit(solution)/shard_map/ppermute | solution.py:425
  104.4 2.3 %collective-permute-start.25 = (f32[32,256]{1,0:T(8,128)S(1)}, f32[32,256]{1,0:T(8,128)S(1)}, u32[]{:S(2)}, u32[]{:S(2)}) collective-permute-start(f32[32,256]{1,0:T(8,128)S(1)} %slice_bitcast_fusion.1), channel_id=1, source_target_pairs={{0,8},{8,0},{16,24},{24,16},{1,9},{9,1},{17,25},{25,17},{2,10},{10... | collective-permute-start | bytes 98312 | tf_op jit(solution)/shard_map/ppermute | solution.py:433
  106.7 0.9 collective-permute-done.25
  107.6 1.5 %collective-permute-start.26 = (f32[32,256]{1,0:T(8,128)S(1)}, f32[32,256]{1,0:T(8,128)S(1)}, u32[]{:S(2)}, u32[]{:S(2)}) collective-permute-start(f32[32,256]{1,0:T(8,128)S(1)} %fusion.1), channel_id=1, source_target_pairs={{0,16},{8,24},{16,0},{24,8},{1,17},{9,25},{17,1},{25,9},{2,18},{10... | collective-permute-start | bytes 98312 | tf_op jit(solution)/shard_map/ppermute | solution.py:433
  109.8 1.8 %collective-permute-done.26 = f32[32,256]{1,0:T(8,128)S(1)} collective-permute-done((f32[32,256]{1,0:T(8,128)S(1)}, f32[32,256]{1,0:T(8,128)S(1)}, u32[]{:S(2)}, u32[]{:S(2)}) %collective-permute-start.26) | collective-permute-done | bytes 32800 | tf_op jit(solution)/shard_map/ppermute | solution.py:433
  (67 shorter events, 9.1 us)
Async XLA Ops:
  4.9 5.1 %collective-permute-start.6 = (f32[22,32,256]{2,1,0:T(8,128)S(1)}, f32[22,32,256]{2,1,0:T(8,128)}, u32[]{:S(2)}, u32[]{:S(2)}) collective-permute-start(f32[22,32,256]{2,1,0:T(8,128)S(1)} %pad_maximum_fusion), channel_id=1, source_target_pairs={{1,8},{14,7},{17,24},{30,23}} | collective-permute-start | bytes 2162696 | tf_op jit(solution)/shard_map/ppermute | solution.py:360
  6.4 6.7 %collective-permute-start.4 = (f32[11,32,256]{2,1,0:T(8,128)}, f32[11,32,256]{2,1,0:T(8,128)S(1)}, u32[]{:S(2)}, u32[]{:S(2)}) collective-permute-start(f32[11,32,256]{2,1,0:T(8,128)} %get-tuple-element.24), channel_id=1, source_target_pairs={{5,2},{7,10},{8,5},{10,13},{21,18},{23,26},{24,21},{26,29}} | collective-permute-start | bytes 1081352 | tf_op jit(solution)/shard_map/ppermute | solution.py:364
  7.1 6.7 %collective-permute-start.2 = (f32[11,32,256]{2,1,0:T(8,128)}, f32[11,32,256]{2,1,0:T(8,128)S(1)}, u32[]{:S(2)}, u32[]{:S(2)}) collective-permute-start(f32[11,32,256]{2,1,0:T(8,128)} %get-tuple-element.24), channel_id=1, source_target_pairs={{4,2},{6,10},{13,5},{15,13},{20,18},{22,26},{29,21},{31,29}} | collective-permute-start | bytes 1081352 | tf_op jit(solution)/shard_map/ppermute | solution.py:364
  7.8 17.7 %collective-permute-start = (f32[11,32,256]{2,1,0:T(8,128)}, f32[11,32,256]{2,1,0:T(8,128)S(1)}, u32[]{:S(2)}, u32[]{:S(2)}) collective-permute-start(f32[11,32,256]{2,1,0:T(8,128)} %get-tuple-element.24), channel_id=1, source_target_pairs={{0,2},{2,10},{9,5},{11,13},{16,18},{18,26},{25,21},{27,29}} | collective-permute-start | bytes 1081352 | tf_op jit(solution)/shard_map/ppermute | solution.py:364
  8.5 22.2 %collective-permute-start.5 = (f32[11,32,256]{2,1,0:T(8,128)}, f32[11,32,256]{2,1,0:T(8,128)S(1)}, u32[]{:S(2)}, u32[]{:S(2)}) collective-permute-start(f32[11,32,256]{2,1,0:T(8,128)} %get-tuple-element.25), channel_id=1, source_target_pairs={{7,2},{5,10},{10,5},{8,13},{23,18},{21,26},{26,21},{24,29}} | collective-permute-start | bytes 1081352 | tf_op jit(solution)/shard_map/ppermute | solution.py:364
  9.9 24.5 %copy-start = (bf16[256,256]{1,0:T(8,128)(2,1)S(1)}, bf16[256,256]{1,0:T(8,128)(2,1)}, u32[]{:S(2)}) copy-start(bf16[256,256]{1,0:T(8,128)(2,1)} %constant.81.clone.refs_19_.refs_15_.refs_28_) | copy-start | bytes 393220
  9.9 24.4 %copy-start.1 = (bf16[256,256]{1,0:T(8,128)(2,1)S(1)}, bf16[256,256]{1,0:T(8,128)(2,1)}, u32[]{:S(2)}) copy-start(bf16[256,256]{1,0:T(8,128)(2,1)} %constant.80.clone.refs_18_.refs_14_.refs_27_) | copy-start | bytes 393220
  9.9 24.4 %copy-start.2 = (bf16[256,256]{1,0:T(8,128)(2,1)S(1)}, bf16[256,256]{1,0:T(8,128)(2,1)}, u32[]{:S(2)}) copy-start(bf16[256,256]{1,0:T(8,128)(2,1)} %constant.79.clone.refs_17_.refs_13_.refs_26_) | copy-start | bytes 393220
  9.9 24.4 %copy-start.3 = (bf16[256,256]{1,0:T(8,128)(2,1)S(1)}, bf16[256,256]{1,0:T(8,128)(2,1)}, u32[]{:S(2)}) copy-start(bf16[256,256]{1,0:T(8,128)(2,1)} %constant.78.clone.refs_16_.refs_12_.refs_25_) | copy-start | bytes 393220
  9.9 24.4 %copy-start.4 = (bf16[256,256]{1,0:T(8,128)(2,1)S(1)}, bf16[256,256]{1,0:T(8,128)(2,1)}, u32[]{:S(2)}) copy-start(bf16[256,256]{1,0:T(8,128)(2,1)} %constant.77.clone.refs_15_.refs_11_.refs_24_) | copy-start | bytes 393220
  10.0 22.7 %collective-permute-start.3 = (f32[11,32,256]{2,1,0:T(8,128)}, f32[11,32,256]{2,1,0:T(8,128)S(1)}, u32[]{:S(2)}, u32[]{:S(2)}) collective-permute-start(f32[11,32,256]{2,1,0:T(8,128)} %get-tuple-element.25), channel_id=1, source_target_pairs={{6,2},{4,10},{15,5},{13,13},{22,18},{20,26},{31,21},{29,29}} | collective-permute-start | bytes 1081352 | tf_op jit(solution)/shard_map/ppermute | solution.py:364
  13.1 19.6 %collective-permute-start.1 = (f32[11,32,256]{2,1,0:T(8,128)}, f32[11,32,256]{2,1,0:T(8,128)S(1)}, u32[]{:S(2)}, u32[]{:S(2)}) collective-permute-start(f32[11,32,256]{2,1,0:T(8,128)} %get-tuple-element.25), channel_id=1, source_target_pairs={{2,2},{0,10},{11,5},{9,13},{18,18},{16,26},{27,21},{25,29}} | collective-permute-start | bytes 1081352 | tf_op jit(solution)/shard_map/ppermute | solution.py:364
  13.8 18.9 %collective-permute-start.8 = (f32[11,32,256]{2,1,0:T(8,128)}, f32[11,32,256]{2,1,0:T(8,128)}, u32[]{:S(2)}, u32[]{:S(2)}) collective-permute-start(f32[11,32,256]{2,1,0:T(8,128)} %get-tuple-element.48), channel_id=1, source_target_pairs={{3,2},{8,10},{7,5},{12,13},{19,18},{24,26},{23,21},{28,29}} | collective-permute-start | bytes 1081352 | tf_op jit(solution)/shard_map/ppermute | solution.py:364
  25.5 8.8 %collective-permute-start.7 = (f32[11,32,256]{2,1,0:T(8,128)}, f32[11,32,256]{2,1,0:T(8,128)}, u32[]{:S(2)}, u32[]{:S(2)}) collective-permute-start(f32[11,32,256]{2,1,0:T(8,128)} %get-tuple-element.49), channel_id=1, source_target_pairs={{8,2},{3,10},{12,5},{7,13},{24,18},{19,26},{28,21},{23,29}} | collective-permute-start | bytes 1081352 | tf_op jit(solution)/shard_map/ppermute | solution.py:364
  30.7 11.9 %collective-permute-start.15 = (f32[20,32,256]{2,1,0:T(8,128)S(1)}, f32[20,32,256]{2,1,0:T(8,128)S(1)}, u32[]{:S(2)}, u32[]{:S(2)}) collective-permute-start(f32[20,32,256]{2,1,0:T(8,128)S(1)} %pad_maximum_fusion.1), channel_id=1, source_target_pairs={{1,8},{3,10},{5,12},{7,14},{8,1},{10,3},{12,5},{14,7},{17,24},{19,... | collective-permute-start | bytes 1966088 | tf_op jit(solution)/shard_map/ppermute | solution.py:360
  35.2 2.2 %collective-permute-start.9 = (f32[2,256,256]{2,1,0:T(8,128)S(1)}, f32[2,256,256]{2,1,0:T(8,128)S(1)}, u32[]{:S(2)}, u32[]{:S(2)}) collective-permute-start(f32[2,256,256]{2,1,0:T(8,128)S(1)} %get-tuple-element.27.refs_2_), channel_id=1, source_target_pairs={{0,8},{8,0},{16,24},{24,16},{1,9},{9,1},{17,25},{25,17},{2,10},{10... | collective-permute-start | bytes 1572872 | tf_op jit(solution)/shard_map/ppermute | solution.py:395
  35.3 17.9 %collective-permute-start.13 = (f32[10,32,256]{2,1,0:T(8,128)S(1)}, f32[10,32,256]{2,1,0:T(8,128)S(1)}, u32[]{:S(2)}, u32[]{:S(2)}) collective-permute-start(f32[10,32,256]{2,1,0:T(8,128)S(1)} %copy-done.11), channel_id=1, source_target_pairs={{4,2},{6,10},{13,5},{15,13},{20,18},{22,26},{29,21},{31,29}} | collective-permute-start | bytes 983048 | tf_op jit(solution)/shard_map/ppermute | solution.py:364
  36.0 17.9 %collective-permute-start.11 = (f32[10,32,256]{2,1,0:T(8,128)S(1)}, f32[10,32,256]{2,1,0:T(8,128)S(1)}, u32[]{:S(2)}, u32[]{:S(2)}) collective-permute-start(f32[10,32,256]{2,1,0:T(8,128)S(1)} %copy-done.11), channel_id=1, source_target_pairs={{0,2},{2,10},{9,5},{11,13},{16,18},{18,26},{25,21},{27,29}} | collective-permute-start | bytes 983048 | tf_op jit(solution)/shard_map/ppermute | solution.py:364
  36.7 27.2 %collective-permute-start.14 = (f32[10,32,256]{2,1,0:T(8,128)S(1)}, f32[10,32,256]{2,1,0:T(8,128)S(1)}, u32[]{:S(2)}, u32[]{:S(2)}) collective-permute-start(f32[10,32,256]{2,1,0:T(8,128)S(1)} %copy-done.10), channel_id=1, source_target_pairs={{6,2},{4,10},{15,5},{13,13},{22,18},{20,26},{31,21},{29,29}} | collective-permute-start | bytes 983048 | tf_op jit(solution)/shard_map/ppermute | solution.py:364
  37.4 27.2 %collective-permute-start.12 = (f32[10,32,256]{2,1,0:T(8,128)S(1)}, f32[10,32,256]{2,1,0:T(8,128)S(1)}, u32[]{:S(2)}, u32[]{:S(2)}) collective-permute-start(f32[10,32,256]{2,1,0:T(8,128)S(1)} %copy-done.10), channel_id=1, source_target_pairs={{2,2},{0,10},{11,5},{9,13},{18,18},{16,26},{27,21},{25,29}} | collective-permute-start | bytes 983048 | tf_op jit(solution)/shard_map/ppermute | solution.py:364
  42.6 36.3 %collective-permute-start.10 = (f32[2,256,256]{2,1,0:T(8,128)S(1)}, f32[2,256,256]{2,1,0:T(8,128)S(1)}, u32[]{:S(2)}, u32[]{:S(2)}) collective-permute-start(f32[2,256,256]{2,1,0:T(8,128)S(1)} %get-tuple-element.33.refs_5_), channel_id=1, source_target_pairs={{0,8},{8,0},{16,24},{24,16},{1,9},{9,1},{17,25},{25,17},{2,10},{10... | collective-permute-start | bytes 1572872 | tf_op jit(solution)/shard_map/ppermute | solution.py:402
  53.1 14.4 %collective-permute-start.19 = (f32[10,32,256]{2,1,0:T(8,128)S(1)}, f32[10,32,256]{2,1,0:T(8,128)S(1)}, u32[]{:S(2)}, u32[]{:S(2)}) collective-permute-start(f32[10,32,256]{2,1,0:T(8,128)S(1)} %get-tuple-element.50), channel_id=1, source_target_pairs={{10,2},{8,10},{7,5},{5,13},{26,18},{24,26},{23,21},{21,29}} | collective-permute-start | bytes 983048 | tf_op jit(solution)/shard_map/ppermute | solution.py:364
  53.8 21.5 %collective-permute-start.17 = (f32[10,32,256]{2,1,0:T(8,128)S(1)}, f32[10,32,256]{2,1,0:T(8,128)S(1)}, u32[]{:S(2)}, u32[]{:S(2)}) collective-permute-start(f32[10,32,256]{2,1,0:T(8,128)S(1)} %get-tuple-element.50), channel_id=1, source_target_pairs={{14,2},{12,10},{3,5},{1,13},{30,18},{28,26},{19,21},{17,29}} | collective-permute-start | bytes 983048 | tf_op jit(solution)/shard_map/ppermute | solution.py:364
  63.8 11.6 %collective-permute-start.18 = (f32[10,32,256]{2,1,0:T(8,128)S(1)}, f32[10,32,256]{2,1,0:T(8,128)S(1)}, u32[]{:S(2)}, u32[]{:S(2)}) collective-permute-start(f32[10,32,256]{2,1,0:T(8,128)S(1)} %get-tuple-element.51), channel_id=1, source_target_pairs={{8,2},{10,10},{5,5},{7,13},{24,18},{26,26},{21,21},{23,29}} | collective-permute-start | bytes 983048 | tf_op jit(solution)/shard_map/ppermute | solution.py:364
  64.5 14.4 %collective-permute-start.16 = (f32[10,32,256]{2,1,0:T(8,128)S(1)}, f32[10,32,256]{2,1,0:T(8,128)S(1)}, u32[]{:S(2)}, u32[]{:S(2)}) collective-permute-start(f32[10,32,256]{2,1,0:T(8,128)S(1)} %get-tuple-element.51), channel_id=1, source_target_pairs={{12,2},{14,10},{1,5},{3,13},{28,18},{30,26},{17,21},{19,29}} | collective-permute-start | bytes 983048 | tf_op jit(solution)/shard_map/ppermute | solution.py:364
  79.9 2.0 %collective-permute-start.20 = (f32[520,256]{1,0:T(8,128)S(1)}, f32[520,256]{1,0:T(8,128)S(1)}, u32[]{:S(2)}, u32[]{:S(2)}) collective-permute-start(f32[520,256]{1,0:T(8,128)S(1)} %get-tuple-element.38.refs_1_), channel_id=1, source_target_pairs={{0,8},{8,0},{16,24},{24,16},{1,9},{9,1},{17,25},{25,17},{2,10},{10... | collective-permute-start | bytes 1597448 | tf_op jit(solution)/shard_map/ppermute | solution.py:416
  82.4 3.3 %collective-permute-start.21 = (f32[3,32,256]{2,1,0:T(8,128)S(1)}, f32[3,32,256]{2,1,0:T(8,128)S(1)}, u32[]{:S(2)}, u32[]{:S(2)}) collective-permute-start(f32[3,32,256]{2,1,0:T(8,128)S(1)} %get-tuple-element.42), channel_id=1, source_target_pairs={{2,0},{10,4},{5,8},{13,12},{18,16},{26,20},{21,24},{29,28}} | collective-permute-start | bytes 294920 | tf_op jit(solution)/shard_map/ppermute | solution.py:425
  83.1 2.7 %collective-permute-start.22 = (f32[3,32,256]{2,1,0:T(8,128)S(1)}, f32[3,32,256]{2,1,0:T(8,128)S(1)}, u32[]{:S(2)}, u32[]{:S(2)}) collective-permute-start(f32[3,32,256]{2,1,0:T(8,128)S(1)} %get-tuple-element.43), channel_id=1, source_target_pairs={{2,1},{10,5},{5,9},{13,13},{18,17},{26,21},{21,25},{29,29}} | collective-permute-start | bytes 294920 | tf_op jit(solution)/shard_map/ppermute | solution.py:425
  83.8 2.0 %collective-permute-start.23 = (f32[3,32,256]{2,1,0:T(8,128)S(1)}, f32[3,32,256]{2,1,0:T(8,128)S(1)}, u32[]{:S(2)}, u32[]{:S(2)}) collective-permute-start(f32[3,32,256]{2,1,0:T(8,128)S(1)} %get-tuple-element.44), channel_id=1, source_target_pairs={{2,2},{10,6},{5,10},{13,14},{18,18},{26,22},{21,26},{29,30}} | collective-permute-start | bytes 294920 | tf_op jit(solution)/shard_map/ppermute | solution.py:425
  84.5 19.9 %collective-permute-start.24 = (f32[3,32,256]{2,1,0:T(8,128)S(1)}, f32[3,32,256]{2,1,0:T(8,128)S(1)}, u32[]{:S(2)}, u32[]{:S(2)}) collective-permute-start(f32[3,32,256]{2,1,0:T(8,128)S(1)} %get-tuple-element.45), channel_id=1, source_target_pairs={{2,3},{10,7},{5,11},{13,15},{18,19},{26,23},{21,27},{29,31}} | collective-permute-start | bytes 294920 | tf_op jit(solution)/shard_map/ppermute | solution.py:425
  104.4 3.2 %collective-permute-start.25 = (f32[32,256]{1,0:T(8,128)S(1)}, f32[32,256]{1,0:T(8,128)S(1)}, u32[]{:S(2)}, u32[]{:S(2)}) collective-permute-start(f32[32,256]{1,0:T(8,128)S(1)} %slice_bitcast_fusion.1), channel_id=1, source_target_pairs={{0,8},{8,0},{16,24},{24,16},{1,9},{9,1},{17,25},{25,17},{2,10},{10... | collective-permute-start | bytes 98312 | tf_op jit(solution)/shard_map/ppermute | solution.py:433
  107.6 3.9 %collective-permute-start.26 = (f32[32,256]{1,0:T(8,128)S(1)}, f32[32,256]{1,0:T(8,128)S(1)}, u32[]{:S(2)}, u32[]{:S(2)}) collective-permute-start(f32[32,256]{1,0:T(8,128)S(1)} %fusion.1), channel_id=1, source_target_pairs={{0,16},{8,24},{16,0},{24,8},{1,17},{9,25},{17,1},{25,9},{2,18},{10... | collective-permute-start | bytes 98312 | tf_op jit(solution)/shard_map/ppermute | solution.py:433
  (9 other events, 132.9 us)

commit v3 on v2

--- a/solution.py
+++ b/solution.py
@@ -278,6 +278,10 @@
     return (blocks // 2 - 1) * (piece % 2)
 
 
+def carrier(piece, pair, turn, blocks):
+    return (piece ^ (1 - turn % 2)) * blocks + pair * 2 + piece % 2
+
+
 def gather_pairs(turn, pieces, blocks, moved):
     pairs = []
     for piece in range(pieces):
@@ -285,20 +289,19 @@
             pair, column = block_of(turn, half, piece % 2, blocks)
             source = piece * blocks + pair * 2 + column
             if column != piece % 2 and moved(piece, pair):
-                source = (piece ^ 1) * blocks + pair * 2 + 1 - column
+                source = carrier(piece, pair, turn, blocks)
             target = (piece - piece % 2 + half) * blocks + home_row(piece, blocks)
             pairs.append((source, target))
     return pairs
 
 
-def move_pairs(pieces, blocks, moved):
+def move_pairs(turn, pieces, blocks, moved):
     pairs = []
     for piece in range(pieces):
         for pair in range(blocks // 2):
             if moved(piece, pair):
-                column = piece % 2
-                source = piece * blocks + pair * 2 + 1 - column
-                pairs.append((source, (piece ^ 1) * blocks + pair * 2 + column))
+                source = piece * blocks + pair * 2 + 1 - piece % 2
+                pairs.append((source, carrier(piece, pair, turn, blocks)))
     return pairs
 
 
@@ -346,40 +349,60 @@
         sends = [jnp.concatenate([take(values, i), *more], axis=0) for i in (odd, 1 - odd)]
         return lax.optimization_barrier(sends)
 
-    away = lax.rem(row + half, 2) == 1
-    far_end = row // 2 == (blocks // 2 - 1) * (1 - half)
-
     def ends(piece, pair):
         return pair == detour(piece, blocks)
 
-    def every(piece, pair):
-        return True
+    def remote(piece, pair):
+        return pair != home_row(piece, blocks) // 2
 
     def move(sends, moved):
-        both = jnp.concatenate(sends, axis=0)
-        return jnp.split(lax.ppermute(both, BOTH, move_pairs(pieces, blocks, moved)), 2)
-
-    def gather(sends, turns, moved):
-        return {
-            k: lax.ppermute(sends[k % 2], BOTH, gather_pairs(k, pieces, blocks, moved))
-            for k in turns
-        }
+        return [
+            lax.ppermute(send, BOTH, move_pairs(i, pieces, blocks, moved))
+            for i, send in enumerate(sends)
+        ]
+
+    device = lax.axis_index("cuts") * blocks + row
+
+    def gather(sends, turns, moved, carried=None):
+        got = {}
+        for i in range(2):
+            groups = []
+            for k in [k for k in turns if k % 2 == i]:
+                pairs = gather_pairs(k, pieces, blocks, moved)
+                carry = {t for _, t in move_pairs(k, pieces, blocks, moved)} if carried else set()
+                own = {s for s, _ in gather_pairs(k, pieces, blocks, lambda *_: False)}
+                sources = {s for s, _ in pairs}
+                passed, direct = (sources & carry) - (sources & own), sources & own
+                for group in groups:
+                    if not (group[1] | passed) & (group[2] | direct):
+                        break
+                else:
+                    group = [[], set(), set()]
+                    groups.append(group)
+                group[0].append((k, pairs))
+                group[1] |= passed
+                group[2] |= direct
+            for rounds, passed, _ in groups:
+                send = sends[i]
+                if passed:
+                    here = functools.reduce(lambda x, t: x | (device == t), sorted(passed), False)
+                    send = jnp.where(here, carried[i], send)
+                got |= {k: lax.ppermute(send, BOTH, pairs) for k, pairs in rounds}
+        return got
 
     turns = blocks // 2
     near, far = range(turns), range(turns, blocks)
     late = sorted({turns + 2, turns + 3, blocks - 2, blocks - 1})
     sends = build(maps, upstream, acquisition_choice_odds)
+    first = gather(sends, [k for k in far if k not in late], ends)
     carried = move(sends, ends)
-    first = gather(sends, near, ends)
-    first |= gather(sends, [k for k in far if k not in late], ends)
-    sends = [jnp.where(away & far_end, c, s) for c, s in zip(carried, sends)]
-    first |= gather(sends, late, ends)
+    first |= gather(sends, near, ends)
+    first |= gather(sends, late, ends, carried)
     first = [first[k] for k in range(blocks)]
     sends = build(data, recon)
-    carried = move(sends, every)
-    second = gather(sends, near, every)
-    sends = [jnp.where(away, c, s) for c, s in zip(carried, sends)]
-    second |= gather(sends, far, every)
+    carried = move(sends, remote)
+    second = gather(sends, near, remote)
+    second |= gather(sends, far, remote, carried)
     second = [second[k] for k in range(blocks)]
 
     image, spectrum = shape(2, n, n), shape(2, n, count * n)

time: 113 us -> 137 us (1.21)
  local copies, waits for them, and re-layouts: 2.82 us -> 25 us
  waiting for transfers between devices: 39.9 us -> 46.8 us
  starting transfers between devices: 56.2 us -> 51.9 us
  other arithmetic: 8.35 us -> 5.44 us
  Pallas kernels: 3.06 us -> 4.71 us
    unnamed x29 -> x79, local copies, waits for them, and re-layouts: 0.72 us -> 22.9 us
    ppermute x18 -> x20, waiting for transfers between devices: 16.8 us -> 28 us  [the longest x16 16.1 us: gather(): got |= {k: lax.ppermute(send, BOTH, pairs) for k, pairs in rounds}]
    ppermute x1, starting transfers between devices: 10.4 us -> 2.19 us  [steps(): other1 = lax.ppermute(part1, 'cuts', swap)]
    ppermute x4, waiting for transfers between devices: 18.6 us -> 14.5 us  [steps(): lax.ppermute(outs[k], BOTH, scatter_pairs(k, pieces, blocks))]
    ppermute x2, starting transfers between devices: 3.85 us -> 7.03 us  [steps(): lax.ppermute(term, 'cuts', [(i, i ^ step) for i in range(pieces)])]
    concatenate x2 -> x0, other arithmetic: 2.26 us -> none  [move(): both = jnp.concatenate(sends, axis=0)]
    concatenate x2, other arithmetic: 2.92 us -> 0.96 us  [build(): jnp.concatenate([take(values, i), *more], axis=0)]
    pallas_call x4, Pallas kernels: 3.06 us -> 4.71 us  [run(): return pl.pallas_call(*args, compiler_params=PARAMS, **kwargs)(*operands)]
  transfers between devices with their start and end apart: 27 -> 29, of which waited for: 8 -> 9; matrix products, arithmetic and copies ran while one was open for 6% -> 4% of each run, Pallas kernels for 1% -> 1%
where the time goes in v3:
time: 137 us; the launch traced here: 136 us
  starting transfers between devices  51.9 us (38%)
  waiting for transfers between devices  46.8 us (34%)
  local copies, waits for them, and re-layouts  25 us (18%)
  other arithmetic  5.44 us (4%)
  Pallas kernels  4.71 us (3%)
  between operations  1.87 us (1%)
    ppermute x16, starting transfers between devices, gather(): got |= {k: lax.ppermute(send, BOTH, pairs) for k, pairs in rounds}  34.2 us
    unnamed x79, local copies, waits for them, and re-layouts  22.9 us
    ppermute x16, waiting for transfers between devices, gather(): got |= {k: lax.ppermute(send, BOTH, pairs) for k, pairs in rounds}  16.1 us
    ppermute x4, waiting for transfers between devices, steps(): lax.ppermute(outs[k], BOTH, scatter_pairs(k, pieces, blocks))  14.5 us
    ppermute x4, waiting for transfers between devices, move(): lax.ppermute(send, BOTH, move_pairs(i, pieces, blocks, moved))  11.9 us
    ppermute x2, starting transfers between devices, steps(): lax.ppermute(term, 'cuts', [(i, i ^ step) for i in range(pieces)])  7.03 us
    ppermute x4, starting transfers between devices, move(): lax.ppermute(send, BOTH, move_pairs(i, pieces, blocks, moved))  4.91 us
    pallas_call x4, Pallas kernels, run(): return pl.pallas_call(*args, compiler_params=PARAMS, **kwargs)(*operands)  4.71 us
  transfers between devices with their start and end apart: 29, of which 9 were waited for; matrix products, arithmetic and copies ran while one was open for 4% of the time, Pallas kernels for 1%

profile of v3, /device:TPU:10, one launch (start us, length us, event | category | flops | bytes accessed | tf_op | source)
XLA Modules:
  0.0 135.8 jit_solution(2974885322955524224)
XLA Ops:
  0.7 2.1 %dynamic-slice_bitcast_fusion = (f32[8,32,256]{2,1,0:T(8,128)}, f32[8,32,256]{2,1,0:T(8,128)}, f32[8,32,256]{2,1,0:T(8,128)S(1)}, f32[8,32,256]{2,1,0:T(8,128)S(1)}) fusion(f32[2,8,32,256]{3,2,1,0:T(8,128)} %bitcast.29, s32[]{:T(128)S(6)} %select_n.50, s32[]{:T(128)S(6)} %select_n.49, f32[2,8,32,256]{3,2,1,0:T(8,128)} %bitcast.30), kind=kLoop, calls=%fused_computation.6 | loop fusion | bytes 2097160 | tf_op jit(solution)/shard_map/jit(dynamic_index_in_dim)/squeeze | solution.py:346
  3.8 1.4 %collective-permute-start.8 = (f32[11,32,256]{2,1,0:T(8,128)S(1)}, f32[11,32,256]{2,1,0:T(8,128)}, u32[]{:S(2)}, u32[]{:S(2)}) collective-permute-start(f32[11,32,256]{2,1,0:T(8,128)S(1)} %get-tuple-element.25), channel_id=1, source_target_pairs={{1,0},{14,15},{17,16},{30,31}} | collective-permute-start | bytes 1081352 | tf_op jit(solution)/shard_map/ppermute | solution.py:360
  12.4 11.4 %collective-permute-start.7 = (f32[11,32,256]{2,1,0:T(8,128)}, f32[11,32,256]{2,1,0:T(8,128)S(1)}, u32[]{:S(2)}, u32[]{:S(2)}) collective-permute-start(f32[11,32,256]{2,1,0:T(8,128)} %broadcast_select_fusion.1), channel_id=1, source_target_pairs={{8,2},{3,10},{12,5},{7,13},{24,18},{19,26},{28,21},{23,29}} | collective-permute-start | bytes 1081352 | tf_op jit(solution)/shard_map/ppermute | solution.py:390
  24.6 1.3 collective-permute-start.9
  29.8 3.1 %collective-permute-done.9.refs_9_ = f32[11,32,256]{2,1,0:T(8,128)S(1)} collective-permute-done((f32[11,32,256]{2,1,0:T(8,128)}, f32[11,32,256]{2,1,0:T(8,128)S(1)}, u32[]{:S(2)}, u32[]{:S(2)}) %collective-permute-start.9) | collective-permute-done | bytes 360480 | tf_op jit(solution)/shard_map/ppermute | solution.py:390
  36.5 1.0 copy-done.18
  37.4 1.0 copy-done.20
  38.4 1.0 copy-done.22
  43.4 1.0 copy-done.32
  44.3 1.6 %shard_map.167 = (f32[8,256,256]{2,1,0:T(8,128)S(1)}, f32[2,256,256]{2,1,0:T(8,128)S(1)}, f32[256,256]{1,0:T(8,128)S(1)}, f32[2,256,1024]{2,1,0:T(8,128)S(1)}, f32[2,256,256]{2,1,0:T(8,128)}) custom-call(s32[3]{0:T(128)S(1)} %pad_add_fusion.refs_0_, f32[1]{0:T(128)} %copy.19.refs_1_, f32[11,32,256]{2,1,0:T(8,128)S(1)} %copy-done.22, ...), custom_call_target="tpu_custom_call" | custom-call | tf_op jit(solution)/shard_map/pallas_call | solution.py:257
  45.9 1.3 copy-done
  48.9 1.3 collective-permute-start.16
  50.2 1.4 %collective-permute-start.18 = (f32[10,32,256]{2,1,0:T(8,128)}, f32[10,32,256]{2,1,0:T(8,128)}, u32[]{:S(2)}, u32[]{:S(2)}) collective-permute-start(f32[10,32,256]{2,1,0:T(8,128)} %get-tuple-element.37), channel_id=1, source_target_pairs={{1,0},{5,4},{7,6},{8,9},{10,11},{14,15},{17,16},{21,20},{23,22},{2... | collective-permute-start | bytes 983048 | tf_op jit(solution)/shard_map/ppermute | solution.py:360
  51.6 1.4 %collective-permute-start.14 = (f32[10,32,256]{2,1,0:T(8,128)}, f32[10,32,256]{2,1,0:T(8,128)}, u32[]{:S(2)}, u32[]{:S(2)}) collective-permute-start(f32[10,32,256]{2,1,0:T(8,128)} %get-tuple-element.36), channel_id=1, source_target_pairs={{4,2},{6,10},{13,5},{15,13},{20,18},{22,26},{29,21},{31,29}} | collective-permute-start | bytes 983048 | tf_op jit(solution)/shard_map/ppermute | solution.py:390
  52.9 1.4 %collective-permute-start.12 = (f32[10,32,256]{2,1,0:T(8,128)}, f32[10,32,256]{2,1,0:T(8,128)}, u32[]{:S(2)}, u32[]{:S(2)}) collective-permute-start(f32[10,32,256]{2,1,0:T(8,128)} %get-tuple-element.36), channel_id=1, source_target_pairs={{0,2},{2,10},{9,5},{11,13},{16,18},{18,26},{25,21},{27,29}} | collective-permute-start | bytes 983048 | tf_op jit(solution)/shard_map/ppermute | solution.py:390
  54.3 11.8 %collective-permute-done.16 = f32[10,32,256]{2,1,0:T(8,128)} collective-permute-done((f32[10,32,256]{2,1,0:T(8,128)}, f32[10,32,256]{2,1,0:T(8,128)}, u32[]{:S(2)}, u32[]{:S(2)}) %collective-permute-start.16) | collective-permute-done | bytes 327712 | tf_op jit(solution)/shard_map/ppermute | solution.py:360
  67.6 1.1 broadcast_select_fusion.2
  72.4 1.5 %shard_map.168 = (f32[2,256,256]{2,1,0:T(8,128)S(1)}, f32[2,256,256]{2,1,0:T(8,128)S(1)}, f32[2,8,128]{2,1,0:T(8,128)S(1)}, f32[2,256,1024]{2,1,0:T(8,128)S(1)}, f32[2,256,256]{2,1,0:T(8,128)S(1)}) custom-call(s32[3]{0:T(128)S(1)} %pad_add_fusion.refs_0_, f32[2,256,256]{2,1,0:T(8,128)S(1)} %get-tuple-element.26.refs_1_, ...), custom_call_target="tpu_custom_call" | custom-call | tf_op jit(solution)/shard_map/pallas_call | solution.py:257
  73.9 2.2 %collective-permute-start.11 = (f32[2,256,256]{2,1,0:T(8,128)S(1)}, f32[2,256,256]{2,1,0:T(8,128)S(1)}, u32[]{:S(2)}, u32[]{:S(2)}) collective-permute-start(f32[2,256,256]{2,1,0:T(8,128)S(1)} %get-tuple-element.33.refs_5_), channel_id=1, source_target_pairs={{0,8},{8,0},{16,24},{24,16},{1,9},{9,1},{17,25},{25,17},{2,10},{10... | collective-permute-start | bytes 1572872 | tf_op jit(solution)/shard_map/ppermute | solution.py:425
  76.1 1.0 broadcast_select_fusion.3
  77.1 10.0 %collective-permute-start.20 = (f32[10,32,256]{2,1,0:T(8,128)S(1)}, f32[10,32,256]{2,1,0:T(8,128)S(1)}, u32[]{:S(2)}, u32[]{:S(2)}) collective-permute-start(f32[10,32,256]{2,1,0:T(8,128)S(1)} %get-tuple-element.48), channel_id=1, source_target_pairs={{8,2},{3,10},{12,5},{7,13},{24,18},{19,26},{28,21},{23,29}} | collective-permute-start | bytes 983048 | tf_op jit(solution)/shard_map/ppermute | solution.py:390
  87.1 1.3 collective-permute-start.17
  88.5 1.3 collective-permute-start.21
  90.5 1.2 collective-permute-done.20.refs_17_
  91.7 11.7 %collective-permute-done.17.refs_15_ = f32[10,32,256]{2,1,0:T(8,128)S(1)} collective-permute-done((f32[10,32,256]{2,1,0:T(8,128)S(1)}, f32[10,32,256]{2,1,0:T(8,128)S(1)}, u32[]{:S(2)}, u32[]{:S(2)}) %collective-permute-start.17) | collective-permute-done | bytes 327712 | tf_op jit(solution)/shard_map/ppermute | solution.py:390
  103.4 1.0 shard_map.169
  104.7 1.7 %collective-permute-done.22.refs_2_ = f32[520,256]{1,0:T(8,128)S(1)} collective-permute-done((f32[520,256]{1,0:T(8,128)S(1)}, f32[520,256]{1,0:T(8,128)S(1)}, u32[]{:S(2)}, u32[]{:S(2)}) %collective-permute-start.22) | collective-permute-done | bytes 532512 | tf_op jit(solution)/shard_map/ppermute | solution.py:439
  109.0 1.3 collective-permute-start.26
  110.3 14.5 %collective-permute-done.26 = f32[3,32,256]{2,1,0:T(8,128)S(1)} collective-permute-done((f32[3,32,256]{2,1,0:T(8,128)S(1)}, f32[3,32,256]{2,1,0:T(8,128)S(1)}, u32[]{:S(2)}, u32[]{:S(2)}) %collective-permute-start.26) | collective-permute-done | bytes 98336 | tf_op jit(solution)/shard_map/ppermute | solution.py:448
  124.9 5.5 %collective-permute-start.27 = (f32[32,256]{1,0:T(8,128)S(1)}, f32[32,256]{1,0:T(8,128)S(1)}, u32[]{:S(2)}, u32[]{:S(2)}) collective-permute-start(f32[32,256]{1,0:T(8,128)S(1)} %slice_bitcast_fusion.1), channel_id=1, source_target_pairs={{0,8},{8,0},{16,24},{24,16},{1,9},{9,1},{17,25},{25,17},{2,10},{10... | collective-permute-start | bytes 98312 | tf_op jit(solution)/shard_map/ppermute | solution.py:456
  131.3 1.5 %collective-permute-start.28 = (f32[32,256]{1,0:T(8,128)S(1)}, f32[32,256]{1,0:T(8,128)S(1)}, u32[]{:S(2)}, u32[]{:S(2)}) collective-permute-start(f32[32,256]{1,0:T(8,128)S(1)} %fusion.1), channel_id=1, source_target_pairs={{0,16},{8,24},{16,0},{24,8},{1,17},{9,25},{17,1},{25,9},{2,18},{10... | collective-permute-start | bytes 98312 | tf_op jit(solution)/shard_map/ppermute | solution.py:456
  133.4 1.8 %collective-permute-done.28 = f32[32,256]{1,0:T(8,128)S(1)} collective-permute-done((f32[32,256]{1,0:T(8,128)S(1)}, f32[32,256]{1,0:T(8,128)S(1)}, u32[]{:S(2)}, u32[]{:S(2)}) %collective-permute-start.28) | collective-permute-done | bytes 32800 | tf_op jit(solution)/shard_map/ppermute | solution.py:456
  (121 shorter events, 31.8 us)
Async XLA Ops:
  2.8 30.9 %copy-start.3 = (bf16[256,256]{1,0:T(8,128)(2,1)S(1)}, bf16[256,256]{1,0:T(8,128)(2,1)}, u32[]{:S(2)}) copy-start(bf16[256,256]{1,0:T(8,128)(2,1)} %constant.119.clone.refs_18_.refs_14_.refs_27_) | copy-start | bytes 393220
  2.8 30.9 %copy-start.4 = (bf16[256,256]{1,0:T(8,128)(2,1)S(1)}, bf16[256,256]{1,0:T(8,128)(2,1)}, u32[]{:S(2)}) copy-start(bf16[256,256]{1,0:T(8,128)(2,1)} %constant.118.clone.refs_17_.refs_13_.refs_26_) | copy-start | bytes 393220
  2.9 4.3 %collective-permute-start.6 = (f32[11,32,256]{2,1,0:T(8,128)S(1)}, f32[11,32,256]{2,1,0:T(8,128)S(1)}, u32[]{:S(2)}, u32[]{:S(2)}) collective-permute-start(f32[11,32,256]{2,1,0:T(8,128)S(1)} %get-tuple-element.24), channel_id=1, source_target_pairs={{1,8},{14,7},{17,24},{30,23}} | collective-permute-start | bytes 1081352 | tf_op jit(solution)/shard_map/ppermute | solution.py:360
  3.8 5.0 %collective-permute-start.8 = (f32[11,32,256]{2,1,0:T(8,128)S(1)}, f32[11,32,256]{2,1,0:T(8,128)}, u32[]{:S(2)}, u32[]{:S(2)}) collective-permute-start(f32[11,32,256]{2,1,0:T(8,128)S(1)} %get-tuple-element.25), channel_id=1, source_target_pairs={{1,0},{14,15},{17,16},{30,31}} | collective-permute-start | bytes 1081352 | tf_op jit(solution)/shard_map/ppermute | solution.py:360
  5.2 5.1 %collective-permute-start.4 = (f32[11,32,256]{2,1,0:T(8,128)S(1)}, f32[11,32,256]{2,1,0:T(8,128)S(1)}, u32[]{:S(2)}, u32[]{:S(2)}) collective-permute-start(f32[11,32,256]{2,1,0:T(8,128)S(1)} %get-tuple-element.24), channel_id=1, source_target_pairs={{5,2},{7,10},{8,5},{10,13},{21,18},{23,26},{24,21},{26,29}} | collective-permute-start | bytes 1081352 | tf_op jit(solution)/shard_map/ppermute | solution.py:390
  5.9 5.8 %collective-permute-start.2 = (f32[11,32,256]{2,1,0:T(8,128)S(1)}, f32[11,32,256]{2,1,0:T(8,128)S(1)}, u32[]{:S(2)}, u32[]{:S(2)}) collective-permute-start(f32[11,32,256]{2,1,0:T(8,128)S(1)} %get-tuple-element.24), channel_id=1, source_target_pairs={{4,2},{6,10},{13,5},{15,13},{20,18},{22,26},{29,21},{31,29}} | collective-permute-start | bytes 1081352 | tf_op jit(solution)/shard_map/ppermute | solution.py:390
  6.6 17.3 %collective-permute-start = (f32[11,32,256]{2,1,0:T(8,128)S(1)}, f32[11,32,256]{2,1,0:T(8,128)S(1)}, u32[]{:S(2)}, u32[]{:S(2)}) collective-permute-start(f32[11,32,256]{2,1,0:T(8,128)S(1)} %get-tuple-element.24), channel_id=1, source_target_pairs={{0,2},{2,10},{9,5},{11,13},{16,18},{18,26},{25,21},{27,29}} | collective-permute-start | bytes 1081352 | tf_op jit(solution)/shard_map/ppermute | solution.py:390
  7.3 19.4 %collective-permute-start.5 = (f32[11,32,256]{2,1,0:T(8,128)S(1)}, f32[11,32,256]{2,1,0:T(8,128)S(1)}, u32[]{:S(2)}, u32[]{:S(2)}) collective-permute-start(f32[11,32,256]{2,1,0:T(8,128)S(1)} %get-tuple-element.25), channel_id=1, source_target_pairs={{7,2},{5,10},{10,5},{8,13},{23,18},{21,26},{26,21},{24,29}} | collective-permute-start | bytes 1081352 | tf_op jit(solution)/shard_map/ppermute | solution.py:390
  8.8 18.6 %collective-permute-start.3 = (f32[11,32,256]{2,1,0:T(8,128)S(1)}, f32[11,32,256]{2,1,0:T(8,128)S(1)}, u32[]{:S(2)}, u32[]{:S(2)}) collective-permute-start(f32[11,32,256]{2,1,0:T(8,128)S(1)} %get-tuple-element.25), channel_id=1, source_target_pairs={{6,2},{4,10},{15,5},{13,13},{22,18},{20,26},{31,21},{29,29}} | collective-permute-start | bytes 1081352 | tf_op jit(solution)/shard_map/ppermute | solution.py:390
  11.0 17.2 %collective-permute-start.1 = (f32[11,32,256]{2,1,0:T(8,128)S(1)}, f32[11,32,256]{2,1,0:T(8,128)S(1)}, u32[]{:S(2)}, u32[]{:S(2)}) collective-permute-start(f32[11,32,256]{2,1,0:T(8,128)S(1)} %get-tuple-element.25), channel_id=1, source_target_pairs={{2,2},{0,10},{11,5},{9,13},{18,18},{16,26},{27,21},{25,29}} | collective-permute-start | bytes 1081352 | tf_op jit(solution)/shard_map/ppermute | solution.py:390
  12.4 16.7 %collective-permute-start.7 = (f32[11,32,256]{2,1,0:T(8,128)}, f32[11,32,256]{2,1,0:T(8,128)S(1)}, u32[]{:S(2)}, u32[]{:S(2)}) collective-permute-start(f32[11,32,256]{2,1,0:T(8,128)} %broadcast_select_fusion.1), channel_id=1, source_target_pairs={{8,2},{3,10},{12,5},{7,13},{24,18},{19,26},{28,21},{23,29}} | collective-permute-start | bytes 1081352 | tf_op jit(solution)/shard_map/ppermute | solution.py:390
  24.6 8.3 %collective-permute-start.9 = (f32[11,32,256]{2,1,0:T(8,128)}, f32[11,32,256]{2,1,0:T(8,128)S(1)}, u32[]{:S(2)}, u32[]{:S(2)}) collective-permute-start(f32[11,32,256]{2,1,0:T(8,128)} %broadcast_select_fusion), channel_id=1, source_target_pairs={{3,2},{0,10},{15,5},{12,13},{19,18},{16,26},{31,21},{28,29}} | collective-permute-start | bytes 1081352 | tf_op jit(solution)/shard_map/ppermute | solution.py:390
  48.0 18.9 %collective-permute-start.10 = (f32[2,256,256]{2,1,0:T(8,128)}, f32[2,256,256]{2,1,0:T(8,128)}, u32[]{:S(2)}, u32[]{:S(2)}) collective-permute-start(f32[2,256,256]{2,1,0:T(8,128)} %get-tuple-element.27.refs_2_), channel_id=1, source_target_pairs={{0,8},{8,0},{16,24},{24,16},{1,9},{9,1},{17,25},{25,17},{2,10},{10... | collective-permute-start | bytes 1572872 | tf_op jit(solution)/shard_map/ppermute | solution.py:418
  48.9 17.3 %collective-permute-start.16 = (f32[10,32,256]{2,1,0:T(8,128)}, f32[10,32,256]{2,1,0:T(8,128)}, u32[]{:S(2)}, u32[]{:S(2)}) collective-permute-start(f32[10,32,256]{2,1,0:T(8,128)} %get-tuple-element.36), channel_id=1, source_target_pairs={{1,8},{5,12},{7,14},{8,1},{10,3},{14,7},{17,24},{21,28},{23,30},{2... | collective-permute-start | bytes 983048 | tf_op jit(solution)/shard_map/ppermute | solution.py:360
  50.2 23.8 %collective-permute-start.18 = (f32[10,32,256]{2,1,0:T(8,128)}, f32[10,32,256]{2,1,0:T(8,128)}, u32[]{:S(2)}, u32[]{:S(2)}) collective-permute-start(f32[10,32,256]{2,1,0:T(8,128)} %get-tuple-element.37), channel_id=1, source_target_pairs={{1,0},{5,4},{7,6},{8,9},{10,11},{14,15},{17,16},{21,20},{23,22},{2... | collective-permute-start | bytes 983048 | tf_op jit(solution)/shard_map/ppermute | solution.py:360
  51.6 25.6 %collective-permute-start.14 = (f32[10,32,256]{2,1,0:T(8,128)}, f32[10,32,256]{2,1,0:T(8,128)}, u32[]{:S(2)}, u32[]{:S(2)}) collective-permute-start(f32[10,32,256]{2,1,0:T(8,128)} %get-tuple-element.36), channel_id=1, source_target_pairs={{4,2},{6,10},{13,5},{15,13},{20,18},{22,26},{29,21},{31,29}} | collective-permute-start | bytes 983048 | tf_op jit(solution)/shard_map/ppermute | solution.py:390
  52.9 34.2 %collective-permute-start.12 = (f32[10,32,256]{2,1,0:T(8,128)}, f32[10,32,256]{2,1,0:T(8,128)}, u32[]{:S(2)}, u32[]{:S(2)}) collective-permute-start(f32[10,32,256]{2,1,0:T(8,128)} %get-tuple-element.36), channel_id=1, source_target_pairs={{0,2},{2,10},{9,5},{11,13},{16,18},{18,26},{25,21},{27,29}} | collective-permute-start | bytes 983048 | tf_op jit(solution)/shard_map/ppermute | solution.py:390
  66.2 22.3 %collective-permute-start.15 = (f32[10,32,256]{2,1,0:T(8,128)}, f32[10,32,256]{2,1,0:T(8,128)S(1)}, u32[]{:S(2)}, u32[]{:S(2)}) collective-permute-start(f32[10,32,256]{2,1,0:T(8,128)} %get-tuple-element.37), channel_id=1, source_target_pairs={{6,2},{4,10},{15,5},{13,13},{22,18},{20,26},{31,21},{29,29}} | collective-permute-start | bytes 983048 | tf_op jit(solution)/shard_map/ppermute | solution.py:390
  66.9 22.9 %collective-permute-start.13 = (f32[10,32,256]{2,1,0:T(8,128)}, f32[10,32,256]{2,1,0:T(8,128)S(1)}, u32[]{:S(2)}, u32[]{:S(2)}) collective-permute-start(f32[10,32,256]{2,1,0:T(8,128)} %get-tuple-element.37), channel_id=1, source_target_pairs={{2,2},{0,10},{11,5},{9,13},{18,18},{16,26},{27,21},{25,29}} | collective-permute-start | bytes 983048 | tf_op jit(solution)/shard_map/ppermute | solution.py:390
  72.4 31.0 %copy-start.1 = (f32[2,256,1024]{2,1,0:T(8,128)S(1)}, f32[2,256,1024]{2,1,0:T(8,128)}, u32[]{:S(2)}) copy-start(f32[2,256,1024]{2,1,0:T(8,128)} %copy-done) | copy-start | bytes 6291460
  73.9 29.4 %collective-permute-start.11 = (f32[2,256,256]{2,1,0:T(8,128)S(1)}, f32[2,256,256]{2,1,0:T(8,128)S(1)}, u32[]{:S(2)}, u32[]{:S(2)}) collective-permute-start(f32[2,256,256]{2,1,0:T(8,128)S(1)} %get-tuple-element.33.refs_5_), channel_id=1, source_target_pairs={{0,8},{8,0},{16,24},{24,16},{1,9},{9,1},{17,25},{25,17},{2,10},{10... | collective-permute-start | bytes 1572872 | tf_op jit(solution)/shard_map/ppermute | solution.py:425
  77.1 14.5 %collective-permute-start.20 = (f32[10,32,256]{2,1,0:T(8,128)S(1)}, f32[10,32,256]{2,1,0:T(8,128)S(1)}, u32[]{:S(2)}, u32[]{:S(2)}) collective-permute-start(f32[10,32,256]{2,1,0:T(8,128)S(1)} %get-tuple-element.48), channel_id=1, source_target_pairs={{8,2},{3,10},{12,5},{7,13},{24,18},{19,26},{28,21},{23,29}} | collective-permute-start | bytes 983048 | tf_op jit(solution)/shard_map/ppermute | solution.py:390
  87.1 16.2 %collective-permute-start.17 = (f32[10,32,256]{2,1,0:T(8,128)S(1)}, f32[10,32,256]{2,1,0:T(8,128)S(1)}, u32[]{:S(2)}, u32[]{:S(2)}) collective-permute-start(f32[10,32,256]{2,1,0:T(8,128)S(1)} %get-tuple-element.49), channel_id=1, source_target_pairs={{12,2},{14,10},{1,5},{3,13},{28,18},{30,26},{17,21},{19,29}} | collective-permute-start | bytes 983048 | tf_op jit(solution)/shard_map/ppermute | solution.py:390
  88.5 14.9 %collective-permute-start.21 = (f32[10,32,256]{2,1,0:T(8,128)S(1)}, f32[10,32,256]{2,1,0:T(8,128)S(1)}, u32[]{:S(2)}, u32[]{:S(2)}) collective-permute-start(f32[10,32,256]{2,1,0:T(8,128)S(1)} %broadcast_select_fusion.3), channel_id=1, source_target_pairs={{3,2},{0,10},{15,5},{12,13},{19,18},{16,26},{31,21},{28,29}} | collective-permute-start | bytes 983048 | tf_op jit(solution)/shard_map/ppermute | solution.py:390
  89.8 13.6 %collective-permute-start.19 = (f32[10,32,256]{2,1,0:T(8,128)S(1)}, f32[10,32,256]{2,1,0:T(8,128)S(1)}, u32[]{:S(2)}, u32[]{:S(2)}) collective-permute-start(f32[10,32,256]{2,1,0:T(8,128)S(1)} %broadcast_select_fusion.3), channel_id=1, source_target_pairs={{6,2},{4,10},{11,5},{9,13},{22,18},{20,26},{27,21},{25,29}} | collective-permute-start | bytes 983048 | tf_op jit(solution)/shard_map/ppermute | solution.py:390
  104.4 2.0 %collective-permute-start.22 = (f32[520,256]{1,0:T(8,128)S(1)}, f32[520,256]{1,0:T(8,128)S(1)}, u32[]{:S(2)}, u32[]{:S(2)}) collective-permute-start(f32[520,256]{1,0:T(8,128)S(1)} %get-tuple-element.38.refs_1_), channel_id=1, source_target_pairs={{0,8},{8,0},{16,24},{24,16},{1,9},{9,1},{17,25},{25,17},{2,10},{10... | collective-permute-start | bytes 1597448 | tf_op jit(solution)/shard_map/ppermute | solution.py:439
  107.0 3.3 %collective-permute-start.23 = (f32[3,32,256]{2,1,0:T(8,128)S(1)}, f32[3,32,256]{2,1,0:T(8,128)S(1)}, u32[]{:S(2)}, u32[]{:S(2)}) collective-permute-start(f32[3,32,256]{2,1,0:T(8,128)S(1)} %get-tuple-element.42), channel_id=1, source_target_pairs={{2,0},{10,4},{5,8},{13,12},{18,16},{26,20},{21,24},{29,28}} | collective-permute-start | bytes 294920 | tf_op jit(solution)/shard_map/ppermute | solution.py:448
  107.6 2.7 %collective-permute-start.24 = (f32[3,32,256]{2,1,0:T(8,128)S(1)}, f32[3,32,256]{2,1,0:T(8,128)S(1)}, u32[]{:S(2)}, u32[]{:S(2)}) collective-permute-start(f32[3,32,256]{2,1,0:T(8,128)S(1)} %get-tuple-element.43), channel_id=1, source_target_pairs={{2,1},{10,5},{5,9},{13,13},{18,17},{26,21},{21,25},{29,29}} | collective-permute-start | bytes 294920 | tf_op jit(solution)/shard_map/ppermute | solution.py:448
  108.3 2.0 %collective-permute-start.25 = (f32[3,32,256]{2,1,0:T(8,128)S(1)}, f32[3,32,256]{2,1,0:T(8,128)S(1)}, u32[]{:S(2)}, u32[]{:S(2)}) collective-permute-start(f32[3,32,256]{2,1,0:T(8,128)S(1)} %get-tuple-element.44), channel_id=1, source_target_pairs={{2,2},{10,6},{5,10},{13,14},{18,18},{26,22},{21,26},{29,30}} | collective-permute-start | bytes 294920 | tf_op jit(solution)/shard_map/ppermute | solution.py:448
  109.0 15.9 %collective-permute-start.26 = (f32[3,32,256]{2,1,0:T(8,128)S(1)}, f32[3,32,256]{2,1,0:T(8,128)S(1)}, u32[]{:S(2)}, u32[]{:S(2)}) collective-permute-start(f32[3,32,256]{2,1,0:T(8,128)S(1)} %get-tuple-element.45), channel_id=1, source_target_pairs={{2,3},{10,7},{5,11},{13,15},{18,19},{26,23},{21,27},{29,31}} | collective-permute-start | bytes 294920 | tf_op jit(solution)/shard_map/ppermute | solution.py:448
  124.9 6.4 %collective-permute-start.27 = (f32[32,256]{1,0:T(8,128)S(1)}, f32[32,256]{1,0:T(8,128)S(1)}, u32[]{:S(2)}, u32[]{:S(2)}) collective-permute-start(f32[32,256]{1,0:T(8,128)S(1)} %slice_bitcast_fusion.1), channel_id=1, source_target_pairs={{0,8},{8,0},{16,24},{24,16},{1,9},{9,1},{17,25},{25,17},{2,10},{10... | collective-permute-start | bytes 98312 | tf_op jit(solution)/shard_map/ppermute | solution.py:456
  131.3 3.9 %collective-permute-start.28 = (f32[32,256]{1,0:T(8,128)S(1)}, f32[32,256]{1,0:T(8,128)S(1)}, u32[]{:S(2)}, u32[]{:S(2)}) collective-permute-start(f32[32,256]{1,0:T(8,128)S(1)} %fusion.1), channel_id=1, source_target_pairs={{0,16},{8,24},{16,0},{24,8},{1,17},{9,25},{17,1},{25,9},{2,18},{10... | collective-permute-start | bytes 98312 | tf_op jit(solution)/shard_map/ppermute | solution.py:456
  (36 other events, 222.9 us)

commit v4 on v3

--- a/solution.py
+++ b/solution.py
@@ -111,11 +111,13 @@
     return total(first[0] * second[0] + first[1] * second[1])
 
 
-def normal(real, imag, maps, count, tables, wt, spec_ref, part_ref):
+def normal(real, imag, maps, count, tables, wt, spec, part_ref, keep):
     re, im = forward(real, imag, maps, count, tables)
-    spec_ref[0], spec_ref[1] = re, im
+    spec[0], spec[1] = re, im
+    keep.start()
     wide = jnp.concatenate([wt] * count, axis=1)
     part_ref[0], part_ref[1] = adjoint(re * wide, im * wide, maps, count, tables)
+    keep.wait()
 
 
 def block_of(turn, half, column, blocks):
@@ -144,8 +146,9 @@
 
 def first_kernel(blocks, planes, info, steep_ref, *refs):
     messages, refs = refs[:blocks], refs[blocks:]
-    tables, refs = refs[:10], refs[10:]
-    maps, image, wt_ref, spec_ref, part_ref, odds, sems = refs
+    table_ref, maps, image, wt_ref, spec_ref, part_ref, odds, tables, spec, sems = refs
+    keep = pltpu.make_async_copy(spec, spec_ref, sems.at[3, 1])
+    load = pltpu.make_async_copy(table_ref, tables, sems.at[3, 0])
     extent = messages[0].shape[1]
     copies = []
     for k, msg in enumerate(messages):
@@ -155,18 +158,20 @@
             pltpu.make_async_copy(msg.at[pl.ds(planes, 2)], image.at[:, rows], sems.at[1, k]),
             pltpu.make_async_copy(msg.at[planes + 2], odds.at[rows], sems.at[2, k]),
         ]
-    for copy in copies:
+    for copy in (*copies, load):
         copy.start()
-    for copy in copies:
+    for copy in (*copies, load):
         copy.wait()
     wt = jax.nn.sigmoid(steep_ref[0] * odds[...]).T
     wt_ref[...] = wt
-    normal(image[0], image[1], maps, planes // 2, tables, wt, spec_ref, part_ref)
-
-
-def second_kernel(info, image, part, other, maps, wt_ref, *refs):
-    tables, refs = refs[:10], refs[10:]
-    residual_ref, dir_ref, sc_ref, spec_ref, part_ref = refs
+    normal(image[0], image[1], maps, planes // 2, tables, wt, spec, part_ref, keep)
+
+
+def second_kernel(info, image, part, other, maps, wt_ref, table_ref, *refs):
+    residual_ref, dir_ref, sc_ref, spec_ref, part_ref, tables, spec, sems = refs
+    load = pltpu.make_async_copy(table_ref, tables, sems.at[0])
+    keep = pltpu.make_async_copy(spec, spec_ref, sems.at[1])
+    load.start()
     u = (image[0], image[1])
     q = tuple(part[i] + other[i] + DAMPING * u[i] for i in range(2))
     norm = inner(u, u)
@@ -179,14 +184,16 @@
         dir_ref[i] = p[i]
     sc_ref[0] = jnp.broadcast_to(alpha, sc_ref.shape[1:])
     sc_ref[1] = jnp.broadcast_to(norm_next, sc_ref.shape[1:])
-    normal(p[0], p[1], maps, maps.shape[0] // 2, tables, wt_ref[...], spec_ref, part_ref)
+    load.wait()
+    normal(p[0], p[1], maps, maps.shape[0] // 2, tables, wt_ref[...], spec, part_ref, keep)
 
 
 def third_kernel(blocks, planes, info, image, res_ref, dir_ref, sc_in, part, other, maps,
                  wt_ref, spec0_ref, spec1_ref, *refs):
     messages, refs = refs[:blocks], refs[blocks:]
-    tables, refs = refs[:10], refs[10:]
-    sol_ref, p_ref, sc_ref, out_ref, data, recon, spec0, spec1, sems = refs
+    table_ref, sol_ref, p_ref, sc_ref, out_ref, data, recon, spec0, spec1, tables, sems = refs
+    load = pltpu.make_async_copy(table_ref, tables, sems.at[2, 2])
+    load.start()
     extent = messages[0].shape[1]
     copies = []
     for k, msg in enumerate(messages):
@@ -213,6 +220,7 @@
         sol_ref[i] = alpha0 * image[i] + alpha1 * p[i]
     p = tuple(r[i] + (norm_next / norm) * p[i] for i in range(2))
     p_ref[0], p_ref[1] = p
+    load.wait()
     re, im = forward(p[0], p[1], maps, count, tables)
     wide = jnp.concatenate([wt_ref[...]] * count, axis=1)
     energy = total(wide * (re * re + im * im))
@@ -261,8 +269,12 @@
 
 VMEM = pl.BlockSpec(memory_space=pltpu.VMEM)
 SMEM = pl.BlockSpec(memory_space=pltpu.SMEM)
-ANY = pl.BlockSpec(memory_space=pl.ANY)
-PARAMS = pltpu.CompilerParams(vmem_limit_bytes=24 << 20)
+HBM = pl.BlockSpec(memory_space=pltpu.HBM)
+PARAMS = pltpu.CompilerParams(vmem_limit_bytes=20 << 20)
+
+
+def in_hbm(values):
+    return pltpu.with_memory_space_constraint(values, pltpu.HBM)
 
 
 def shape(*dims):
@@ -336,7 +348,9 @@
     coils = receiver_profile_maps.shape[1]
     planes = coils
     count = coils // 2
-    tables = [jnp.asarray(t) for t in dft_tables(n)]
+    tables = jnp.asarray(np.stack(dft_tables(n)))
+    table_space = pltpu.VMEM(tables.shape, BF16)
+    spec_space = pltpu.VMEM((2, n, count * n), F32)
     swap = [(i, i ^ 1) for i in range(pieces)]
 
     maps = receiver_profile_maps.reshape(2, planes, extent, n)
@@ -398,44 +412,53 @@
     carried = move(sends, ends)
     first |= gather(sends, near, ends)
     first |= gather(sends, late, ends, carried)
-    first = [first[k] for k in range(blocks)]
+    first = [in_hbm(first[k]) for k in range(blocks)]
     sends = build(data, recon)
     carried = move(sends, remote)
     second = gather(sends, near, remote)
     second |= gather(sends, far, remote, carried)
-    second = [second[k] for k in range(blocks)]
+    second = [in_hbm(second[k]) for k in range(blocks)]
 
     image, spectrum = shape(2, n, n), shape(2, n, count * n)
     scalars = shape(2, 8, 128)
     stacked = shape(planes, n, n)
     maps_full, u, wt, spec0, part0 = call(
         at_home(functools.partial(first_kernel, blocks, planes)),
-        in_specs=[SMEM, SMEM] + [ANY] * blocks + [VMEM] * 10,
-        out_specs=[VMEM] * 5,
+        in_specs=[SMEM, SMEM] + [HBM] * (blocks + 1),
+        out_specs=[VMEM] * 3 + [HBM] + [VMEM],
         out_shape=[stacked, image, shape(n, n), spectrum, image],
-        scratch_shapes=[pltpu.VMEM((n, n), F32), pltpu.SemaphoreType.DMA((3, blocks))],
-    )(info, sigmoid_steepness, *first, *tables)
+        scratch_shapes=[
+            pltpu.VMEM((n, n), F32),
+            table_space,
+            spec_space,
+            pltpu.SemaphoreType.DMA((4, blocks)),
+        ],
+    )(info, sigmoid_steepness, *first, tables)
+    u, wt, spec0 = in_hbm(u), in_hbm(wt), in_hbm(spec0)
     other0 = lax.ppermute(part0, "cuts", swap)
     res1, dir1, sc1, spec1, part1 = call(
         at_home(second_kernel),
-        in_specs=[SMEM] + [VMEM] * 15,
-        out_specs=[VMEM] * 5,
+        in_specs=[SMEM] + [VMEM] * 5 + [HBM],
+        out_specs=[VMEM] * 3 + [HBM] + [VMEM],
         out_shape=[image, image, scalars, spectrum, image],
-    )(info, u, part0, other0, maps_full, wt, *tables)
+        scratch_shapes=[table_space, spec_space, pltpu.SemaphoreType.DMA((2,))],
+    )(info, u, part0, other0, maps_full, wt, tables)
+    spec1 = in_hbm(spec1)
     other1 = lax.ppermute(part1, "cuts", swap)
     sol2, dir2, sc2, mine = call(
         at_home(functools.partial(third_kernel, blocks, planes)),
-        in_specs=[SMEM] + [VMEM] * 8 + [ANY] * 2 + [ANY] * blocks + [VMEM] * 10,
+        in_specs=[SMEM] + [VMEM] * 8 + [HBM] * (blocks + 3),
         out_specs=[VMEM] * 4,
         out_shape=[image, image, scalars, shape(2 * n + 8, n)],
         scratch_shapes=[
             pltpu.VMEM((planes, n, n), F32),
             pltpu.VMEM((2, n, n), F32),
-            pltpu.VMEM((2, n, count * n), F32),
-            pltpu.VMEM((2, n, count * n), F32),
+            spec_space,
+            spec_space,
+            table_space,
             pltpu.SemaphoreType.DMA((3, blocks)),
         ],
-    )(info, u, res1, dir1, sc1, part1, other1, maps_full, wt, spec0, spec1, *second, *tables)
+    )(info, u, res1, dir1, sc1, part1, other1, maps_full, wt, spec0, spec1, *second, tables)
     other = lax.ppermute(mine, "cuts", swap)
     outs = call(
         at_home(fourth_kernel),

time: 137 us -> 125 us (0.912)
  local copies, waits for them, and re-layouts: 25 us -> 7.89 us
  waiting for transfers between devices: 46.8 us -> 49.6 us
  starting transfers between devices: 51.9 us -> 54.1 us
    unnamed x79 -> x39, local copies, waits for them, and re-layouts: 22.9 us -> 5.79 us
    ppermute x16, waiting for transfers between devices: 16.1 us -> 19.4 us  [gather(): got |= {k: lax.ppermute(send, BOTH, pairs) for k, pairs in rounds}]
where the time goes in v4:
time: 125 us; the launch traced here: 124 us
  starting transfers between devices  54.1 us (43%)
  waiting for transfers between devices  49.6 us (40%)
  local copies, waits for them, and re-layouts  7.89 us (6%)
  other arithmetic  5.48 us (4%)
  Pallas kernels  5.39 us (4%)
  between operations  1.75 us (1%)
    ppermute x16, starting transfers between devices, gather(): got |= {k: lax.ppermute(send, BOTH, pairs) for k, pairs in rounds}  35.5 us
    ppermute x16, waiting for transfers between devices, gather(): got |= {k: lax.ppermute(send, BOTH, pairs) for k, pairs in rounds}  19.4 us
    ppermute x4, waiting for transfers between devices, steps(): lax.ppermute(outs[k], BOTH, scatter_pairs(k, pieces, blocks))  13.8 us
    ppermute x4, waiting for transfers between devices, move(): lax.ppermute(send, BOTH, move_pairs(i, pieces, blocks, moved))  12.2 us
    ppermute x2, starting transfers between devices, steps(): lax.ppermute(term, 'cuts', [(i, i ^ step) for i in range(pieces)])  7.16 us
    unnamed x39, local copies, waits for them, and re-layouts  5.79 us
    pallas_call x4, Pallas kernels, run(): return pl.pallas_call(*args, compiler_params=PARAMS, **kwargs)(*operands)  5.39 us
    ppermute x4, starting transfers between devices, move(): lax.ppermute(send, BOTH, move_pairs(i, pieces, blocks, moved))  4.92 us
  transfers between devices with their start and end apart: 29, of which 9 were waited for; matrix products, arithmetic and copies ran while one was open for 4% of the time, Pallas kernels for 1%

profile of v4, /device:TPU:10, one launch (start us, length us, event | category | flops | bytes accessed | tf_op | source)
XLA Modules:
  0.0 124.2 jit_solution(441844723519765274)
XLA Ops:
  0.7 2.1 %dynamic-slice_bitcast_fusion = (f32[8,32,256]{2,1,0:T(8,128)}, f32[8,32,256]{2,1,0:T(8,128)}, f32[8,32,256]{2,1,0:T(8,128)S(1)}, f32[8,32,256]{2,1,0:T(8,128)S(1)}) fusion(f32[2,8,32,256]{3,2,1,0:T(8,128)} %bitcast.29, s32[]{:T(128)S(6)} %select_n.50, s32[]{:T(128)S(6)} %select_n.49, f32[2,8,32,256]{3,2,1,0:T(8,128)} %bitcast.30), kind=kLoop, calls=%fused_computation.6 | loop fusion | bytes 2097160 | tf_op jit(solution)/shard_map/jit(dynamic_index_in_dim)/squeeze | solution.py:360
  2.9 1.6 %collective-permute-start.6 = (f32[11,32,256]{2,1,0:T(8,128)S(1)}, f32[11,32,256]{2,1,0:T(8,128)}, u32[]{:S(2)}, u32[]{:S(2)}) collective-permute-start(f32[11,32,256]{2,1,0:T(8,128)S(1)} %get-tuple-element.24), channel_id=1, source_target_pairs={{1,8},{14,7},{17,24},{30,23}} | collective-permute-start | bytes 1081352 | tf_op jit(solution)/shard_map/ppermute | solution.py:374
  7.2 1.4 %collective-permute-start.5 = (f32[11,32,256]{2,1,0:T(8,128)S(1)}, f32[11,32,256]{2,1,0:T(8,128)}, u32[]{:S(2)}, u32[]{:S(2)}) collective-permute-start(f32[11,32,256]{2,1,0:T(8,128)S(1)} %get-tuple-element.25), channel_id=1, source_target_pairs={{7,2},{5,10},{10,5},{8,13},{23,18},{21,26},{26,21},{24,29}} | collective-permute-start | bytes 1081352 | tf_op jit(solution)/shard_map/ppermute | solution.py:404
  9.4 1.4 %collective-permute-start.3 = (f32[11,32,256]{2,1,0:T(8,128)S(1)}, f32[11,32,256]{2,1,0:T(8,128)}, u32[]{:S(2)}, u32[]{:S(2)}) collective-permute-start(f32[11,32,256]{2,1,0:T(8,128)S(1)} %get-tuple-element.25), channel_id=1, source_target_pairs={{6,2},{4,10},{15,5},{13,13},{22,18},{20,26},{31,21},{29,29}} | collective-permute-start | bytes 1081352 | tf_op jit(solution)/shard_map/ppermute | solution.py:404
  11.7 1.4 %collective-permute-start.1 = (f32[11,32,256]{2,1,0:T(8,128)S(1)}, f32[11,32,256]{2,1,0:T(8,128)}, u32[]{:S(2)}, u32[]{:S(2)}) collective-permute-start(f32[11,32,256]{2,1,0:T(8,128)S(1)} %get-tuple-element.25), channel_id=1, source_target_pairs={{2,2},{0,10},{11,5},{9,13},{18,18},{16,26},{27,21},{25,29}} | collective-permute-start | bytes 1081352 | tf_op jit(solution)/shard_map/ppermute | solution.py:404
  13.1 9.5 %collective-permute-start.7 = (f32[11,32,256]{2,1,0:T(8,128)}, f32[11,32,256]{2,1,0:T(8,128)}, u32[]{:S(2)}, u32[]{:S(2)}) collective-permute-start(f32[11,32,256]{2,1,0:T(8,128)} %broadcast_select_fusion.1), channel_id=1, source_target_pairs={{8,2},{3,10},{12,5},{7,13},{24,18},{19,26},{28,21},{23,29}} | collective-permute-start | bytes 1081352 | tf_op jit(solution)/shard_map/ppermute | solution.py:404
  22.6 2.5 %collective-permute-start.9 = (f32[11,32,256]{2,1,0:T(8,128)}, f32[11,32,256]{2,1,0:T(8,128)}, u32[]{:S(2)}, u32[]{:S(2)}) collective-permute-start(f32[11,32,256]{2,1,0:T(8,128)} %broadcast_select_fusion), channel_id=1, source_target_pairs={{3,2},{0,10},{15,5},{12,13},{19,18},{16,26},{31,21},{28,29}} | collective-permute-start | bytes 1081352 | tf_op jit(solution)/shard_map/ppermute | solution.py:404
  25.8 3.1 %collective-permute-done.7.refs_8_ = f32[11,32,256]{2,1,0:T(8,128)} collective-permute-done((f32[11,32,256]{2,1,0:T(8,128)}, f32[11,32,256]{2,1,0:T(8,128)}, u32[]{:S(2)}, u32[]{:S(2)}) %collective-permute-start.7) | collective-permute-done | bytes 360480 | tf_op jit(solution)/shard_map/ppermute | solution.py:404
  28.9 3.9 %collective-permute-done.9.refs_9_ = f32[11,32,256]{2,1,0:T(8,128)} collective-permute-done((f32[11,32,256]{2,1,0:T(8,128)}, f32[11,32,256]{2,1,0:T(8,128)}, u32[]{:S(2)}, u32[]{:S(2)}) %collective-permute-start.9) | collective-permute-done | bytes 360480 | tf_op jit(solution)/shard_map/ppermute | solution.py:404
  32.8 1.6 %shard_map.86 = (f32[8,256,256]{2,1,0:T(8,128)S(1)}, f32[2,256,256]{2,1,0:T(8,128)S(1)}, f32[256,256]{1,0:T(8,128)S(1)}, f32[2,256,1024]{2,1,0:T(8,128)S(1)}, f32[2,256,256]{2,1,0:T(8,128)}) custom-call(s32[3]{0:T(128)S(1)} %pad_add_fusion.refs_0_, f32[1]{0:T(128)} %copy.10.refs_1_, f32[11,32,256]{2,1,0:T(8,128)} %copy-done.9, ...), custom_call_target="tpu_custom_call" | custom-call | tf_op jit(solution)/shard_map/pallas_call | solution.py:265
  34.4 1.3 %copy-done.1 = f32[2,256,1024]{2,1,0:T(8,128)} copy-done((f32[2,256,1024]{2,1,0:T(8,128)}, f32[2,256,1024]{2,1,0:T(8,128)S(1)}, u32[]{:S(2)}) %copy-start.1) | copy-done | bytes 2097176
  38.2 1.3 %collective-permute-start.16 = (f32[10,32,256]{2,1,0:T(8,128)}, f32[10,32,256]{2,1,0:T(8,128)}, u32[]{:S(2)}, u32[]{:S(2)}) collective-permute-start(f32[10,32,256]{2,1,0:T(8,128)} %get-tuple-element.36), channel_id=1, source_target_pairs={{1,8},{5,12},{7,14},{8,1},{10,3},{14,7},{17,24},{21,28},{23,30},{2... | collective-permute-start | bytes 983048 | tf_op jit(solution)/shard_map/ppermute | solution.py:374
  39.5 1.4 %collective-permute-start.18 = (f32[10,32,256]{2,1,0:T(8,128)}, f32[10,32,256]{2,1,0:T(8,128)}, u32[]{:S(2)}, u32[]{:S(2)}) collective-permute-start(f32[10,32,256]{2,1,0:T(8,128)} %get-tuple-element.37), channel_id=1, source_target_pairs={{1,0},{5,4},{7,6},{8,9},{10,11},{14,15},{17,16},{21,20},{23,22},{2... | collective-permute-start | bytes 983048 | tf_op jit(solution)/shard_map/ppermute | solution.py:374
  40.9 1.4 %collective-permute-start.14 = (f32[10,32,256]{2,1,0:T(8,128)}, f32[10,32,256]{2,1,0:T(8,128)}, u32[]{:S(2)}, u32[]{:S(2)}) collective-permute-start(f32[10,32,256]{2,1,0:T(8,128)} %get-tuple-element.36), channel_id=1, source_target_pairs={{4,2},{6,10},{13,5},{15,13},{20,18},{22,26},{29,21},{31,29}} | collective-permute-start | bytes 983048 | tf_op jit(solution)/shard_map/ppermute | solution.py:404
  42.3 1.4 %collective-permute-start.12 = (f32[10,32,256]{2,1,0:T(8,128)}, f32[10,32,256]{2,1,0:T(8,128)}, u32[]{:S(2)}, u32[]{:S(2)}) collective-permute-start(f32[10,32,256]{2,1,0:T(8,128)} %get-tuple-element.36), channel_id=1, source_target_pairs={{0,2},{2,10},{9,5},{11,13},{16,18},{18,26},{25,21},{27,29}} | collective-permute-start | bytes 983048 | tf_op jit(solution)/shard_map/ppermute | solution.py:404
  43.7 12.1 %collective-permute-done.16 = f32[10,32,256]{2,1,0:T(8,128)} collective-permute-done((f32[10,32,256]{2,1,0:T(8,128)}, f32[10,32,256]{2,1,0:T(8,128)}, u32[]{:S(2)}, u32[]{:S(2)}) %collective-permute-start.16) | collective-permute-done | bytes 327712 | tf_op jit(solution)/shard_map/ppermute | solution.py:374
  57.2 1.1 broadcast_select_fusion.2
  58.4 1.6 %shard_map.87 = (f32[2,256,256]{2,1,0:T(8,128)S(1)}, f32[2,256,256]{2,1,0:T(8,128)S(1)}, f32[2,8,128]{2,1,0:T(8,128)S(1)}, f32[2,256,1024]{2,1,0:T(8,128)S(1)}, f32[2,256,256]{2,1,0:T(8,128)S(1)}) custom-call(s32[3]{0:T(128)S(1)} %pad_add_fusion.refs_0_, f32[2,256,256]{2,1,0:T(8,128)} %copy-done.3, f32[2,256,256]{2,1,0:T(8,128)} %get-tuple-element.27.refs_2_, ...), custom_call_target="tpu_custom_call" | custom-call | tf_op jit(solution)/shard_map/pallas_call | solution.py:265
  60.0 1.3 %copy-done.2 = f32[2,256,1024]{2,1,0:T(8,128)} copy-done((f32[2,256,1024]{2,1,0:T(8,128)}, f32[2,256,1024]{2,1,0:T(8,128)S(1)}, u32[]{:S(2)}) %copy-start.2) | copy-done | bytes 2097176
  61.4 2.7 %collective-permute-start.11 = (f32[2,256,256]{2,1,0:T(8,128)S(1)}, f32[2,256,256]{2,1,0:T(8,128)S(1)}, u32[]{:S(2)}, u32[]{:S(2)}) collective-permute-start(f32[2,256,256]{2,1,0:T(8,128)S(1)} %get-tuple-element.33.refs_5_), channel_id=1, source_target_pairs={{0,8},{8,0},{16,24},{24,16},{1,9},{9,1},{17,25},{25,17},{2,10},{10... | collective-permute-start | bytes 1572872 | tf_op jit(solution)/shard_map/ppermute | solution.py:447
  65.1 9.8 %collective-permute-start.20 = (f32[10,32,256]{2,1,0:T(8,128)S(1)}, f32[10,32,256]{2,1,0:T(8,128)S(1)}, u32[]{:S(2)}, u32[]{:S(2)}) collective-permute-start(f32[10,32,256]{2,1,0:T(8,128)S(1)} %get-tuple-element.48), channel_id=1, source_target_pairs={{8,2},{3,10},{12,5},{7,13},{24,18},{19,26},{28,21},{23,29}} | collective-permute-start | bytes 983048 | tf_op jit(solution)/shard_map/ppermute | solution.py:404
  74.9 1.3 %collective-permute-start.17 = (f32[10,32,256]{2,1,0:T(8,128)S(1)}, f32[10,32,256]{2,1,0:T(8,128)S(1)}, u32[]{:S(2)}, u32[]{:S(2)}) collective-permute-start(f32[10,32,256]{2,1,0:T(8,128)S(1)} %get-tuple-element.49), channel_id=1, source_target_pairs={{12,2},{14,10},{1,5},{3,13},{28,18},{30,26},{17,21},{19,29}} | collective-permute-start | bytes 983048 | tf_op jit(solution)/shard_map/ppermute | solution.py:404
  76.3 1.3 %collective-permute-start.21 = (f32[10,32,256]{2,1,0:T(8,128)S(1)}, f32[10,32,256]{2,1,0:T(8,128)S(1)}, u32[]{:S(2)}, u32[]{:S(2)}) collective-permute-start(f32[10,32,256]{2,1,0:T(8,128)S(1)} %broadcast_select_fusion.3), channel_id=1, source_target_pairs={{3,2},{0,10},{15,5},{12,13},{19,18},{16,26},{31,21},{28,29}} | collective-permute-start | bytes 983048 | tf_op jit(solution)/shard_map/ppermute | solution.py:404
  78.3 1.2 collective-permute-done.20.refs_17_
  79.5 11.3 %collective-permute-done.17.refs_15_ = f32[10,32,256]{2,1,0:T(8,128)S(1)} collective-permute-done((f32[10,32,256]{2,1,0:T(8,128)S(1)}, f32[10,32,256]{2,1,0:T(8,128)S(1)}, u32[]{:S(2)}, u32[]{:S(2)}) %collective-permute-start.17) | collective-permute-done | bytes 327712 | tf_op jit(solution)/shard_map/ppermute | solution.py:404
  91.7 1.6 %shard_map.88 = (f32[2,256,256]{2,1,0:T(8,128)S(1)}, f32[2,256,256]{2,1,0:T(8,128)S(1)}, f32[2,8,128]{2,1,0:T(8,128)S(1)}, f32[520,256]{1,0:T(8,128)S(1)}) custom-call(s32[3]{0:T(128)S(1)} %pad_add_fusion.refs_0_, f32[2,256,256]{2,1,0:T(8,128)} %copy-done.3, f32[2,256,256]{2,1,0:T(8,128)S(1)} %get-tuple-element.30.refs_2_, ...), custom_call_target="tpu_custom_call" | custom-call | tf_op jit(solution)/shard_map/pallas_call | solution.py:265
  93.8 1.5 %collective-permute-done.22.refs_2_ = f32[520,256]{1,0:T(8,128)S(1)} collective-permute-done((f32[520,256]{1,0:T(8,128)S(1)}, f32[520,256]{1,0:T(8,128)S(1)}, u32[]{:S(2)}, u32[]{:S(2)}) %collective-permute-start.22) | collective-permute-done | bytes 532512 | tf_op jit(solution)/shard_map/ppermute | solution.py:462
  98.0 1.3 %collective-permute-start.26 = (f32[3,32,256]{2,1,0:T(8,128)S(1)}, f32[3,32,256]{2,1,0:T(8,128)S(1)}, u32[]{:S(2)}, u32[]{:S(2)}) collective-permute-start(f32[3,32,256]{2,1,0:T(8,128)S(1)} %get-tuple-element.45), channel_id=1, source_target_pairs={{2,3},{10,7},{5,11},{13,15},{18,19},{26,23},{21,27},{29,31}} | collective-permute-start | bytes 294920 | tf_op jit(solution)/shard_map/ppermute | solution.py:471
  99.3 13.8 %collective-permute-done.26 = f32[3,32,256]{2,1,0:T(8,128)S(1)} collective-permute-done((f32[3,32,256]{2,1,0:T(8,128)S(1)}, f32[3,32,256]{2,1,0:T(8,128)S(1)}, u32[]{:S(2)}, u32[]{:S(2)}) %collective-permute-start.26) | collective-permute-done | bytes 98336 | tf_op jit(solution)/shard_map/ppermute | solution.py:471
  113.2 5.6 %collective-permute-start.27 = (f32[32,256]{1,0:T(8,128)S(1)}, f32[32,256]{1,0:T(8,128)S(1)}, u32[]{:S(2)}, u32[]{:S(2)}) collective-permute-start(f32[32,256]{1,0:T(8,128)S(1)} %slice_bitcast_fusion.1), channel_id=1, source_target_pairs={{0,8},{8,0},{16,24},{24,16},{1,9},{9,1},{17,25},{25,17},{2,10},{10... | collective-permute-start | bytes 98312 | tf_op jit(solution)/shard_map/ppermute | solution.py:479
  119.7 1.5 %collective-permute-start.28 = (f32[32,256]{1,0:T(8,128)S(1)}, f32[32,256]{1,0:T(8,128)S(1)}, u32[]{:S(2)}, u32[]{:S(2)}) collective-permute-start(f32[32,256]{1,0:T(8,128)S(1)} %fusion.1), channel_id=1, source_target_pairs={{0,16},{8,24},{16,0},{24,8},{1,17},{9,25},{17,1},{25,9},{2,18},{10... | collective-permute-start | bytes 98312 | tf_op jit(solution)/shard_map/ppermute | solution.py:479
  121.8 1.8 %collective-permute-done.28 = f32[32,256]{1,0:T(8,128)S(1)} collective-permute-done((f32[32,256]{1,0:T(8,128)S(1)}, f32[32,256]{1,0:T(8,128)S(1)}, u32[]{:S(2)}, u32[]{:S(2)}) %collective-permute-start.28) | collective-permute-done | bytes 32800 | tf_op jit(solution)/shard_map/ppermute | solution.py:479
  (81 shorter events, 16.2 us)
Async XLA Ops:
  2.8 30.0 %copy-start = (bf16[10,256,256]{2,1,0:T(8,128)(2,1)S(1)}, bf16[10,256,256]{2,1,0:T(8,128)(2,1)}, u32[]{:S(2)}) copy-start(bf16[10,256,256]{2,1,0:T(8,128)(2,1)} %constant.93.clone.refs_10_.refs_6_.refs_19_) | copy-start | bytes 3932164
  2.9 4.4 %collective-permute-start.6 = (f32[11,32,256]{2,1,0:T(8,128)S(1)}, f32[11,32,256]{2,1,0:T(8,128)}, u32[]{:S(2)}, u32[]{:S(2)}) collective-permute-start(f32[11,32,256]{2,1,0:T(8,128)S(1)} %get-tuple-element.24), channel_id=1, source_target_pairs={{1,8},{14,7},{17,24},{30,23}} | collective-permute-start | bytes 1081352 | tf_op jit(solution)/shard_map/ppermute | solution.py:374
  4.4 5.0 %collective-permute-start.8 = (f32[11,32,256]{2,1,0:T(8,128)S(1)}, f32[11,32,256]{2,1,0:T(8,128)S(1)}, u32[]{:S(2)}, u32[]{:S(2)}) collective-permute-start(f32[11,32,256]{2,1,0:T(8,128)S(1)} %get-tuple-element.25), channel_id=1, source_target_pairs={{1,0},{14,15},{17,16},{30,31}} | collective-permute-start | bytes 1081352 | tf_op jit(solution)/shard_map/ppermute | solution.py:374
  5.1 6.6 %collective-permute-start.4 = (f32[11,32,256]{2,1,0:T(8,128)S(1)}, f32[11,32,256]{2,1,0:T(8,128)S(1)}, u32[]{:S(2)}, u32[]{:S(2)}) collective-permute-start(f32[11,32,256]{2,1,0:T(8,128)S(1)} %get-tuple-element.24), channel_id=1, source_target_pairs={{5,2},{7,10},{8,5},{10,13},{21,18},{23,26},{24,21},{26,29}} | collective-permute-start | bytes 1081352 | tf_op jit(solution)/shard_map/ppermute | solution.py:404
  5.8 7.3 %collective-permute-start.2 = (f32[11,32,256]{2,1,0:T(8,128)S(1)}, f32[11,32,256]{2,1,0:T(8,128)S(1)}, u32[]{:S(2)}, u32[]{:S(2)}) collective-permute-start(f32[11,32,256]{2,1,0:T(8,128)S(1)} %get-tuple-element.24), channel_id=1, source_target_pairs={{4,2},{6,10},{13,5},{15,13},{20,18},{22,26},{29,21},{31,29}} | collective-permute-start | bytes 1081352 | tf_op jit(solution)/shard_map/ppermute | solution.py:404
  6.5 16.1 %collective-permute-start = (f32[11,32,256]{2,1,0:T(8,128)S(1)}, f32[11,32,256]{2,1,0:T(8,128)S(1)}, u32[]{:S(2)}, u32[]{:S(2)}) collective-permute-start(f32[11,32,256]{2,1,0:T(8,128)S(1)} %get-tuple-element.24), channel_id=1, source_target_pairs={{0,2},{2,10},{9,5},{11,13},{16,18},{18,26},{25,21},{27,29}} | collective-permute-start | bytes 1081352 | tf_op jit(solution)/shard_map/ppermute | solution.py:404
  7.2 18.6 %collective-permute-start.5 = (f32[11,32,256]{2,1,0:T(8,128)S(1)}, f32[11,32,256]{2,1,0:T(8,128)}, u32[]{:S(2)}, u32[]{:S(2)}) collective-permute-start(f32[11,32,256]{2,1,0:T(8,128)S(1)} %get-tuple-element.25), channel_id=1, source_target_pairs={{7,2},{5,10},{10,5},{8,13},{23,18},{21,26},{26,21},{24,29}} | collective-permute-start | bytes 1081352 | tf_op jit(solution)/shard_map/ppermute | solution.py:404
  9.4 16.4 %collective-permute-start.3 = (f32[11,32,256]{2,1,0:T(8,128)S(1)}, f32[11,32,256]{2,1,0:T(8,128)}, u32[]{:S(2)}, u32[]{:S(2)}) collective-permute-start(f32[11,32,256]{2,1,0:T(8,128)S(1)} %get-tuple-element.25), channel_id=1, source_target_pairs={{6,2},{4,10},{15,5},{13,13},{22,18},{20,26},{31,21},{29,29}} | collective-permute-start | bytes 1081352 | tf_op jit(solution)/shard_map/ppermute | solution.py:404
  11.7 17.3 %copy-start.7 = (f32[11,32,256]{2,1,0:T(8,128)}, f32[11,32,256]{2,1,0:T(8,128)S(1)}, u32[]{:S(2)}) copy-start(f32[11,32,256]{2,1,0:T(8,128)S(1)} %collective-permute-done.4.refs_6_) | copy-start | bytes 1081348
  11.7 14.2 %collective-permute-start.1 = (f32[11,32,256]{2,1,0:T(8,128)S(1)}, f32[11,32,256]{2,1,0:T(8,128)}, u32[]{:S(2)}, u32[]{:S(2)}) collective-permute-start(f32[11,32,256]{2,1,0:T(8,128)S(1)} %get-tuple-element.25), channel_id=1, source_target_pairs={{2,2},{0,10},{11,5},{9,13},{18,18},{16,26},{27,21},{25,29}} | collective-permute-start | bytes 1081352 | tf_op jit(solution)/shard_map/ppermute | solution.py:404
  13.1 15.8 %copy-start.8 = (f32[11,32,256]{2,1,0:T(8,128)}, f32[11,32,256]{2,1,0:T(8,128)S(1)}, u32[]{:S(2)}) copy-start(f32[11,32,256]{2,1,0:T(8,128)S(1)} %collective-permute-done.2.refs_4_) | copy-start | bytes 1081348
  13.1 15.8 %collective-permute-start.7 = (f32[11,32,256]{2,1,0:T(8,128)}, f32[11,32,256]{2,1,0:T(8,128)}, u32[]{:S(2)}, u32[]{:S(2)}) collective-permute-start(f32[11,32,256]{2,1,0:T(8,128)} %broadcast_select_fusion.1), channel_id=1, source_target_pairs={{8,2},{3,10},{12,5},{7,13},{24,18},{19,26},{28,21},{23,29}} | collective-permute-start | bytes 1081352 | tf_op jit(solution)/shard_map/ppermute | solution.py:404
  22.6 10.2 %collective-permute-start.9 = (f32[11,32,256]{2,1,0:T(8,128)}, f32[11,32,256]{2,1,0:T(8,128)}, u32[]{:S(2)}, u32[]{:S(2)}) collective-permute-start(f32[11,32,256]{2,1,0:T(8,128)} %broadcast_select_fusion), channel_id=1, source_target_pairs={{3,2},{0,10},{15,5},{12,13},{19,18},{16,26},{31,21},{28,29}} | collective-permute-start | bytes 1081352 | tf_op jit(solution)/shard_map/ppermute | solution.py:404
  37.3 19.2 %collective-permute-start.10 = (f32[2,256,256]{2,1,0:T(8,128)}, f32[2,256,256]{2,1,0:T(8,128)}, u32[]{:S(2)}, u32[]{:S(2)}) collective-permute-start(f32[2,256,256]{2,1,0:T(8,128)} %get-tuple-element.27.refs_2_), channel_id=1, source_target_pairs={{0,8},{8,0},{16,24},{24,16},{1,9},{9,1},{17,25},{25,17},{2,10},{10... | collective-permute-start | bytes 1572872 | tf_op jit(solution)/shard_map/ppermute | solution.py:438
  38.2 17.6 %collective-permute-start.16 = (f32[10,32,256]{2,1,0:T(8,128)}, f32[10,32,256]{2,1,0:T(8,128)}, u32[]{:S(2)}, u32[]{:S(2)}) collective-permute-start(f32[10,32,256]{2,1,0:T(8,128)} %get-tuple-element.36), channel_id=1, source_target_pairs={{1,8},{5,12},{7,14},{8,1},{10,3},{14,7},{17,24},{21,28},{23,30},{2... | collective-permute-start | bytes 983048 | tf_op jit(solution)/shard_map/ppermute | solution.py:374
  39.5 21.9 %collective-permute-start.18 = (f32[10,32,256]{2,1,0:T(8,128)}, f32[10,32,256]{2,1,0:T(8,128)}, u32[]{:S(2)}, u32[]{:S(2)}) collective-permute-start(f32[10,32,256]{2,1,0:T(8,128)} %get-tuple-element.37), channel_id=1, source_target_pairs={{1,0},{5,4},{7,6},{8,9},{10,11},{14,15},{17,16},{21,20},{23,22},{2... | collective-permute-start | bytes 983048 | tf_op jit(solution)/shard_map/ppermute | solution.py:374
  40.9 24.2 %collective-permute-start.14 = (f32[10,32,256]{2,1,0:T(8,128)}, f32[10,32,256]{2,1,0:T(8,128)}, u32[]{:S(2)}, u32[]{:S(2)}) collective-permute-start(f32[10,32,256]{2,1,0:T(8,128)} %get-tuple-element.36), channel_id=1, source_target_pairs={{4,2},{6,10},{13,5},{15,13},{20,18},{22,26},{29,21},{31,29}} | collective-permute-start | bytes 983048 | tf_op jit(solution)/shard_map/ppermute | solution.py:404
  42.3 32.6 %collective-permute-start.12 = (f32[10,32,256]{2,1,0:T(8,128)}, f32[10,32,256]{2,1,0:T(8,128)}, u32[]{:S(2)}, u32[]{:S(2)}) collective-permute-start(f32[10,32,256]{2,1,0:T(8,128)} %get-tuple-element.36), channel_id=1, source_target_pairs={{0,2},{2,10},{9,5},{11,13},{16,18},{18,26},{25,21},{27,29}} | collective-permute-start | bytes 983048 | tf_op jit(solution)/shard_map/ppermute | solution.py:404
  55.8 20.4 %collective-permute-start.15 = (f32[10,32,256]{2,1,0:T(8,128)}, f32[10,32,256]{2,1,0:T(8,128)S(1)}, u32[]{:S(2)}, u32[]{:S(2)}) collective-permute-start(f32[10,32,256]{2,1,0:T(8,128)} %get-tuple-element.37), channel_id=1, source_target_pairs={{6,2},{4,10},{15,5},{13,13},{22,18},{20,26},{31,21},{29,29}} | collective-permute-start | bytes 983048 | tf_op jit(solution)/shard_map/ppermute | solution.py:404
  56.5 21.1 %collective-permute-start.13 = (f32[10,32,256]{2,1,0:T(8,128)}, f32[10,32,256]{2,1,0:T(8,128)S(1)}, u32[]{:S(2)}, u32[]{:S(2)}) collective-permute-start(f32[10,32,256]{2,1,0:T(8,128)} %get-tuple-element.37), channel_id=1, source_target_pairs={{2,2},{0,10},{11,5},{9,13},{18,18},{16,26},{27,21},{25,29}} | collective-permute-start | bytes 983048 | tf_op jit(solution)/shard_map/ppermute | solution.py:404
  61.4 29.4 %collective-permute-start.11 = (f32[2,256,256]{2,1,0:T(8,128)S(1)}, f32[2,256,256]{2,1,0:T(8,128)S(1)}, u32[]{:S(2)}, u32[]{:S(2)}) collective-permute-start(f32[2,256,256]{2,1,0:T(8,128)S(1)} %get-tuple-element.33.refs_5_), channel_id=1, source_target_pairs={{0,8},{8,0},{16,24},{24,16},{1,9},{9,1},{17,25},{25,17},{2,10},{10... | collective-permute-start | bytes 1572872 | tf_op jit(solution)/shard_map/ppermute | solution.py:447
  65.1 14.4 %collective-permute-start.20 = (f32[10,32,256]{2,1,0:T(8,128)S(1)}, f32[10,32,256]{2,1,0:T(8,128)S(1)}, u32[]{:S(2)}, u32[]{:S(2)}) collective-permute-start(f32[10,32,256]{2,1,0:T(8,128)S(1)} %get-tuple-element.48), channel_id=1, source_target_pairs={{8,2},{3,10},{12,5},{7,13},{24,18},{19,26},{28,21},{23,29}} | collective-permute-start | bytes 983048 | tf_op jit(solution)/shard_map/ppermute | solution.py:404
  74.9 15.8 %collective-permute-start.17 = (f32[10,32,256]{2,1,0:T(8,128)S(1)}, f32[10,32,256]{2,1,0:T(8,128)S(1)}, u32[]{:S(2)}, u32[]{:S(2)}) collective-permute-start(f32[10,32,256]{2,1,0:T(8,128)S(1)} %get-tuple-element.49), channel_id=1, source_target_pairs={{12,2},{14,10},{1,5},{3,13},{28,18},{30,26},{17,21},{19,29}} | collective-permute-start | bytes 983048 | tf_op jit(solution)/shard_map/ppermute | solution.py:404
  76.3 14.5 %collective-permute-start.21 = (f32[10,32,256]{2,1,0:T(8,128)S(1)}, f32[10,32,256]{2,1,0:T(8,128)S(1)}, u32[]{:S(2)}, u32[]{:S(2)}) collective-permute-start(f32[10,32,256]{2,1,0:T(8,128)S(1)} %broadcast_select_fusion.3), channel_id=1, source_target_pairs={{3,2},{0,10},{15,5},{12,13},{19,18},{16,26},{31,21},{28,29}} | collective-permute-start | bytes 983048 | tf_op jit(solution)/shard_map/ppermute | solution.py:404
  77.6 13.2 %collective-permute-start.19 = (f32[10,32,256]{2,1,0:T(8,128)S(1)}, f32[10,32,256]{2,1,0:T(8,128)S(1)}, u32[]{:S(2)}, u32[]{:S(2)}) collective-permute-start(f32[10,32,256]{2,1,0:T(8,128)S(1)} %broadcast_select_fusion.3), channel_id=1, source_target_pairs={{6,2},{4,10},{11,5},{9,13},{22,18},{20,26},{27,21},{25,29}} | collective-permute-start | bytes 983048 | tf_op jit(solution)/shard_map/ppermute | solution.py:404
  93.3 2.1 %collective-permute-start.22 = (f32[520,256]{1,0:T(8,128)S(1)}, f32[520,256]{1,0:T(8,128)S(1)}, u32[]{:S(2)}, u32[]{:S(2)}) collective-permute-start(f32[520,256]{1,0:T(8,128)S(1)} %get-tuple-element.38.refs_1_), channel_id=1, source_target_pairs={{0,8},{8,0},{16,24},{24,16},{1,9},{9,1},{17,25},{25,17},{2,10},{10... | collective-permute-start | bytes 1597448 | tf_op jit(solution)/shard_map/ppermute | solution.py:462
  96.0 3.3 %collective-permute-start.23 = (f32[3,32,256]{2,1,0:T(8,128)S(1)}, f32[3,32,256]{2,1,0:T(8,128)S(1)}, u32[]{:S(2)}, u32[]{:S(2)}) collective-permute-start(f32[3,32,256]{2,1,0:T(8,128)S(1)} %get-tuple-element.42), channel_id=1, source_target_pairs={{2,0},{10,4},{5,8},{13,12},{18,16},{26,20},{21,24},{29,28}} | collective-permute-start | bytes 294920 | tf_op jit(solution)/shard_map/ppermute | solution.py:471
  96.6 2.7 %collective-permute-start.24 = (f32[3,32,256]{2,1,0:T(8,128)S(1)}, f32[3,32,256]{2,1,0:T(8,128)S(1)}, u32[]{:S(2)}, u32[]{:S(2)}) collective-permute-start(f32[3,32,256]{2,1,0:T(8,128)S(1)} %get-tuple-element.43), channel_id=1, source_target_pairs={{2,1},{10,5},{5,9},{13,13},{18,17},{26,21},{21,25},{29,29}} | collective-permute-start | bytes 294920 | tf_op jit(solution)/shard_map/ppermute | solution.py:471
  97.3 2.0 %collective-permute-start.25 = (f32[3,32,256]{2,1,0:T(8,128)S(1)}, f32[3,32,256]{2,1,0:T(8,128)S(1)}, u32[]{:S(2)}, u32[]{:S(2)}) collective-permute-start(f32[3,32,256]{2,1,0:T(8,128)S(1)} %get-tuple-element.44), channel_id=1, source_target_pairs={{2,2},{10,6},{5,10},{13,14},{18,18},{26,22},{21,26},{29,30}} | collective-permute-start | bytes 294920 | tf_op jit(solution)/shard_map/ppermute | solution.py:471
  98.0 15.1 %collective-permute-start.26 = (f32[3,32,256]{2,1,0:T(8,128)S(1)}, f32[3,32,256]{2,1,0:T(8,128)S(1)}, u32[]{:S(2)}, u32[]{:S(2)}) collective-permute-start(f32[3,32,256]{2,1,0:T(8,128)S(1)} %get-tuple-element.45), channel_id=1, source_target_pairs={{2,3},{10,7},{5,11},{13,15},{18,19},{26,23},{21,27},{29,31}} | collective-permute-start | bytes 294920 | tf_op jit(solution)/shard_map/ppermute | solution.py:471
  113.2 6.5 %collective-permute-start.27 = (f32[32,256]{1,0:T(8,128)S(1)}, f32[32,256]{1,0:T(8,128)S(1)}, u32[]{:S(2)}, u32[]{:S(2)}) collective-permute-start(f32[32,256]{1,0:T(8,128)S(1)} %slice_bitcast_fusion.1), channel_id=1, source_target_pairs={{0,8},{8,0},{16,24},{24,16},{1,9},{9,1},{17,25},{25,17},{2,10},{10... | collective-permute-start | bytes 98312 | tf_op jit(solution)/shard_map/ppermute | solution.py:479
  119.7 3.9 %collective-permute-start.28 = (f32[32,256]{1,0:T(8,128)S(1)}, f32[32,256]{1,0:T(8,128)S(1)}, u32[]{:S(2)}, u32[]{:S(2)}) collective-permute-start(f32[32,256]{1,0:T(8,128)S(1)} %fusion.1), channel_id=1, source_target_pairs={{0,16},{8,24},{16,0},{24,8},{1,17},{9,25},{17,1},{25,9},{2,18},{10... | collective-permute-start | bytes 98312 | tf_op jit(solution)/shard_map/ppermute | solution.py:479
  (16 other events, 90.9 us)

commit v5 on v4

--- a/solution.py
+++ b/solution.py
@@ -367,7 +367,7 @@
         return pair == detour(piece, blocks)
 
     def remote(piece, pair):
-        return pair != home_row(piece, blocks) // 2
+        return all(pair != home_row(i, blocks) // 2 for i in range(2))
 
     def move(sends, moved):
         return [
@@ -377,8 +377,8 @@
 
     device = lax.axis_index("cuts") * blocks + row
 
-    def gather(sends, turns, moved, carried=None):
-        got = {}
+    def passing(sends, turns, moved, carried=None):
+        out = []
         for i in range(2):
             groups = []
             for k in [k for k in turns if k % 2 == i]:
@@ -401,7 +401,13 @@
                 if passed:
                     here = functools.reduce(lambda x, t: x | (device == t), sorted(passed), False)
                     send = jnp.where(here, carried[i], send)
-                got |= {k: lax.ppermute(send, BOTH, pairs) for k, pairs in rounds}
+                out.append((send, rounds))
+        return out
+
+    def gather(sends, turns, moved, carried=None):
+        got = {}
+        for send, rounds in passing(sends, turns, moved, carried):
+            got |= {k: lax.ppermute(send, BOTH, pairs) for k, pairs in rounds}
         return got
 
     turns = blocks // 2
@@ -416,8 +422,12 @@
     sends = build(data, recon)
     carried = move(sends, remote)
     second = gather(sends, near, remote)
-    second |= gather(sends, far, remote, carried)
-    second = [in_hbm(second[k]) for k in range(blocks)]
+    sends = passing(sends, far, remote, carried)
+    ready = lax.optimization_barrier((info, *[send for send, _ in sends]))
+    info, sends = ready[0], [(send, rounds) for send, (_, rounds) in zip(ready[1:], sends)]
+    for send, rounds in sends:
+        second |= {k: lax.ppermute(send, BOTH, pairs) for k, pairs in rounds}
+    second = [second[k] for k in range(blocks)]
 
     image, spectrum = shape(2, n, n), shape(2, n, count * n)
     scalars = shape(2, 8, 128)
@@ -434,7 +444,6 @@
             pltpu.SemaphoreType.DMA((4, blocks)),
         ],
     )(info, sigmoid_steepness, *first, tables)
-    u, wt, spec0 = in_hbm(u), in_hbm(wt), in_hbm(spec0)
     other0 = lax.ppermute(part0, "cuts", swap)
     res1, dir1, sc1, spec1, part1 = call(
         at_home(second_kernel),
@@ -443,7 +452,6 @@
         out_shape=[image, image, scalars, spectrum, image],
         scratch_shapes=[table_space, spec_space, pltpu.SemaphoreType.DMA((2,))],
     )(info, u, part0, other0, maps_full, wt, tables)
-    spec1 = in_hbm(spec1)
     other1 = lax.ppermute(part1, "cuts", swap)
     sol2, dir2, sc2, mine = call(
         at_home(functools.partial(third_kernel, blocks, planes)),

time: 125 us -> 114 us (0.912)
  starting transfers between devices: 54.1 us -> 63.7 us
  waiting for transfers between devices: 49.6 us -> 41.4 us
  local copies, waits for them, and re-layouts: 7.89 us -> 2.7 us
  other arithmetic: 5.48 us -> 1.1 us
  Pallas kernels: 5.39 us -> 3.12 us
    ppermute x16 -> x12, starting transfers between devices: 35.5 us -> 18.7 us  [gather(): got |= {k: lax.ppermute(send, BOTH, pairs) for k, pairs in rounds}]
    ppermute x1, starting transfers between devices: 2.71 us -> 18.7 us  [steps(): other1 = lax.ppermute(part1, 'cuts', swap)]
    ppermute x0 -> x4, starting transfers between devices: none -> 13.8 us  [steps(): second |= {k: lax.ppermute(send, BOTH, pairs) for k, pairs in rounds}]
    ppermute x4, waiting for transfers between devices: 12.2 us -> 0.01 us  [move(): lax.ppermute(send, BOTH, move_pairs(i, pieces, blocks, moved))]
    ppermute x0 -> x4, waiting for transfers between devices: none -> 10.5 us  [steps(): second |= {k: lax.ppermute(send, BOTH, pairs) for k, pairs in rounds}]
    ppermute x16 -> x12, waiting for transfers between devices: 19.4 us -> 10.7 us  [gather(): got |= {k: lax.ppermute(send, BOTH, pairs) for k, pairs in rounds}]
    unnamed x39 -> x23, local copies, waits for them, and re-layouts: 5.79 us -> 1.4 us
    select_n x4, other arithmetic: 3.75 us -> 0.22 us  [passing(): send = jnp.where(here, carried[i], send)]
  transfers between devices with their start and end apart: 29 -> 29, of which waited for: 9 -> 7; matrix products, arithmetic and copies ran while one was open for 4% -> 1% of each run, Pallas kernels for 1% -> 1%
where the time goes in v5:
time: 114 us
  starting transfers between devices  63.7 us (56%)
  waiting for transfers between devices  41.4 us (36%)
  Pallas kernels  3.12 us (3%)
  local copies, waits for them, and re-layouts  2.7 us (2%)
  between operations  1.87 us (2%)
    ppermute x1, starting transfers between devices, steps(): other1 = lax.ppermute(part1, 'cuts', swap)  18.7 us
    ppermute x12, starting transfers between devices, gather(): got |= {k: lax.ppermute(send, BOTH, pairs) for k, pairs in rounds}  18.7 us
    ppermute x4, waiting for transfers between devices, steps(): lax.ppermute(outs[k], BOTH, scatter_pairs(k, pieces, blocks))  15.7 us
    ppermute x4, starting transfers between devices, steps(): second |= {k: lax.ppermute(send, BOTH, pairs) for k, pairs in rounds}  13.8 us
    ppermute x12, waiting for transfers between devices, gather(): got |= {k: lax.ppermute(send, BOTH, pairs) for k, pairs in rounds}  10.7 us
    ppermute x4, waiting for transfers between devices, steps(): second |= {k: lax.ppermute(send, BOTH, pairs) for k, pairs in rounds}  10.5 us
    ppermute x2, starting transfers between devices, steps(): lax.ppermute(term, 'cuts', [(i, i ^ step) for i in range(pieces)])  4.85 us
    ppermute x4, starting transfers between devices, move(): lax.ppermute(send, BOTH, move_pairs(i, pieces, blocks, moved))  4.31 us
  transfers between devices with their start and end apart: 29, of which 7 were waited for; matrix products, arithmetic and copies ran while one was open for 1% of the time, Pallas kernels for 1%

profile of v5, /device:TPU:10, one launch (start us, length us, event | category | flops | bytes accessed | tf_op | source)
XLA Modules:
  0.0 113.9 jit_solution(3046377424042588515)
XLA Ops:
  0.7 1.3 %dynamic-slice_bitcast_fusion = (f32[8,32,256]{2,1,0:T(8,128)S(1)}, f32[8,32,256]{2,1,0:T(8,128)S(1)}, f32[8,32,256]{2,1,0:T(8,128)S(1)}, f32[8,32,256]{2,1,0:T(8,128)S(1)}) fusion(f32[2,8,32,256]{3,2,1,0:T(8,128)} %bitcast.29, s32[]{:T(128)S(6)} %select_n.45, s32[]{:T(128)S(6)} %select_n.44, f32[2,8,32,256]{3,2,1,0:T(8,128)} %bitcast.30), kind=kLoop, calls=%fused_computation.6 | loop fusion | bytes 2097160 | tf_op jit(solution)/shard_map/jit(dynamic_index_in_dim)/squeeze | solution.py:360
  2.1 1.4 %collective-permute-start.8 = (f32[11,32,256]{2,1,0:T(8,128)S(1)}, f32[11,32,256]{2,1,0:T(8,128)}, u32[]{:S(2)}, u32[]{:S(2)}) collective-permute-start(f32[11,32,256]{2,1,0:T(8,128)S(1)} %get-tuple-element.30), channel_id=1, source_target_pairs={{1,8},{14,7},{17,24},{30,23}} | collective-permute-start | bytes 1081352 | tf_op jit(solution)/shard_map/ppermute | solution.py:374
  3.5 1.4 %collective-permute-start.10 = (f32[11,32,256]{2,1,0:T(8,128)S(1)}, f32[11,32,256]{2,1,0:T(8,128)}, u32[]{:S(2)}, u32[]{:S(2)}) collective-permute-start(f32[11,32,256]{2,1,0:T(8,128)S(1)} %get-tuple-element.31), channel_id=1, source_target_pairs={{1,0},{14,15},{17,16},{30,31}} | collective-permute-start | bytes 1081352 | tf_op jit(solution)/shard_map/ppermute | solution.py:374
  5.6 0.7 collective-permute-start.4
  6.3 1.4 %collective-permute-start.2 = (f32[11,32,256]{2,1,0:T(8,128)S(1)}, f32[11,32,256]{2,1,0:T(8,128)}, u32[]{:S(2)}, u32[]{:S(2)}) collective-permute-start(f32[11,32,256]{2,1,0:T(8,128)S(1)} %get-tuple-element.30), channel_id=1, source_target_pairs={{0,2},{2,10},{9,5},{11,13},{16,18},{18,26},{25,21},{27,29}} | collective-permute-start | bytes 1081352 | tf_op jit(solution)/shard_map/ppermute | solution.py:410
  8.5 0.8 collective-permute-start
  9.3 0.7 collective-permute-start.1
  10.2 0.7 collective-permute-start.7
  10.9 0.7 collective-permute-start.5
  11.6 0.7 collective-permute-start.3
  12.3 9.3 %collective-permute-start.9 = (f32[11,32,256]{2,1,0:T(8,128)S(1)}, f32[11,32,256]{2,1,0:T(8,128)S(1)}, u32[]{:S(2)}, u32[]{:S(2)}) collective-permute-start(f32[11,32,256]{2,1,0:T(8,128)S(1)} %broadcast_select_fusion.1), channel_id=1, source_target_pairs={{8,2},{3,10},{12,5},{7,13},{24,18},{19,26},{28,21},{23,29}} | collective-permute-start | bytes 1081352 | tf_op jit(solution)/shard_map/ppermute | solution.py:410
  21.7 1.8 %collective-permute-start.11 = (f32[11,32,256]{2,1,0:T(8,128)S(1)}, f32[11,32,256]{2,1,0:T(8,128)S(1)}, u32[]{:S(2)}, u32[]{:S(2)}) collective-permute-start(f32[11,32,256]{2,1,0:T(8,128)S(1)} %broadcast_select_fusion), channel_id=1, source_target_pairs={{3,2},{0,10},{15,5},{12,13},{19,18},{16,26},{31,21},{28,29}} | collective-permute-start | bytes 1081352 | tf_op jit(solution)/shard_map/ppermute | solution.py:410
  23.6 6.8 %collective-permute-done.9.refs_8_ = f32[11,32,256]{2,1,0:T(8,128)S(1)} collective-permute-done((f32[11,32,256]{2,1,0:T(8,128)S(1)}, f32[11,32,256]{2,1,0:T(8,128)S(1)}, u32[]{:S(2)}, u32[]{:S(2)}) %collective-permute-start.9) | collective-permute-done | bytes 360480 | tf_op jit(solution)/shard_map/ppermute | solution.py:410
  30.4 3.9 %collective-permute-done.11.refs_9_ = f32[11,32,256]{2,1,0:T(8,128)S(1)} collective-permute-done((f32[11,32,256]{2,1,0:T(8,128)S(1)}, f32[11,32,256]{2,1,0:T(8,128)S(1)}, u32[]{:S(2)}, u32[]{:S(2)}) %collective-permute-start.11) | collective-permute-done | bytes 360480 | tf_op jit(solution)/shard_map/ppermute | solution.py:410
  34.3 0.7 copy-done.7
  35.0 0.8 shard_map.86
  36.0 0.7 collective-permute-start.16
  36.7 0.7 collective-permute-start.14
  37.3 0.7 collective-permute-start.17
  38.7 0.7 shard_map.87
  39.5 18.7 %collective-permute-start.13 = (f32[2,256,256]{2,1,0:T(8,128)S(1)}, f32[2,256,256]{2,1,0:T(8,128)S(1)}, u32[]{:S(2)}, u32[]{:S(2)}) collective-permute-start(f32[2,256,256]{2,1,0:T(8,128)S(1)} %get-tuple-element.39.refs_5_), channel_id=1, source_target_pairs={{0,8},{8,0},{16,24},{24,16},{1,9},{9,1},{17,25},{25,17},{2,10},{10... | collective-permute-start | bytes 1572872 | tf_op jit(solution)/shard_map/ppermute | solution.py:455
  58.2 8.4 %collective-permute-start.20 = (f32[10,32,256]{2,1,0:T(8,128)S(1)}, f32[10,32,256]{2,1,0:T(8,128)S(1)}, u32[]{:S(2)}, u32[]{:S(2)}) collective-permute-start(f32[10,32,256]{2,1,0:T(8,128)S(1)} %broadcast_select_fusion.3), channel_id=1, source_target_pairs={{8,2},{3,10},{12,5},{7,13},{24,18},{19,26},{28,21},{23,29}} | collective-permute-start | bytes 983048 | tf_op jit(solution)/shard_map/ppermute | solution.py:429
  67.3 4.0 %collective-permute-start.21 = (f32[10,32,256]{2,1,0:T(8,128)S(1)}, f32[10,32,256]{2,1,0:T(8,128)S(1)}, u32[]{:S(2)}, u32[]{:S(2)}) collective-permute-start(f32[10,32,256]{2,1,0:T(8,128)S(1)} %broadcast_select_fusion.2), channel_id=1, source_target_pairs={{3,2},{0,10},{15,5},{12,13},{19,18},{16,26},{31,21},{28,29}} | collective-permute-start | bytes 983048 | tf_op jit(solution)/shard_map/ppermute | solution.py:429
  72.0 10.4 %collective-permute-done.21.refs_18_ = f32[10,32,256]{2,1,0:T(8,128)S(1)} collective-permute-done((f32[10,32,256]{2,1,0:T(8,128)S(1)}, f32[10,32,256]{2,1,0:T(8,128)S(1)}, u32[]{:S(2)}, u32[]{:S(2)}) %collective-permute-start.21) | collective-permute-done | bytes 327712 | tf_op jit(solution)/shard_map/ppermute | solution.py:429
  82.5 1.0 shard_map.88
  83.5 1.9 %collective-permute-done.22.refs_2_ = f32[520,256]{1,0:T(8,128)S(1)} collective-permute-done((f32[520,256]{1,0:T(8,128)S(1)}, f32[520,256]{1,0:T(8,128)S(1)}, u32[]{:S(2)}, u32[]{:S(2)}) %collective-permute-start.22) | collective-permute-done | bytes 532512 | tf_op jit(solution)/shard_map/ppermute | solution.py:470
  88.0 1.3 %collective-permute-start.26 = (f32[3,32,256]{2,1,0:T(8,128)S(1)}, f32[3,32,256]{2,1,0:T(8,128)S(1)}, u32[]{:S(2)}, u32[]{:S(2)}) collective-permute-start(f32[3,32,256]{2,1,0:T(8,128)S(1)} %get-tuple-element.51), channel_id=1, source_target_pairs={{2,3},{10,7},{5,11},{13,15},{18,19},{26,23},{21,27},{29,31}} | collective-permute-start | bytes 294920 | tf_op jit(solution)/shard_map/ppermute | solution.py:479
  89.4 15.7 %collective-permute-done.26 = f32[3,32,256]{2,1,0:T(8,128)S(1)} collective-permute-done((f32[3,32,256]{2,1,0:T(8,128)S(1)}, f32[3,32,256]{2,1,0:T(8,128)S(1)}, u32[]{:S(2)}, u32[]{:S(2)}) %collective-permute-start.26) | collective-permute-done | bytes 98336 | tf_op jit(solution)/shard_map/ppermute | solution.py:479
  105.1 3.3 %collective-permute-start.27 = (f32[32,256]{1,0:T(8,128)S(1)}, f32[32,256]{1,0:T(8,128)S(1)}, u32[]{:S(2)}, u32[]{:S(2)}) collective-permute-start(f32[32,256]{1,0:T(8,128)S(1)} %slice_bitcast_fusion.1), channel_id=1, source_target_pairs={{0,8},{8,0},{16,24},{24,16},{1,9},{9,1},{17,25},{25,17},{2,10},{10... | collective-permute-start | bytes 98312 | tf_op jit(solution)/shard_map/ppermute | solution.py:487
  108.4 0.9 collective-permute-done.27
  109.3 1.5 %collective-permute-start.28 = (f32[32,256]{1,0:T(8,128)S(1)}, f32[32,256]{1,0:T(8,128)S(1)}, u32[]{:S(2)}, u32[]{:S(2)}) collective-permute-start(f32[32,256]{1,0:T(8,128)S(1)} %fusion.1), channel_id=1, source_target_pairs={{0,16},{8,24},{16,0},{24,8},{1,17},{9,25},{17,1},{25,9},{2,18},{10... | collective-permute-start | bytes 98312 | tf_op jit(solution)/shard_map/ppermute | solution.py:487
  111.5 1.8 %collective-permute-done.28 = f32[32,256]{1,0:T(8,128)S(1)} collective-permute-done((f32[32,256]{1,0:T(8,128)S(1)}, f32[32,256]{1,0:T(8,128)S(1)}, u32[]{:S(2)}, u32[]{:S(2)}) %collective-permute-start.28) | collective-permute-done | bytes 32800 | tf_op jit(solution)/shard_map/ppermute | solution.py:487
  (65 shorter events, 7.2 us)
Async XLA Ops:
  2.1 6.4 %collective-permute-start.8 = (f32[11,32,256]{2,1,0:T(8,128)S(1)}, f32[11,32,256]{2,1,0:T(8,128)}, u32[]{:S(2)}, u32[]{:S(2)}) collective-permute-start(f32[11,32,256]{2,1,0:T(8,128)S(1)} %get-tuple-element.30), channel_id=1, source_target_pairs={{1,8},{14,7},{17,24},{30,23}} | collective-permute-start | bytes 1081352 | tf_op jit(solution)/shard_map/ppermute | solution.py:374
  3.5 5.8 %collective-permute-start.10 = (f32[11,32,256]{2,1,0:T(8,128)S(1)}, f32[11,32,256]{2,1,0:T(8,128)}, u32[]{:S(2)}, u32[]{:S(2)}) collective-permute-start(f32[11,32,256]{2,1,0:T(8,128)S(1)} %get-tuple-element.31), channel_id=1, source_target_pairs={{1,0},{14,15},{17,16},{30,31}} | collective-permute-start | bytes 1081352 | tf_op jit(solution)/shard_map/ppermute | solution.py:374
  4.9 6.7 %collective-permute-start.6 = (f32[11,32,256]{2,1,0:T(8,128)S(1)}, f32[11,32,256]{2,1,0:T(8,128)S(1)}, u32[]{:S(2)}, u32[]{:S(2)}) collective-permute-start(f32[11,32,256]{2,1,0:T(8,128)S(1)} %get-tuple-element.30), channel_id=1, source_target_pairs={{5,2},{7,10},{8,5},{10,13},{21,18},{23,26},{24,21},{26,29}} | collective-permute-start | bytes 1081352 | tf_op jit(solution)/shard_map/ppermute | solution.py:410
  5.6 6.7 %collective-permute-start.4 = (f32[11,32,256]{2,1,0:T(8,128)S(1)}, f32[11,32,256]{2,1,0:T(8,128)S(1)}, u32[]{:S(2)}, u32[]{:S(2)}) collective-permute-start(f32[11,32,256]{2,1,0:T(8,128)S(1)} %get-tuple-element.30), channel_id=1, source_target_pairs={{4,2},{6,10},{13,5},{15,13},{20,18},{22,26},{29,21},{31,29}} | collective-permute-start | bytes 1081352 | tf_op jit(solution)/shard_map/ppermute | solution.py:410
  6.3 15.4 %collective-permute-start.2 = (f32[11,32,256]{2,1,0:T(8,128)S(1)}, f32[11,32,256]{2,1,0:T(8,128)}, u32[]{:S(2)}, u32[]{:S(2)}) collective-permute-start(f32[11,32,256]{2,1,0:T(8,128)S(1)} %get-tuple-element.30), channel_id=1, source_target_pairs={{0,2},{2,10},{9,5},{11,13},{16,18},{18,26},{25,21},{27,29}} | collective-permute-start | bytes 1081352 | tf_op jit(solution)/shard_map/ppermute | solution.py:410
  8.4 26.6 %copy-start = (bf16[10,256,256]{2,1,0:T(8,128)(2,1)S(1)}, bf16[10,256,256]{2,1,0:T(8,128)(2,1)}, u32[]{:S(2)}) copy-start(bf16[10,256,256]{2,1,0:T(8,128)(2,1)} %constant.78.clone.refs_10_.refs_6_.refs_19_) | copy-start | bytes 3932164
  8.5 1.7 %collective-permute-start = (f32[10,32,256]{2,1,0:T(8,128)S(1)}, f32[10,32,256]{2,1,0:T(8,128)S(1)}, u32[]{:S(2)}, u32[]{:S(2)}) collective-permute-start(f32[10,32,256]{2,1,0:T(8,128)S(1)} %get-tuple-element.27), channel_id=1, source_target_pairs={{1,8},{7,14},{8,1},{14,7},{17,24},{23,30},{24,17},{30,23}} | collective-permute-start | bytes 983048 | tf_op jit(solution)/shard_map/ppermute | solution.py:374
  9.3 1.5 %collective-permute-start.1 = (f32[10,32,256]{2,1,0:T(8,128)S(1)}, f32[10,32,256]{2,1,0:T(8,128)S(1)}, u32[]{:S(2)}, u32[]{:S(2)}) collective-permute-start(f32[10,32,256]{2,1,0:T(8,128)S(1)} %get-tuple-element.28), channel_id=1, source_target_pairs={{1,0},{7,6},{8,9},{14,15},{17,16},{23,22},{24,25},{30,31}} | collective-permute-start | bytes 983048 | tf_op jit(solution)/shard_map/ppermute | solution.py:374
  10.2 13.4 %collective-permute-start.7 = (f32[11,32,256]{2,1,0:T(8,128)S(1)}, f32[11,32,256]{2,1,0:T(8,128)S(1)}, u32[]{:S(2)}, u32[]{:S(2)}) collective-permute-start(f32[11,32,256]{2,1,0:T(8,128)S(1)} %get-tuple-element.31), channel_id=1, source_target_pairs={{7,2},{5,10},{10,5},{8,13},{23,18},{21,26},{26,21},{24,29}} | collective-permute-start | bytes 1081352 | tf_op jit(solution)/shard_map/ppermute | solution.py:410
  10.9 12.7 %collective-permute-start.5 = (f32[11,32,256]{2,1,0:T(8,128)S(1)}, f32[11,32,256]{2,1,0:T(8,128)S(1)}, u32[]{:S(2)}, u32[]{:S(2)}) collective-permute-start(f32[11,32,256]{2,1,0:T(8,128)S(1)} %get-tuple-element.31), channel_id=1, source_target_pairs={{6,2},{4,10},{15,5},{13,13},{22,18},{20,26},{31,21},{29,29}} | collective-permute-start | bytes 1081352 | tf_op jit(solution)/shard_map/ppermute | solution.py:410
  11.6 22.7 %copy-start.1 = (f32[11,32,256]{2,1,0:T(8,128)}, f32[11,32,256]{2,1,0:T(8,128)S(1)}, u32[]{:S(2)}) copy-start(f32[11,32,256]{2,1,0:T(8,128)S(1)} %collective-permute-done.6.refs_6_) | copy-start | bytes 1081348
  11.6 12.0 %collective-permute-start.3 = (f32[11,32,256]{2,1,0:T(8,128)S(1)}, f32[11,32,256]{2,1,0:T(8,128)S(1)}, u32[]{:S(2)}, u32[]{:S(2)}) collective-permute-start(f32[11,32,256]{2,1,0:T(8,128)S(1)} %get-tuple-element.31), channel_id=1, source_target_pairs={{2,2},{0,10},{11,5},{9,13},{18,18},{16,26},{27,21},{25,29}} | collective-permute-start | bytes 1081352 | tf_op jit(solution)/shard_map/ppermute | solution.py:410
  12.3 22.0 %copy-start.2 = (f32[11,32,256]{2,1,0:T(8,128)}, f32[11,32,256]{2,1,0:T(8,128)S(1)}, u32[]{:S(2)}) copy-start(f32[11,32,256]{2,1,0:T(8,128)S(1)} %collective-permute-done.4.refs_4_) | copy-start | bytes 1081348
  12.3 18.1 %collective-permute-start.9 = (f32[11,32,256]{2,1,0:T(8,128)S(1)}, f32[11,32,256]{2,1,0:T(8,128)S(1)}, u32[]{:S(2)}, u32[]{:S(2)}) collective-permute-start(f32[11,32,256]{2,1,0:T(8,128)S(1)} %broadcast_select_fusion.1), channel_id=1, source_target_pairs={{8,2},{3,10},{12,5},{7,13},{24,18},{19,26},{28,21},{23,29}} | collective-permute-start | bytes 1081352 | tf_op jit(solution)/shard_map/ppermute | solution.py:410
  21.7 12.6 %collective-permute-start.11 = (f32[11,32,256]{2,1,0:T(8,128)S(1)}, f32[11,32,256]{2,1,0:T(8,128)S(1)}, u32[]{:S(2)}, u32[]{:S(2)}) collective-permute-start(f32[11,32,256]{2,1,0:T(8,128)S(1)} %broadcast_select_fusion), channel_id=1, source_target_pairs={{3,2},{0,10},{15,5},{12,13},{19,18},{16,26},{31,21},{28,29}} | collective-permute-start | bytes 1081352 | tf_op jit(solution)/shard_map/ppermute | solution.py:410
  35.9 2.8 %collective-permute-start.12 = (f32[2,256,256]{2,1,0:T(8,128)S(1)}, f32[2,256,256]{2,1,0:T(8,128)S(1)}, u32[]{:S(2)}, u32[]{:S(2)}) collective-permute-start(f32[2,256,256]{2,1,0:T(8,128)S(1)} %get-tuple-element.33.refs_2_), channel_id=1, source_target_pairs={{0,8},{8,0},{16,24},{24,16},{1,9},{9,1},{17,25},{25,17},{2,10},{10... | collective-permute-start | bytes 1572872 | tf_op jit(solution)/shard_map/ppermute | solution.py:447
  36.0 22.2 %collective-permute-start.16 = (f32[10,32,256]{2,1,0:T(8,128)S(1)}, f32[10,32,256]{2,1,0:T(8,128)S(1)}, u32[]{:S(2)}, u32[]{:S(2)}) collective-permute-start(f32[10,32,256]{2,1,0:T(8,128)S(1)} %get-tuple-element.27), channel_id=1, source_target_pairs={{4,2},{6,10},{13,5},{15,13},{20,18},{22,26},{29,21},{31,29}} | collective-permute-start | bytes 983048 | tf_op jit(solution)/shard_map/ppermute | solution.py:410
  36.7 29.9 %collective-permute-start.14 = (f32[10,32,256]{2,1,0:T(8,128)S(1)}, f32[10,32,256]{2,1,0:T(8,128)S(1)}, u32[]{:S(2)}, u32[]{:S(2)}) collective-permute-start(f32[10,32,256]{2,1,0:T(8,128)S(1)} %get-tuple-element.27), channel_id=1, source_target_pairs={{0,2},{2,10},{9,5},{11,13},{16,18},{18,26},{25,21},{27,29}} | collective-permute-start | bytes 983048 | tf_op jit(solution)/shard_map/ppermute | solution.py:410
  37.3 30.0 %collective-permute-start.17 = (f32[10,32,256]{2,1,0:T(8,128)S(1)}, f32[10,32,256]{2,1,0:T(8,128)S(1)}, u32[]{:S(2)}, u32[]{:S(2)}) collective-permute-start(f32[10,32,256]{2,1,0:T(8,128)S(1)} %get-tuple-element.28), channel_id=1, source_target_pairs={{6,2},{4,10},{15,5},{13,13},{22,18},{20,26},{31,21},{29,29}} | collective-permute-start | bytes 983048 | tf_op jit(solution)/shard_map/ppermute | solution.py:410
  38.0 33.3 %collective-permute-start.15 = (f32[10,32,256]{2,1,0:T(8,128)S(1)}, f32[10,32,256]{2,1,0:T(8,128)S(1)}, u32[]{:S(2)}, u32[]{:S(2)}) collective-permute-start(f32[10,32,256]{2,1,0:T(8,128)S(1)} %get-tuple-element.28), channel_id=1, source_target_pairs={{2,2},{0,10},{11,5},{9,13},{18,18},{16,26},{27,21},{25,29}} | collective-permute-start | bytes 983048 | tf_op jit(solution)/shard_map/ppermute | solution.py:410
  39.5 43.0 %collective-permute-start.13 = (f32[2,256,256]{2,1,0:T(8,128)S(1)}, f32[2,256,256]{2,1,0:T(8,128)S(1)}, u32[]{:S(2)}, u32[]{:S(2)}) collective-permute-start(f32[2,256,256]{2,1,0:T(8,128)S(1)} %get-tuple-element.39.refs_5_), channel_id=1, source_target_pairs={{0,8},{8,0},{16,24},{24,16},{1,9},{9,1},{17,25},{25,17},{2,10},{10... | collective-permute-start | bytes 1572872 | tf_op jit(solution)/shard_map/ppermute | solution.py:455
  58.2 13.8 %collective-permute-start.20 = (f32[10,32,256]{2,1,0:T(8,128)S(1)}, f32[10,32,256]{2,1,0:T(8,128)S(1)}, u32[]{:S(2)}, u32[]{:S(2)}) collective-permute-start(f32[10,32,256]{2,1,0:T(8,128)S(1)} %broadcast_select_fusion.3), channel_id=1, source_target_pairs={{8,2},{3,10},{12,5},{7,13},{24,18},{19,26},{28,21},{23,29}} | collective-permute-start | bytes 983048 | tf_op jit(solution)/shard_map/ppermute | solution.py:429
  66.6 5.4 %collective-permute-start.18 = (f32[10,32,256]{2,1,0:T(8,128)S(1)}, f32[10,32,256]{2,1,0:T(8,128)S(1)}, u32[]{:S(2)}, u32[]{:S(2)}) collective-permute-start(f32[10,32,256]{2,1,0:T(8,128)S(1)} %broadcast_select_fusion.3), channel_id=1, source_target_pairs={{5,2},{14,10},{1,5},{10,13},{21,18},{30,26},{17,21},{26,29}} | collective-permute-start | bytes 983048 | tf_op jit(solution)/shard_map/ppermute | solution.py:429
  67.3 15.2 %collective-permute-start.21 = (f32[10,32,256]{2,1,0:T(8,128)S(1)}, f32[10,32,256]{2,1,0:T(8,128)S(1)}, u32[]{:S(2)}, u32[]{:S(2)}) collective-permute-start(f32[10,32,256]{2,1,0:T(8,128)S(1)} %broadcast_select_fusion.2), channel_id=1, source_target_pairs={{3,2},{0,10},{15,5},{12,13},{19,18},{16,26},{31,21},{28,29}} | collective-permute-start | bytes 983048 | tf_op jit(solution)/shard_map/ppermute | solution.py:429
  71.3 11.2 %collective-permute-start.19 = (f32[10,32,256]{2,1,0:T(8,128)S(1)}, f32[10,32,256]{2,1,0:T(8,128)S(1)}, u32[]{:S(2)}, u32[]{:S(2)}) collective-permute-start(f32[10,32,256]{2,1,0:T(8,128)S(1)} %broadcast_select_fusion.2), channel_id=1, source_target_pairs={{6,2},{5,10},{10,5},{9,13},{22,18},{21,26},{26,21},{25,29}} | collective-permute-start | bytes 983048 | tf_op jit(solution)/shard_map/ppermute | solution.py:429
  83.5 2.0 %collective-permute-start.22 = (f32[520,256]{1,0:T(8,128)S(1)}, f32[520,256]{1,0:T(8,128)S(1)}, u32[]{:S(2)}, u32[]{:S(2)}) collective-permute-start(f32[520,256]{1,0:T(8,128)S(1)} %get-tuple-element.44.refs_1_), channel_id=1, source_target_pairs={{0,8},{8,0},{16,24},{24,16},{1,9},{9,1},{17,25},{25,17},{2,10},{10... | collective-permute-start | bytes 1597448 | tf_op jit(solution)/shard_map/ppermute | solution.py:470
  86.0 3.3 %collective-permute-start.23 = (f32[3,32,256]{2,1,0:T(8,128)S(1)}, f32[3,32,256]{2,1,0:T(8,128)S(1)}, u32[]{:S(2)}, u32[]{:S(2)}) collective-permute-start(f32[3,32,256]{2,1,0:T(8,128)S(1)} %get-tuple-element.48), channel_id=1, source_target_pairs={{2,0},{10,4},{5,8},{13,12},{18,16},{26,20},{21,24},{29,28}} | collective-permute-start | bytes 294920 | tf_op jit(solution)/shard_map/ppermute | solution.py:479
  86.7 2.7 %collective-permute-start.24 = (f32[3,32,256]{2,1,0:T(8,128)S(1)}, f32[3,32,256]{2,1,0:T(8,128)S(1)}, u32[]{:S(2)}, u32[]{:S(2)}) collective-permute-start(f32[3,32,256]{2,1,0:T(8,128)S(1)} %get-tuple-element.49), channel_id=1, source_target_pairs={{2,1},{10,5},{5,9},{13,13},{18,17},{26,21},{21,25},{29,29}} | collective-permute-start | bytes 294920 | tf_op jit(solution)/shard_map/ppermute | solution.py:479
  87.4 2.0 %collective-permute-start.25 = (f32[3,32,256]{2,1,0:T(8,128)S(1)}, f32[3,32,256]{2,1,0:T(8,128)S(1)}, u32[]{:S(2)}, u32[]{:S(2)}) collective-permute-start(f32[3,32,256]{2,1,0:T(8,128)S(1)} %get-tuple-element.50), channel_id=1, source_target_pairs={{2,2},{10,6},{5,10},{13,14},{18,18},{26,22},{21,26},{29,30}} | collective-permute-start | bytes 294920 | tf_op jit(solution)/shard_map/ppermute | solution.py:479
  88.0 17.0 %collective-permute-start.26 = (f32[3,32,256]{2,1,0:T(8,128)S(1)}, f32[3,32,256]{2,1,0:T(8,128)S(1)}, u32[]{:S(2)}, u32[]{:S(2)}) collective-permute-start(f32[3,32,256]{2,1,0:T(8,128)S(1)} %get-tuple-element.51), channel_id=1, source_target_pairs={{2,3},{10,7},{5,11},{13,15},{18,19},{26,23},{21,27},{29,31}} | collective-permute-start | bytes 294920 | tf_op jit(solution)/shard_map/ppermute | solution.py:479
  105.1 4.2 %collective-permute-start.27 = (f32[32,256]{1,0:T(8,128)S(1)}, f32[32,256]{1,0:T(8,128)S(1)}, u32[]{:S(2)}, u32[]{:S(2)}) collective-permute-start(f32[32,256]{1,0:T(8,128)S(1)} %slice_bitcast_fusion.1), channel_id=1, source_target_pairs={{0,8},{8,0},{16,24},{24,16},{1,9},{9,1},{17,25},{25,17},{2,10},{10... | collective-permute-start | bytes 98312 | tf_op jit(solution)/shard_map/ppermute | solution.py:487
  109.3 3.9 %collective-permute-start.28 = (f32[32,256]{1,0:T(8,128)S(1)}, f32[32,256]{1,0:T(8,128)S(1)}, u32[]{:S(2)}, u32[]{:S(2)}) collective-permute-start(f32[32,256]{1,0:T(8,128)S(1)} %fusion.1), channel_id=1, source_target_pairs={{0,16},{8,24},{16,0},{24,8},{1,17},{9,25},{17,1},{25,9},{2,18},{10... | collective-permute-start | bytes 98312 | tf_op jit(solution)/shard_map/ppermute | solution.py:487
  (8 other events, 47.1 us)

commit v6 on v5

--- a/solution.py
+++ b/solution.py
@@ -122,14 +122,16 @@
 
 def block_of(turn, half, column, blocks):
     if turn < blocks // 2:
-        return turn ^ half, column
+        return turn ^ half ^ (2 * column), column
     return (turn - blocks // 2) ^ half ^ (2 - 2 * column), 1 - column
 
 
 def block_row(turn, info, blocks, extent):
     column, half = info[0], info[2]
     pair = lax.bitwise_xor(jnp.int32(turn % (blocks // 2)), half)
-    if turn >= blocks // 2:
+    if turn < blocks // 2:
+        pair = lax.bitwise_xor(pair, 2 * column)
+    else:
         pair = lax.bitwise_xor(pair, 2 - 2 * column)
         column = 1 - column
     return pl.multiple_of((pair * 2 + column) * extent, extent)
@@ -253,8 +255,10 @@
     terms[...] = (
         (mine[:n] + other[:n]) + alpha * (mine[n : 2 * n] + other[n : 2 * n])
     ).T
+    lower, upper = (scatter_order(i, 2 * len(outs)) for i in range(2))
     for k, out in enumerate(outs):
-        rows = pl.ds(pl.multiple_of((half * len(outs) + k) * extent, extent), extent)
+        block = jnp.where(half == 1, len(outs) + upper[k], lower[k])
+        rows = pl.ds(pl.multiple_of(block * extent, extent), extent)
         out[0] = sol[0, rows] + alpha * p_ref[0, rows]
         out[1] = sol[1, rows] + alpha * p_ref[1, rows]
         out[2] = terms[rows]
@@ -317,13 +321,18 @@
     return pairs
 
 
+def scatter_order(half, blocks):
+    last = home_row(half, blocks) - half * (blocks // 2)
+    return [i for i in range(blocks // 2) if i != last] + [last]
+
+
 def scatter_pairs(turn, pieces, blocks):
     pairs = []
     for piece in range(pieces):
         for half in range(2):
             source = (piece - piece % 2 + half) * blocks + home_row(piece, blocks)
-            target = piece * blocks + turn + half * (blocks // 2)
-            pairs.append((source, target))
+            block = scatter_order(half, blocks)[turn] + half * (blocks // 2)
+            pairs.append((source, piece * blocks + block))
     return pairs
 
 
@@ -421,8 +430,8 @@
     first = [in_hbm(first[k]) for k in range(blocks)]
     sends = build(data, recon)
     carried = move(sends, remote)
-    second = gather(sends, near, remote)
-    sends = passing(sends, far, remote, carried)
+    second = gather(sends, near[2:], remote)
+    sends = passing(sends, near[:2], remote) + passing(sends, far, remote, carried)
     ready = lax.optimization_barrier((info, *[send for send, _ in sends]))
     info, sends = ready[0], [(send, rounds) for send, (_, rounds) in zip(ready[1:], sends)]
     for send, rounds in sends:

time: 114 us -> 115 us (level)
  the two profiles are of different devices: /device:TPU:10 before, /device:TPU:8 now
where the time goes in v6:
time: 115 us; the launch traced here: 114 us
  starting transfers between devices  42.3 us (37%)
  waiting for transfers between devices  37.2 us (32%)
  Pallas kernels  29.1 us (25%)
  local copies, waits for them, and re-layouts  2.7 us (2%)
  between operations  1.86 us (2%)
    pallas_call x4, Pallas kernels, run(): return pl.pallas_call(*args, compiler_params=PARAMS, **kwargs)(*operands)  29.1 us
    ppermute x10, waiting for transfers between devices, gather(): got |= {k: lax.ppermute(send, BOTH, pairs) for k, pairs in rounds}  17.7 us
    ppermute x10, starting transfers between devices, gather(): got |= {k: lax.ppermute(send, BOTH, pairs) for k, pairs in rounds}  15.6 us
    ppermute x6, waiting for transfers between devices, steps(): second |= {k: lax.ppermute(send, BOTH, pairs) for k, pairs in rounds}  13.4 us
    ppermute x6, starting transfers between devices, steps(): second |= {k: lax.ppermute(send, BOTH, pairs) for k, pairs in rounds}  7.77 us
    ppermute x2, starting transfers between devices, steps(): lax.ppermute(term, 'cuts', [(i, i ^ step) for i in range(pieces)])  6.35 us
    ppermute x4, starting transfers between devices, steps(): lax.ppermute(outs[k], BOTH, scatter_pairs(k, pieces, blocks))  4.55 us
    ppermute x4, starting transfers between devices, move(): lax.ppermute(send, BOTH, move_pairs(i, pieces, blocks, moved))  4.31 us
  transfers between devices with their start and end apart: 29, of which 14 were waited for; matrix products, arithmetic and copies ran while one was open for 1% of the time, Pallas kernels for 7%

profile of v6, /device:TPU:8, one launch (start us, length us, event | category | flops | bytes accessed | tf_op | source)
XLA Modules:
  0.0 114.2 jit_solution(5116423958156993281)
XLA Ops:
  0.7 1.3 %dynamic-slice_bitcast_fusion = (f32[8,32,256]{2,1,0:T(8,128)S(1)}, f32[8,32,256]{2,1,0:T(8,128)S(1)}, f32[8,32,256]{2,1,0:T(8,128)S(1)}, f32[8,32,256]{2,1,0:T(8,128)S(1)}) fusion(f32[2,8,32,256]{3,2,1,0:T(8,128)} %bitcast.29, s32[]{:T(128)S(6)} %select_n.44, s32[]{:T(128)S(6)} %select_n.43, f32[2,8,32,256]{3,2,1,0:T(8,128)} %bitcast.30), kind=kLoop, calls=%fused_computation.6 | loop fusion | bytes 2097160 | tf_op jit(solution)/shard_map/jit(dynamic_index_in_dim)/squeeze | solution.py:369
  2.1 1.4 %collective-permute-start.8 = (f32[11,32,256]{2,1,0:T(8,128)S(1)}, f32[11,32,256]{2,1,0:T(8,128)}, u32[]{:S(2)}, u32[]{:S(2)}) collective-permute-start(f32[11,32,256]{2,1,0:T(8,128)S(1)} %get-tuple-element.32), channel_id=1, source_target_pairs={{1,8},{14,7},{17,24},{30,23}} | collective-permute-start | bytes 1081352 | tf_op jit(solution)/shard_map/ppermute | solution.py:383
  3.5 1.4 %collective-permute-start.10 = (f32[11,32,256]{2,1,0:T(8,128)S(1)}, f32[11,32,256]{2,1,0:T(8,128)}, u32[]{:S(2)}, u32[]{:S(2)}) collective-permute-start(f32[11,32,256]{2,1,0:T(8,128)S(1)} %get-tuple-element.33), channel_id=1, source_target_pairs={{1,0},{14,15},{17,16},{30,31}} | collective-permute-start | bytes 1081352 | tf_op jit(solution)/shard_map/ppermute | solution.py:383
  6.2 1.3 %collective-permute-start.4 = (f32[11,32,256]{2,1,0:T(8,128)S(1)}, f32[11,32,256]{2,1,0:T(8,128)S(1)}, u32[]{:S(2)}, u32[]{:S(2)}) collective-permute-start(f32[11,32,256]{2,1,0:T(8,128)S(1)} %get-tuple-element.32), channel_id=1, source_target_pairs={{4,2},{6,10},{9,5},{11,13},{20,18},{22,26},{25,21},{27,29}} | collective-permute-start | bytes 1081352 | tf_op jit(solution)/shard_map/ppermute | solution.py:419
  7.5 4.6 %collective-permute-start.2 = (f32[11,32,256]{2,1,0:T(8,128)S(1)}, f32[11,32,256]{2,1,0:T(8,128)}, u32[]{:S(2)}, u32[]{:S(2)}) collective-permute-start(f32[11,32,256]{2,1,0:T(8,128)S(1)} %get-tuple-element.32), channel_id=1, source_target_pairs={{0,2},{2,10},{13,5},{15,13},{16,18},{18,26},{29,21},{31,29}} | collective-permute-start | bytes 1081352 | tf_op jit(solution)/shard_map/ppermute | solution.py:419
  14.6 1.3 %collective-permute-start.7 = (f32[11,32,256]{2,1,0:T(8,128)S(1)}, f32[11,32,256]{2,1,0:T(8,128)S(1)}, u32[]{:S(2)}, u32[]{:S(2)}) collective-permute-start(f32[11,32,256]{2,1,0:T(8,128)S(1)} %get-tuple-element.33), channel_id=1, source_target_pairs={{7,2},{5,10},{10,5},{8,13},{23,18},{21,26},{26,21},{24,29}} | collective-permute-start | bytes 1081352 | tf_op jit(solution)/shard_map/ppermute | solution.py:419
  16.0 1.3 %collective-permute-start.5 = (f32[11,32,256]{2,1,0:T(8,128)S(1)}, f32[11,32,256]{2,1,0:T(8,128)S(1)}, u32[]{:S(2)}, u32[]{:S(2)}) collective-permute-start(f32[11,32,256]{2,1,0:T(8,128)S(1)} %get-tuple-element.33), channel_id=1, source_target_pairs={{6,2},{4,10},{11,5},{9,13},{22,18},{20,26},{27,21},{25,29}} | collective-permute-start | bytes 1081352 | tf_op jit(solution)/shard_map/ppermute | solution.py:419
  17.3 1.7 %collective-permute-done.6.refs_6_ = f32[11,32,256]{2,1,0:T(8,128)S(1)} collective-permute-done((f32[11,32,256]{2,1,0:T(8,128)S(1)}, f32[11,32,256]{2,1,0:T(8,128)S(1)}, u32[]{:S(2)}, u32[]{:S(2)}) %collective-permute-start.6) | collective-permute-done | bytes 360480 | tf_op jit(solution)/shard_map/ppermute | solution.py:419
  21.0 1.3 %collective-permute-start.11 = (f32[11,32,256]{2,1,0:T(8,128)S(1)}, f32[11,32,256]{2,1,0:T(8,128)S(1)}, u32[]{:S(2)}, u32[]{:S(2)}) collective-permute-start(f32[11,32,256]{2,1,0:T(8,128)S(1)} %broadcast_select_fusion), channel_id=1, source_target_pairs={{3,2},{0,10},{15,5},{12,13},{19,18},{16,26},{31,21},{28,29}} | collective-permute-start | bytes 1081352 | tf_op jit(solution)/shard_map/ppermute | solution.py:419
  22.4 7.6 %collective-permute-done.7.refs_7_ = f32[11,32,256]{2,1,0:T(8,128)S(1)} collective-permute-done((f32[11,32,256]{2,1,0:T(8,128)S(1)}, f32[11,32,256]{2,1,0:T(8,128)S(1)}, u32[]{:S(2)}, u32[]{:S(2)}) %collective-permute-start.7) | collective-permute-done | bytes 360480 | tf_op jit(solution)/shard_map/ppermute | solution.py:419
  30.0 3.4 %collective-permute-done.5.refs_5_ = f32[11,32,256]{2,1,0:T(8,128)S(1)} collective-permute-done((f32[11,32,256]{2,1,0:T(8,128)S(1)}, f32[11,32,256]{2,1,0:T(8,128)S(1)}, u32[]{:S(2)}, u32[]{:S(2)}) %collective-permute-start.5) | collective-permute-done | bytes 360480 | tf_op jit(solution)/shard_map/ppermute | solution.py:419
  33.5 1.4 %collective-permute-done.9.refs_8_ = f32[11,32,256]{2,1,0:T(8,128)S(1)} collective-permute-done((f32[11,32,256]{2,1,0:T(8,128)S(1)}, f32[11,32,256]{2,1,0:T(8,128)S(1)}, u32[]{:S(2)}, u32[]{:S(2)}) %collective-permute-start.9) | collective-permute-done | bytes 360480 | tf_op jit(solution)/shard_map/ppermute | solution.py:419
  34.8 1.4 %collective-permute-done.11.refs_9_ = f32[11,32,256]{2,1,0:T(8,128)S(1)} collective-permute-done((f32[11,32,256]{2,1,0:T(8,128)S(1)}, f32[11,32,256]{2,1,0:T(8,128)S(1)}, u32[]{:S(2)}, u32[]{:S(2)}) %collective-permute-start.11) | collective-permute-done | bytes 360480 | tf_op jit(solution)/shard_map/ppermute | solution.py:419
  37.0 9.7 %shard_map.86 = (f32[8,256,256]{2,1,0:T(8,128)S(1)}, f32[2,256,256]{2,1,0:T(8,128)S(1)}, f32[256,256]{1,0:T(8,128)S(1)}, f32[2,256,1024]{2,1,0:T(8,128)S(1)}, f32[2,256,256]{2,1,0:T(8,128)S(1)}) custom-call(s32[3]{0:T(128)S(1)} %pad_add_fusion.refs_0_, f32[1]{0:T(128)} %copy.10.refs_1_, f32[11,32,256]{2,1,0:T(8,128)} %collective-permute-done.2.refs_2_, ...), custom_call_target="tpu_custom_call" | custom-call | tf_op jit(solution)/shard_map/pallas_call | solution.py:269
  46.7 3.6 %collective-permute-start.12 = (f32[2,256,256]{2,1,0:T(8,128)S(1)}, f32[2,256,256]{2,1,0:T(8,128)S(1)}, u32[]{:S(2)}, u32[]{:S(2)}) collective-permute-start(f32[2,256,256]{2,1,0:T(8,128)S(1)} %get-tuple-element.35.refs_2_), channel_id=1, source_target_pairs={{0,8},{8,0},{16,24},{24,16},{1,9},{9,1},{17,25},{25,17},{2,10},{10... | collective-permute-start | bytes 1572872 | tf_op jit(solution)/shard_map/ppermute | solution.py:456
  51.5 1.3 %collective-permute-start.17 = (f32[10,32,256]{2,1,0:T(8,128)S(1)}, f32[10,32,256]{2,1,0:T(8,128)S(1)}, u32[]{:S(2)}, u32[]{:S(2)}) collective-permute-start(f32[10,32,256]{2,1,0:T(8,128)S(1)} %get-tuple-element.45), channel_id=1, source_target_pairs={{6,2},{4,10},{11,5},{9,13},{22,18},{20,26},{27,21},{25,29}} | collective-permute-start | bytes 983048 | tf_op jit(solution)/shard_map/ppermute | solution.py:419
  52.8 1.9 %collective-permute-start.14 = (f32[10,32,256]{2,1,0:T(8,128)S(1)}, f32[10,32,256]{2,1,0:T(8,128)S(1)}, u32[]{:S(2)}, u32[]{:S(2)}) collective-permute-start(f32[10,32,256]{2,1,0:T(8,128)S(1)} %get-tuple-element.44), channel_id=1, source_target_pairs={{0,2},{2,10},{13,5},{15,13},{16,18},{18,26},{29,21},{31,29}} | collective-permute-start | bytes 983048 | tf_op jit(solution)/shard_map/ppermute | solution.py:438
  55.5 8.5 %shard_map.87 = (f32[2,256,256]{2,1,0:T(8,128)S(1)}, f32[2,256,256]{2,1,0:T(8,128)S(1)}, f32[2,8,128]{2,1,0:T(8,128)S(1)}, f32[2,256,1024]{2,1,0:T(8,128)S(1)}, f32[2,256,256]{2,1,0:T(8,128)S(1)}) custom-call(s32[3]{0:T(128)S(1)} %pad_add_fusion.refs_0_, f32[2,256,256]{2,1,0:T(8,128)S(1)} %get-tuple-element.34.refs_1_, ...), custom_call_target="tpu_custom_call" | custom-call | tf_op jit(solution)/shard_map/pallas_call | solution.py:269
  64.0 2.2 %collective-permute-done.16.refs_13_ = f32[10,32,256]{2,1,0:T(8,128)S(1)} collective-permute-done((f32[10,32,256]{2,1,0:T(8,128)S(1)}, f32[10,32,256]{2,1,0:T(8,128)S(1)}, u32[]{:S(2)}, u32[]{:S(2)}) %collective-permute-start.16) | collective-permute-done | bytes 327712 | tf_op jit(solution)/shard_map/ppermute | solution.py:419
  67.5 1.3 %collective-permute-start.18 = (f32[10,32,256]{2,1,0:T(8,128)S(1)}, f32[10,32,256]{2,1,0:T(8,128)S(1)}, u32[]{:S(2)}, u32[]{:S(2)}) collective-permute-start(f32[10,32,256]{2,1,0:T(8,128)S(1)} %broadcast_select_fusion.3), channel_id=1, source_target_pairs={{5,2},{14,10},{1,5},{10,13},{21,18},{30,26},{17,21},{26,29}} | collective-permute-start | bytes 983048 | tf_op jit(solution)/shard_map/ppermute | solution.py:438
  71.4 3.2 %collective-permute-done.20.refs_17_ = f32[10,32,256]{2,1,0:T(8,128)S(1)} collective-permute-done((f32[10,32,256]{2,1,0:T(8,128)S(1)}, f32[10,32,256]{2,1,0:T(8,128)S(1)}, u32[]{:S(2)}, u32[]{:S(2)}) %collective-permute-start.20) | collective-permute-done | bytes 327712 | tf_op jit(solution)/shard_map/ppermute | solution.py:438
  74.6 3.6 %collective-permute-done.18.refs_15_ = f32[10,32,256]{2,1,0:T(8,128)S(1)} collective-permute-done((f32[10,32,256]{2,1,0:T(8,128)S(1)}, f32[10,32,256]{2,1,0:T(8,128)S(1)}, u32[]{:S(2)}, u32[]{:S(2)}) %collective-permute-start.18) | collective-permute-done | bytes 327712 | tf_op jit(solution)/shard_map/ppermute | solution.py:438
  78.2 6.6 %collective-permute-done.21.refs_18_ = f32[10,32,256]{2,1,0:T(8,128)S(1)} collective-permute-done((f32[10,32,256]{2,1,0:T(8,128)S(1)}, f32[10,32,256]{2,1,0:T(8,128)S(1)}, u32[]{:S(2)}, u32[]{:S(2)}) %collective-permute-start.21) | collective-permute-done | bytes 327712 | tf_op jit(solution)/shard_map/ppermute | solution.py:438
  84.8 10.2 %shard_map.88 = (f32[2,256,256]{2,1,0:T(8,128)S(1)}, f32[2,256,256]{2,1,0:T(8,128)S(1)}, f32[2,8,128]{2,1,0:T(8,128)S(1)}, f32[520,256]{1,0:T(8,128)S(1)}) custom-call(s32[3]{0:T(128)S(1)} %pad_add_fusion.refs_0_, f32[2,256,256]{2,1,0:T(8,128)S(1)} %get-tuple-element.34.refs_1_, f32[2,256,256]{2,1,0:T(8,128)S(1)} %get-tuple-element.38.refs_2_, ...), custom_call_target="tpu_custom_call" | custom-call | tf_op jit(solution)/shard_map/pallas_call | solution.py:269
  95.1 1.9 %collective-permute-done.22.refs_2_ = f32[520,256]{1,0:T(8,128)S(1)} collective-permute-done((f32[520,256]{1,0:T(8,128)S(1)}, f32[520,256]{1,0:T(8,128)S(1)}, u32[]{:S(2)}, u32[]{:S(2)}) %collective-permute-start.22) | collective-permute-done | bytes 532512 | tf_op jit(solution)/shard_map/ppermute | solution.py:479
  97.8 1.3 %collective-permute-start.23 = (f32[3,32,256]{2,1,0:T(8,128)S(1)}, f32[3,32,256]{2,1,0:T(8,128)S(1)}, u32[]{:S(2)}, u32[]{:S(2)}) collective-permute-start(f32[3,32,256]{2,1,0:T(8,128)S(1)} %get-tuple-element.52), channel_id=1, source_target_pairs={{2,0},{10,4},{5,8},{13,12},{18,16},{26,20},{21,24},{29,28}} | collective-permute-start | bytes 294920 | tf_op jit(solution)/shard_map/ppermute | solution.py:488
  99.1 1.3 %collective-permute-start.24 = (f32[3,32,256]{2,1,0:T(8,128)S(1)}, f32[3,32,256]{2,1,0:T(8,128)S(1)}, u32[]{:S(2)}, u32[]{:S(2)}) collective-permute-start(f32[3,32,256]{2,1,0:T(8,128)S(1)} %get-tuple-element.53), channel_id=1, source_target_pairs={{2,1},{10,6},{5,9},{13,14},{18,17},{26,22},{21,25},{29,30}} | collective-permute-start | bytes 294920 | tf_op jit(solution)/shard_map/ppermute | solution.py:488
  100.4 1.3 %collective-permute-start.25 = (f32[3,32,256]{2,1,0:T(8,128)S(1)}, f32[3,32,256]{2,1,0:T(8,128)S(1)}, u32[]{:S(2)}, u32[]{:S(2)}) collective-permute-start(f32[3,32,256]{2,1,0:T(8,128)S(1)} %get-tuple-element.54), channel_id=1, source_target_pairs={{2,3},{10,7},{5,11},{13,15},{18,19},{26,23},{21,27},{29,31}} | collective-permute-start | bytes 294920 | tf_op jit(solution)/shard_map/ppermute | solution.py:488
  102.6 1.3 %collective-permute-done.25 = f32[3,32,256]{2,1,0:T(8,128)S(1)} collective-permute-done((f32[3,32,256]{2,1,0:T(8,128)S(1)}, f32[3,32,256]{2,1,0:T(8,128)S(1)}, u32[]{:S(2)}, u32[]{:S(2)}) %collective-permute-start.25) | collective-permute-done | bytes 98336 | tf_op jit(solution)/shard_map/ppermute | solution.py:488
  104.0 4.8 %collective-permute-start.27 = (f32[32,256]{1,0:T(8,128)S(1)}, f32[32,256]{1,0:T(8,128)S(1)}, u32[]{:S(2)}, u32[]{:S(2)}) collective-permute-start(f32[32,256]{1,0:T(8,128)S(1)} %slice_bitcast_fusion.1), channel_id=1, source_target_pairs={{0,8},{8,0},{16,24},{24,16},{1,9},{9,1},{17,25},{25,17},{2,10},{10... | collective-permute-start | bytes 98312 | tf_op jit(solution)/shard_map/ppermute | solution.py:496
  109.7 1.5 %collective-permute-start.28 = (f32[32,256]{1,0:T(8,128)S(1)}, f32[32,256]{1,0:T(8,128)S(1)}, u32[]{:S(2)}, u32[]{:S(2)}) collective-permute-start(f32[32,256]{1,0:T(8,128)S(1)} %fusion.1), channel_id=1, source_target_pairs={{0,16},{8,24},{16,0},{24,8},{1,17},{9,25},{17,1},{25,9},{2,18},{10... | collective-permute-start | bytes 98312 | tf_op jit(solution)/shard_map/ppermute | solution.py:496
  111.8 1.8 %collective-permute-done.28 = f32[32,256]{1,0:T(8,128)S(1)} collective-permute-done((f32[32,256]{1,0:T(8,128)S(1)}, f32[32,256]{1,0:T(8,128)S(1)}, u32[]{:S(2)}, u32[]{:S(2)}) %collective-permute-start.28) | collective-permute-done | bytes 32800 | tf_op jit(solution)/shard_map/ppermute | solution.py:496
  (65 shorter events, 15.7 us)
Async XLA Ops:
  2.1 10.9 %collective-permute-start.8 = (f32[11,32,256]{2,1,0:T(8,128)S(1)}, f32[11,32,256]{2,1,0:T(8,128)}, u32[]{:S(2)}, u32[]{:S(2)}) collective-permute-start(f32[11,32,256]{2,1,0:T(8,128)S(1)} %get-tuple-element.32), channel_id=1, source_target_pairs={{1,8},{14,7},{17,24},{30,23}} | collective-permute-start | bytes 1081352 | tf_op jit(solution)/shard_map/ppermute | solution.py:383
  3.5 10.3 %collective-permute-start.10 = (f32[11,32,256]{2,1,0:T(8,128)S(1)}, f32[11,32,256]{2,1,0:T(8,128)}, u32[]{:S(2)}, u32[]{:S(2)}) collective-permute-start(f32[11,32,256]{2,1,0:T(8,128)S(1)} %get-tuple-element.33), channel_id=1, source_target_pairs={{1,0},{14,15},{17,16},{30,31}} | collective-permute-start | bytes 1081352 | tf_op jit(solution)/shard_map/ppermute | solution.py:383
  4.9 14.1 %collective-permute-start.6 = (f32[11,32,256]{2,1,0:T(8,128)S(1)}, f32[11,32,256]{2,1,0:T(8,128)S(1)}, u32[]{:S(2)}, u32[]{:S(2)}) collective-permute-start(f32[11,32,256]{2,1,0:T(8,128)S(1)} %get-tuple-element.32), channel_id=1, source_target_pairs={{5,2},{7,10},{8,5},{10,13},{21,18},{23,26},{24,21},{26,29}} | collective-permute-start | bytes 1081352 | tf_op jit(solution)/shard_map/ppermute | solution.py:419
  6.2 13.5 %collective-permute-start.4 = (f32[11,32,256]{2,1,0:T(8,128)S(1)}, f32[11,32,256]{2,1,0:T(8,128)S(1)}, u32[]{:S(2)}, u32[]{:S(2)}) collective-permute-start(f32[11,32,256]{2,1,0:T(8,128)S(1)} %get-tuple-element.32), channel_id=1, source_target_pairs={{4,2},{6,10},{9,5},{11,13},{20,18},{22,26},{25,21},{27,29}} | collective-permute-start | bytes 1081352 | tf_op jit(solution)/shard_map/ppermute | solution.py:419
  7.5 13.5 %collective-permute-start.2 = (f32[11,32,256]{2,1,0:T(8,128)S(1)}, f32[11,32,256]{2,1,0:T(8,128)}, u32[]{:S(2)}, u32[]{:S(2)}) collective-permute-start(f32[11,32,256]{2,1,0:T(8,128)S(1)} %get-tuple-element.32), channel_id=1, source_target_pairs={{0,2},{2,10},{13,5},{15,13},{16,18},{18,26},{29,21},{31,29}} | collective-permute-start | bytes 1081352 | tf_op jit(solution)/shard_map/ppermute | solution.py:419
  12.9 24.1 %copy-start = (bf16[10,256,256]{2,1,0:T(8,128)(2,1)S(1)}, bf16[10,256,256]{2,1,0:T(8,128)(2,1)}, u32[]{:S(2)}) copy-start(bf16[10,256,256]{2,1,0:T(8,128)(2,1)} %constant.78.clone.refs_10_.refs_6_.refs_19_) | copy-start | bytes 3932164
  13.0 1.7 %collective-permute-start = (f32[10,32,256]{2,1,0:T(8,128)S(1)}, f32[10,32,256]{2,1,0:T(8,128)S(1)}, u32[]{:S(2)}, u32[]{:S(2)}) collective-permute-start(f32[10,32,256]{2,1,0:T(8,128)S(1)} %get-tuple-element.44), channel_id=1, source_target_pairs={{1,8},{7,14},{8,1},{14,7},{17,24},{23,30},{24,17},{30,23}} | collective-permute-start | bytes 983048 | tf_op jit(solution)/shard_map/ppermute | solution.py:383
  13.8 2.1 %collective-permute-start.1 = (f32[10,32,256]{2,1,0:T(8,128)S(1)}, f32[10,32,256]{2,1,0:T(8,128)S(1)}, u32[]{:S(2)}, u32[]{:S(2)}) collective-permute-start(f32[10,32,256]{2,1,0:T(8,128)S(1)} %get-tuple-element.45), channel_id=1, source_target_pairs={{1,0},{7,6},{8,9},{14,15},{17,16},{23,22},{24,25},{30,31}} | collective-permute-start | bytes 983048 | tf_op jit(solution)/shard_map/ppermute | solution.py:383
  14.6 15.4 %collective-permute-start.7 = (f32[11,32,256]{2,1,0:T(8,128)S(1)}, f32[11,32,256]{2,1,0:T(8,128)S(1)}, u32[]{:S(2)}, u32[]{:S(2)}) collective-permute-start(f32[11,32,256]{2,1,0:T(8,128)S(1)} %get-tuple-element.33), channel_id=1, source_target_pairs={{7,2},{5,10},{10,5},{8,13},{23,18},{21,26},{26,21},{24,29}} | collective-permute-start | bytes 1081352 | tf_op jit(solution)/shard_map/ppermute | solution.py:419
  16.0 17.5 %collective-permute-start.5 = (f32[11,32,256]{2,1,0:T(8,128)S(1)}, f32[11,32,256]{2,1,0:T(8,128)S(1)}, u32[]{:S(2)}, u32[]{:S(2)}) collective-permute-start(f32[11,32,256]{2,1,0:T(8,128)S(1)} %get-tuple-element.33), channel_id=1, source_target_pairs={{6,2},{4,10},{11,5},{9,13},{22,18},{20,26},{27,21},{25,29}} | collective-permute-start | bytes 1081352 | tf_op jit(solution)/shard_map/ppermute | solution.py:419
  19.0 17.3 %copy-start.1 = (f32[11,32,256]{2,1,0:T(8,128)}, f32[11,32,256]{2,1,0:T(8,128)S(1)}, u32[]{:S(2)}) copy-start(f32[11,32,256]{2,1,0:T(8,128)S(1)} %collective-permute-done.6.refs_6_) | copy-start | bytes 1081348
  19.0 14.5 %collective-permute-start.3 = (f32[11,32,256]{2,1,0:T(8,128)S(1)}, f32[11,32,256]{2,1,0:T(8,128)S(1)}, u32[]{:S(2)}, u32[]{:S(2)}) collective-permute-start(f32[11,32,256]{2,1,0:T(8,128)S(1)} %get-tuple-element.33), channel_id=1, source_target_pairs={{2,2},{0,10},{15,5},{13,13},{18,18},{16,26},{31,21},{29,29}} | collective-permute-start | bytes 1081352 | tf_op jit(solution)/shard_map/ppermute | solution.py:419
  19.7 16.6 %copy-start.2 = (f32[11,32,256]{2,1,0:T(8,128)}, f32[11,32,256]{2,1,0:T(8,128)S(1)}, u32[]{:S(2)}) copy-start(f32[11,32,256]{2,1,0:T(8,128)S(1)} %collective-permute-done.4.refs_4_) | copy-start | bytes 1081348
  19.7 15.1 %collective-permute-start.9 = (f32[11,32,256]{2,1,0:T(8,128)S(1)}, f32[11,32,256]{2,1,0:T(8,128)S(1)}, u32[]{:S(2)}, u32[]{:S(2)}) collective-permute-start(f32[11,32,256]{2,1,0:T(8,128)S(1)} %broadcast_select_fusion.1), channel_id=1, source_target_pairs={{8,2},{3,10},{12,5},{7,13},{24,18},{19,26},{28,21},{23,29}} | collective-permute-start | bytes 1081352 | tf_op jit(solution)/shard_map/ppermute | solution.py:419
  21.0 15.2 %collective-permute-start.11 = (f32[11,32,256]{2,1,0:T(8,128)S(1)}, f32[11,32,256]{2,1,0:T(8,128)S(1)}, u32[]{:S(2)}, u32[]{:S(2)}) collective-permute-start(f32[11,32,256]{2,1,0:T(8,128)S(1)} %broadcast_select_fusion), channel_id=1, source_target_pairs={{3,2},{0,10},{15,5},{12,13},{19,18},{16,26},{31,21},{28,29}} | collective-permute-start | bytes 1081352 | tf_op jit(solution)/shard_map/ppermute | solution.py:419
  46.7 8.8 %collective-permute-start.12 = (f32[2,256,256]{2,1,0:T(8,128)S(1)}, f32[2,256,256]{2,1,0:T(8,128)S(1)}, u32[]{:S(2)}, u32[]{:S(2)}) collective-permute-start(f32[2,256,256]{2,1,0:T(8,128)S(1)} %get-tuple-element.35.refs_2_), channel_id=1, source_target_pairs={{0,8},{8,0},{16,24},{24,16},{1,9},{9,1},{17,25},{25,17},{2,10},{10... | collective-permute-start | bytes 1572872 | tf_op jit(solution)/shard_map/ppermute | solution.py:456
  50.3 16.0 %collective-permute-start.16 = (f32[10,32,256]{2,1,0:T(8,128)S(1)}, f32[10,32,256]{2,1,0:T(8,128)S(1)}, u32[]{:S(2)}, u32[]{:S(2)}) collective-permute-start(f32[10,32,256]{2,1,0:T(8,128)S(1)} %get-tuple-element.44), channel_id=1, source_target_pairs={{4,2},{6,10},{9,5},{11,13},{20,18},{22,26},{25,21},{27,29}} | collective-permute-start | bytes 983048 | tf_op jit(solution)/shard_map/ppermute | solution.py:419
  51.5 16.0 %collective-permute-start.17 = (f32[10,32,256]{2,1,0:T(8,128)S(1)}, f32[10,32,256]{2,1,0:T(8,128)S(1)}, u32[]{:S(2)}, u32[]{:S(2)}) collective-permute-start(f32[10,32,256]{2,1,0:T(8,128)S(1)} %get-tuple-element.45), channel_id=1, source_target_pairs={{6,2},{4,10},{11,5},{9,13},{22,18},{20,26},{27,21},{25,29}} | collective-permute-start | bytes 983048 | tf_op jit(solution)/shard_map/ppermute | solution.py:419
  52.8 16.0 %collective-permute-start.14 = (f32[10,32,256]{2,1,0:T(8,128)S(1)}, f32[10,32,256]{2,1,0:T(8,128)S(1)}, u32[]{:S(2)}, u32[]{:S(2)}) collective-permute-start(f32[10,32,256]{2,1,0:T(8,128)S(1)} %get-tuple-element.44), channel_id=1, source_target_pairs={{0,2},{2,10},{13,5},{15,13},{16,18},{18,26},{29,21},{31,29}} | collective-permute-start | bytes 983048 | tf_op jit(solution)/shard_map/ppermute | solution.py:438
  54.8 15.4 %collective-permute-start.15 = (f32[10,32,256]{2,1,0:T(8,128)S(1)}, f32[10,32,256]{2,1,0:T(8,128)S(1)}, u32[]{:S(2)}, u32[]{:S(2)}) collective-permute-start(f32[10,32,256]{2,1,0:T(8,128)S(1)} %get-tuple-element.45), channel_id=1, source_target_pairs={{2,2},{0,10},{15,5},{13,13},{18,18},{16,26},{31,21},{29,29}} | collective-permute-start | bytes 983048 | tf_op jit(solution)/shard_map/ppermute | solution.py:438
  64.0 20.9 %collective-permute-start.13 = (f32[2,256,256]{2,1,0:T(8,128)S(1)}, f32[2,256,256]{2,1,0:T(8,128)S(1)}, u32[]{:S(2)}, u32[]{:S(2)}) collective-permute-start(f32[2,256,256]{2,1,0:T(8,128)S(1)} %get-tuple-element.41.refs_5_), channel_id=1, source_target_pairs={{0,8},{8,0},{16,24},{24,16},{1,9},{9,1},{17,25},{25,17},{2,10},{10... | collective-permute-start | bytes 1572872 | tf_op jit(solution)/shard_map/ppermute | solution.py:464
  66.2 8.4 %collective-permute-start.20 = (f32[10,32,256]{2,1,0:T(8,128)S(1)}, f32[10,32,256]{2,1,0:T(8,128)S(1)}, u32[]{:S(2)}, u32[]{:S(2)}) collective-permute-start(f32[10,32,256]{2,1,0:T(8,128)S(1)} %broadcast_select_fusion.3), channel_id=1, source_target_pairs={{8,2},{3,10},{12,5},{7,13},{24,18},{19,26},{28,21},{23,29}} | collective-permute-start | bytes 983048 | tf_op jit(solution)/shard_map/ppermute | solution.py:438
  67.5 10.7 %collective-permute-start.18 = (f32[10,32,256]{2,1,0:T(8,128)S(1)}, f32[10,32,256]{2,1,0:T(8,128)S(1)}, u32[]{:S(2)}, u32[]{:S(2)}) collective-permute-start(f32[10,32,256]{2,1,0:T(8,128)S(1)} %broadcast_select_fusion.3), channel_id=1, source_target_pairs={{5,2},{14,10},{1,5},{10,13},{21,18},{30,26},{17,21},{26,29}} | collective-permute-start | bytes 983048 | tf_op jit(solution)/shard_map/ppermute | solution.py:438
  68.8 16.0 %collective-permute-start.21 = (f32[10,32,256]{2,1,0:T(8,128)S(1)}, f32[10,32,256]{2,1,0:T(8,128)S(1)}, u32[]{:S(2)}, u32[]{:S(2)}) collective-permute-start(f32[10,32,256]{2,1,0:T(8,128)S(1)} %broadcast_select_fusion.2), channel_id=1, source_target_pairs={{3,2},{0,10},{15,5},{12,13},{19,18},{16,26},{31,21},{28,29}} | collective-permute-start | bytes 983048 | tf_op jit(solution)/shard_map/ppermute | solution.py:438
  70.1 14.7 %collective-permute-start.19 = (f32[10,32,256]{2,1,0:T(8,128)S(1)}, f32[10,32,256]{2,1,0:T(8,128)S(1)}, u32[]{:S(2)}, u32[]{:S(2)}) collective-permute-start(f32[10,32,256]{2,1,0:T(8,128)S(1)} %broadcast_select_fusion.2), channel_id=1, source_target_pairs={{6,2},{5,10},{10,5},{9,13},{22,18},{21,26},{26,21},{25,29}} | collective-permute-start | bytes 983048 | tf_op jit(solution)/shard_map/ppermute | solution.py:438
  95.1 2.0 %collective-permute-start.22 = (f32[520,256]{1,0:T(8,128)S(1)}, f32[520,256]{1,0:T(8,128)S(1)}, u32[]{:S(2)}, u32[]{:S(2)}) collective-permute-start(f32[520,256]{1,0:T(8,128)S(1)} %get-tuple-element.48.refs_1_), channel_id=1, source_target_pairs={{0,8},{8,0},{16,24},{24,16},{1,9},{9,1},{17,25},{25,17},{2,10},{10... | collective-permute-start | bytes 1597448 | tf_op jit(solution)/shard_map/ppermute | solution.py:479
  97.8 4.6 %collective-permute-start.23 = (f32[3,32,256]{2,1,0:T(8,128)S(1)}, f32[3,32,256]{2,1,0:T(8,128)S(1)}, u32[]{:S(2)}, u32[]{:S(2)}) collective-permute-start(f32[3,32,256]{2,1,0:T(8,128)S(1)} %get-tuple-element.52), channel_id=1, source_target_pairs={{2,0},{10,4},{5,8},{13,12},{18,16},{26,20},{21,24},{29,28}} | collective-permute-start | bytes 294920 | tf_op jit(solution)/shard_map/ppermute | solution.py:488
  99.1 3.5 %collective-permute-start.24 = (f32[3,32,256]{2,1,0:T(8,128)S(1)}, f32[3,32,256]{2,1,0:T(8,128)S(1)}, u32[]{:S(2)}, u32[]{:S(2)}) collective-permute-start(f32[3,32,256]{2,1,0:T(8,128)S(1)} %get-tuple-element.53), channel_id=1, source_target_pairs={{2,1},{10,6},{5,9},{13,14},{18,17},{26,22},{21,25},{29,30}} | collective-permute-start | bytes 294920 | tf_op jit(solution)/shard_map/ppermute | solution.py:488
  100.4 3.5 %collective-permute-start.25 = (f32[3,32,256]{2,1,0:T(8,128)S(1)}, f32[3,32,256]{2,1,0:T(8,128)S(1)}, u32[]{:S(2)}, u32[]{:S(2)}) collective-permute-start(f32[3,32,256]{2,1,0:T(8,128)S(1)} %get-tuple-element.54), channel_id=1, source_target_pairs={{2,3},{10,7},{5,11},{13,15},{18,19},{26,23},{21,27},{29,31}} | collective-permute-start | bytes 294920 | tf_op jit(solution)/shard_map/ppermute | solution.py:488
  101.7 2.2 %collective-permute-start.26 = (f32[3,32,256]{2,1,0:T(8,128)S(1)}, f32[3,32,256]{2,1,0:T(8,128)S(1)}, u32[]{:S(2)}, u32[]{:S(2)}) collective-permute-start(f32[3,32,256]{2,1,0:T(8,128)S(1)} %get-tuple-element.55), channel_id=1, source_target_pairs={{2,2},{10,5},{5,10},{13,13},{18,18},{26,21},{21,26},{29,29}} | collective-permute-start | bytes 294920 | tf_op jit(solution)/shard_map/ppermute | solution.py:488
  104.0 5.7 %collective-permute-start.27 = (f32[32,256]{1,0:T(8,128)S(1)}, f32[32,256]{1,0:T(8,128)S(1)}, u32[]{:S(2)}, u32[]{:S(2)}) collective-permute-start(f32[32,256]{1,0:T(8,128)S(1)} %slice_bitcast_fusion.1), channel_id=1, source_target_pairs={{0,8},{8,0},{16,24},{24,16},{1,9},{9,1},{17,25},{25,17},{2,10},{10... | collective-permute-start | bytes 98312 | tf_op jit(solution)/shard_map/ppermute | solution.py:496
  109.7 3.9 %collective-permute-start.28 = (f32[32,256]{1,0:T(8,128)S(1)}, f32[32,256]{1,0:T(8,128)S(1)}, u32[]{:S(2)}, u32[]{:S(2)}) collective-permute-start(f32[32,256]{1,0:T(8,128)S(1)} %fusion.1), channel_id=1, source_target_pairs={{0,16},{8,24},{16,0},{24,8},{1,17},{9,25},{17,1},{25,9},{2,18},{10... | collective-permute-start | bytes 98312 | tf_op jit(solution)/shard_map/ppermute | solution.py:496
  (8 other events, 28.8 us)
